TPU v7x, 512 devices: a whole 4x8x8 slice. The times are simulated.
512 devices in a mesh: row: 2 (over core), ax: 8 (over x, z_lo), az: 32 (over z_hi, y).
Axes of the slice: x: 4, y: 8, z: 8 (z_hi: 4, z_lo: 2; z = z_hi * 2 + z_lo), core: 2. Of those that a mesh axis runs over, the one named last changes fastest.
Arguments:
- density: float32 [2, 16, 1024, 512], P('row', 'ax', 'az'), may hold values from 0.8 to 1.6
- velocity: float32 [2, 3, 16, 1024, 512], P('row', None, 'ax', 'az'), may hold values from -1.5 to 1.5
- pressure: float32 [2, 16, 1024, 512], P('row', 'ax', 'az'), may hold values from 0.4 to 1.2
- offsets: int32 [3], replicated, may hold values from 0 to 1023
Outputs:
- final_state: float32 [2, 5, 16, 1024, 512], P('row', None, 'ax', 'az')
All inputs are finite; a program needn't handle non-finite values.
Results may differ from a plain program's by a relative error of at most 0.00002.
Values sent between devices are 32-bit elements; how exact they have to be, the bound alone decides.
No kernel may reach another device: no remote copies, remote signals or barrier semaphores. Data moves between devices by JAX's collectives and lax.ppermute only.
A program may use at most 128 MiB of HBM per device.

v0:
```python
import functools
import math

import jax
import jax.numpy as jnp
from jax import lax
from jax.experimental import pallas as pl
from jax.experimental.pallas import tpu as pltpu
from jax.sharding import PartitionSpec as P

HEAT_RATIO = 1.4
VISCOSITY = 0.8
CONDUCTION = 0.6
TIME_STEP = 0.1
AXIAL_CURVE = 4.0
AXES = ("row", "ax", "az")
FIELDS = 5
SUB = 8
LANES = 128
HALF = 64
EDGE = 4
IN_BRANCH = True
LOOP = True


def cell(state):
    rho, mt, mr, mz, energy = state
    inv = 1.0 / rho
    vt, vr, vz = mt * inv, mr * inv, mz * inv
    tt, rr, zz = mt * vt, mr * vr, mz * vz
    press = (HEAT_RATIO - 1.0) * (energy - 0.5 * (tt + rr + zz))
    visc = (
        None,
        VISCOSITY * vt,
        VISCOSITY * vr,
        VISCOSITY * vz,
        CONDUCTION * (press * inv),
    )
    return dict(
        mt=mt, mr=mr, mz=mz, vt=vt, vr=vr, vz=vz, tt=tt, rr=rr, zz=zz,
        tr=mt * vr, tz=mt * vz, rz=mr * vz, press=press, enth=energy + press, visc=visc,
    )


def flux_theta(c):
    return (c["mt"], c["tt"] + c["press"], c["tr"], c["tz"], c["enth"] * c["vt"])


def flux_radial(c):
    return (c["mr"], c["tr"], c["rr"] + c["press"], c["rz"], c["enth"] * c["vr"])


def flux_axial(c):
    return (c["mz"], c["tz"], c["rz"], c["zz"] + c["press"], c["enth"] * c["vz"])


def axial_terms(c):
    above, below = [], []
    for flux, visc in zip(flux_axial(c), c["visc"]):
        if visc is None:
            above.append(flux)
            below.append(-flux)
        else:
            side = AXIAL_CURVE * visc
            above.append(side + flux)
            below.append(side - flux)
    return above, below


def theta_terms(c, co):
    flux = [co["half_arc"] * f for f in flux_theta(c)]
    flux[1] = flux[1] - co["cross"] * c["visc"][2]
    flux[2] = flux[2] + co["cross"] * c["visc"][1]
    nxt, prv = [flux[0]], [-flux[0]]
    for k in range(1, FIELDS):
        side = co["arc2"] * c["visc"][k]
        nxt.append(side + flux[k])
        prv.append(side - flux[k])
    return nxt, prv


def radial_terms(c, co):
    out, inn = [], []
    for flux, visc in zip(flux_radial(c), c["visc"]):
        odd = co["half_r"] * flux
        if visc is None:
            out.append(odd)
            inn.append(-odd)
        else:
            odd = odd + 0.5 * visc
            even = co["r"] * visc
            out.append(even + odd)
            inn.append(even - odd)
    return out, inn


def wall_terms(c, half_rg, weight, sign):
    flux = flux_radial(c)
    signs = (-1.0, 1.0, 1.0, 1.0, -1.0)
    out = []
    for k in range(FIELDS):
        term = (sign * signs[k]) * (half_rg * flux[k])
        if k:
            term = term + (1.0 if k == 4 else -1.0) * (weight * c["visc"][k])
        out.append(term)
    return out


def centre_terms(c, co):
    centre = [None] + [-(co["centre"] * v) for v in c["visc"][1:]]
    centre[1] = centre[1] - co["inv_r"] * (c["tr"] + co["inv_r"] * c["visc"][1])
    centre[2] = centre[2] + co["inv_r"] * (c["tt"] + c["press"] - co["inv_r"] * c["visc"][2])
    return centre


def lanes_of():
    lane = lax.broadcasted_iota(jnp.int32, (SUB, LANES), 1)
    return lane, jnp.where(lane < HALF, lane, lane - HALF)


def coefficients(segment, cycle_cells):
    dtheta = 2.0 * math.pi / cycle_cells
    cells = (lanes_of()[1] + segment * HALF).astype(jnp.float32)
    r = cycle_cells / (2.0 * math.pi) + cells + 0.5
    inv_r = 1.0 / r
    arc2 = 1.0 / ((r * dtheta) * (r * dtheta))
    return dict(
        r=r, half_r=0.5 * r, inv_r=inv_r, half_arc=1.0 / (2.0 * r * dtheta), arc2=arc2,
        cross=1.0 / (r * r * dtheta), centre=2.0 * arc2 + 2.0 + 2.0 * AXIAL_CURVE,
    )


def pack_kernel(rho_ref, vel_ref, press_ref, out_ref):
    lane, _ = lanes_of()
    low = lane < HALF
    for b in range(rho_ref.shape[1] // SUB):
        rows = pl.ds(b * SUB, SUB)
        for w in range(rho_ref.shape[2] // LANES):
            cols = pl.ds(w * LANES, LANES)
            both = []
            for p in range(2):
                rho = rho_ref[p, rows, cols]
                vel = [vel_ref[d, p, rows, cols] for d in range(3)]
                square = vel[0] * vel[0] + vel[1] * vel[1] + vel[2] * vel[2]
                energy = press_ref[p, rows, cols] / (HEAT_RATIO - 1.0) + 0.5 * rho * square
                both.append([rho] + [rho * v for v in vel] + [energy])
            for k in range(FIELDS):
                first, second = both[0][k], both[1][k]
                out_ref[2 * w, k, rows, :] = jnp.where(low, first, pltpu.roll(second, HALF, 1))
                out_ref[2 * w + 1, k, rows, :] = jnp.where(low, pltpu.roll(first, HALF, 1), second)


def edge_kernel(flag_ref, in_ref, up_ref, down_ref):
    front = lax.broadcasted_iota(jnp.int32, (SUB, LANES), 0) < EDGE
    rotor = flag_ref[6] == 1
    end = pl.ds(in_ref.shape[2] - SUB, SUB)
    for i in range(up_ref.shape[0]):
        one, two = divmod(2 * i, FIELDS), divmod(2 * i + 1, FIELDS)
        head = jnp.where(
            front, in_ref[*one, pl.ds(0, SUB), :], pltpu.roll(in_ref[*two, pl.ds(0, SUB), :], EDGE, 0)
        )
        tail = jnp.where(front, pltpu.roll(in_ref[*one, end, :], EDGE, 0), in_ref[*two, end, :])
        up_ref[i] = jnp.where(rotor, tail, head)
        down_ref[i] = jnp.where(rotor, head, tail)


def unpack_kernel(in_ref, out_ref):
    lane, _ = lanes_of()
    low = lane < HALF
    for b in range(out_ref.shape[2] // SUB):
        rows = pl.ds(b * SUB, SUB)
        for w in range(in_ref.shape[0] // 2):
            cols = pl.ds(w * LANES, LANES)
            for k in range(FIELDS):
                inner, outer = in_ref[2 * w, k, rows, :], in_ref[2 * w + 1, k, rows, :]
                out_ref[k, 0, rows, cols] = jnp.where(low, inner, pltpu.roll(outer, HALF, 1))
                out_ref[k, 1, rows, cols] = jnp.where(low, pltpu.roll(inner, HALF, 1), outer)


def write_sends(state_ref, co, up_ref, out_ref, inn_ref):
    lane, place = lanes_of()
    pairs = state_ref.shape[0]
    blocks = state_ref.shape[2] // SUB
    top = []
    for b in range(blocks):
        rows = pl.ds(b * SUB, SUB)
        packed_out = jnp.zeros((SUB, LANES), jnp.float32)
        packed_in = jnp.zeros((SUB, LANES), jnp.float32)
        for a in range(pairs):
            c = cell([state_ref[a, k, rows, :] for k in range(FIELDS)])
            to_out, to_in = radial_terms(c, co)
            for k in range(FIELDS):
                j = a * FIELDS + k
                here = place == j
                moved = pltpu.roll(to_out[k], (j + 1 - HALF) % LANES, 1)
                packed_out = jnp.where(here, moved, packed_out)
                moved = pltpu.roll(to_in[k], j, 1) if j else to_in[k]
                packed_in = jnp.where(here, moved, packed_in)
            if a == pairs - 1:
                top.append(axial_terms(c)[0])
        out_ref[rows, :] = packed_out
        inn_ref[rows, :] = packed_in
    half = up_ref.shape[1] // SUB
    for b in range(half):
        for k in range(FIELDS):
            value = pltpu.roll(top[b][k], HALF, 1)
            if b + half < blocks:
                value = jnp.where(lane < HALF, value, top[b + half][k])
            up_ref[k, pl.ds(b * SUB, SUB), :] = value


def first_kernel(cycle_cells, flag_ref, in_ref, one_ref, two_ref, state_ref, *sends):
    rotor = flag_ref[6] == 1
    rows = in_ref.shape[2]
    for a in range(in_ref.shape[0]):
        for k in range(FIELDS):
            i, half = divmod(a * FIELDS + k, 2)
            half = pl.ds(half * EDGE, EDGE)
            one, two = one_ref[i, half, :], two_ref[i, half, :]
            state_ref[a, k, pl.ds(0, EDGE), :] = jnp.where(rotor, one, two)
            state_ref[a, k, pl.ds(EDGE, rows), :] = in_ref[a, k]
            state_ref[a, k, pl.ds(EDGE + rows, EDGE), :] = jnp.where(rotor, two, one)
    co = coefficients(flag_ref[0], cycle_cells)
    write_sends(state_ref, co, *sends)


def local_kernel(cycle_cells, flag_ref, weight_ref, old_ref, now_ref, base_ref, nxt_s, prv_s, up_s, dn_s):
    segment, segments = flag_ref[0], flag_ref[1]
    co = coefficients(segment, cycle_cells)
    lane, place = lanes_of()
    low = lane < HALF
    pairs = now_ref.shape[0]
    blocks = now_ref.shape[2] // SUB
    at_inner, at_outer = segment == 0, segment == segments - 1
    is_inner, is_outer = place == 0, place == HALF - 1
    low_half, low_weight = 0.5 * (co["r"] - 1.0), co["r"] - 0.5
    high_half, high_weight = 0.5 * (co["r"] + 1.0), co["r"] + 0.5
    zero = jnp.zeros((SUB, LANES), jnp.float32)
    low_half = jnp.where(at_inner, low_half, zero)
    low_weight = jnp.where(at_inner, low_weight, zero)
    high_half = jnp.where(at_outer, high_half, zero)
    high_weight = jnp.where(at_outer, high_weight, zero)
    rows_end = blocks * SUB
    for k in range(FIELDS):
        nxt_s[k, pl.ds(0, SUB), :] = zero
        prv_s[k, pl.ds(rows_end, SUB), :] = zero

    def pair(a, carry):
        for b in range(blocks):
            rows = pl.ds(b * SUB, SUB)
            c = cell([now_ref[a, k, rows, :] for k in range(FIELDS)])
            to_out, to_in = radial_terms(c, co)
            inner = wall_terms(c, low_half, low_weight, 1.0)
            outer = wall_terms(c, high_half, high_weight, -1.0)
            centre = centre_terms(c, co)
            nxt, prv = theta_terms(c, co)
            above, below = axial_terms(c)
            for k in range(FIELDS):
                inside = jnp.where(is_inner, inner[k], pltpu.roll(to_out[k], 1, 1))
                outside = jnp.where(is_outer, outer[k], pltpu.roll(to_in[k], LANES - 1, 1))
                total = co["inv_r"] * (inside + outside)
                if centre[k] is not None:
                    total = total + centre[k]
                nxt_s[k, pl.ds(b * SUB + SUB, SUB), :] = nxt[k]
                prv_s[k, rows, :] = prv[k]
                swapped_up = pltpu.roll(above[k], HALF, 1)
                swapped_dn = pltpu.roll(below[k], HALF, 1)
                total = total + jnp.where(low, swapped_dn, swapped_up)
                base_ref[a, k, rows, :] = total
                up_s[a, k, rows, :] = swapped_up
                dn_s[a, k, rows, :] = swapped_dn
        for b in range(blocks):
            rows = pl.ds(b * SUB, SUB)
            for k in range(FIELDS):
                base_ref[a, k, rows, :] = (
                    base_ref[a, k, rows, :]
                    + nxt_s[k, pl.ds(b * SUB + SUB - 1, SUB), :]
                    + prv_s[k, pl.ds(b * SUB + 1, SUB), :]
                )
        return carry

    lax.fori_loop(0, pairs, pair, 0)
    old_w, now_w, rate_w = weight_ref[0], weight_ref[1], weight_ref[2]

    def finish(a, carry):
        lower = jnp.maximum(a - 1, 0)
        upper = jnp.minimum(a + 1, pairs - 1)
        has_upper = a < pairs - 1
        first = a == 0
        for b in range(blocks):
            rows = pl.ds(b * SUB, SUB)
            for k in range(FIELDS):
                from_below = up_s[lower, k, rows, :]
                from_below = jnp.where(first, pltpu.roll(from_below, HALF, 1), from_below)
                from_above = jnp.where(has_upper, dn_s[upper, k, rows, :], zero)
                rate = base_ref[a, k, rows, :] + jnp.where(low, from_below, from_above)
                base_ref[a, k, rows, :] = (
                    old_w * old_ref[a, k, rows, :] + now_w * now_ref[a, k, rows, :] + rate_w * rate
                )
        return carry

    lax.fori_loop(0, pairs, finish, 0)


def join_kernel(cycle_cells, flag_ref, weight_ref, base_ref, turn_ref, turn2_ref, inside_ref,
                outside_ref, state_ref, own_ref, *sends):
    co = coefficients(flag_ref[0], cycle_cells)
    split, flip, shift, shift2 = flag_ref[2], flag_ref[3], flag_ref[4], flag_ref[5]
    rate_w = weight_ref[2]
    lane, place = lanes_of()
    pairs = base_ref.shape[0]
    blocks = base_ref.shape[2] // SUB
    rows_all = blocks * SUB
    row_id = lax.broadcasted_iota(jnp.int32, (rows_all, LANES), 0)
    from_first = (row_id >= split) != (flip == 1)
    upper_half = lax.broadcasted_iota(jnp.int32, (rows_all, LANES), 1) >= HALF
    weight_r = rate_w * co["inv_r"]
    at_low = jnp.where(place == 0, weight_r, 0.0)
    at_high = jnp.where(place == HALF - 1, weight_r, 0.0)

    def opened(value):
        both = jnp.concatenate([pltpu.roll(value, HALF, 1), value], axis=0)
        return both[:rows_all]

    for b in range(blocks):
        rows = pl.ds(b * SUB, SUB)
        inside, outside = inside_ref[rows, :], outside_ref[rows, :]
        for a in range(pairs):
            for k in range(FIELDS):
                j = a * FIELDS + k
                moved = pltpu.roll(inside, LANES - j, 1) if j else inside
                value = base_ref[a, k, rows, :] + at_low * moved
                value = value + at_high * pltpu.roll(outside, HALF - 1 - j, 1)
                state_ref[a, k, rows, :] = value
    for k in range(FIELDS):
        mixed = jnp.where(
            from_first,
            pltpu.roll(opened(turn_ref[k]), shift, 0),
            pltpu.roll(opened(turn2_ref[k]), shift2, 0),
        )
        turned = jnp.where(upper_half, mixed, 0.0)
        signed = -rate_w if k == 3 else rate_w
        state_ref[pairs - 1, k] = state_ref[pairs - 1, k] + signed * turned
    for a in range(pairs):
        for k in range(FIELDS):
            own_ref[a, k] = state_ref[a, k, pl.ds(EDGE, own_ref.shape[2]), :]
    write_sends(state_ref, co, *sends)


def body(density, velocity, pressure, offsets):
    n_ax, n_az = lax.axis_size("ax"), lax.axis_size("az")
    planes, tile, cells = density.shape[1:]
    cycle_cells = tile * n_az
    is_rotor = lax.axis_index("row") == 0

    vmem = pl.BlockSpec(memory_space=pltpu.VMEM)
    smem = pl.BlockSpec(memory_space=pltpu.SMEM)
    struct = lambda *shape: jax.ShapeDtypeStruct(shape, jnp.float32)
    tall = tile + 2 * EDGE
    block = struct(n_ax, FIELDS, tall, LANES)
    own = struct(n_ax, FIELDS, tile, LANES)
    outer_rows = struct(n_ax * FIELDS // 2, 2 * EDGE, LANES)
    half_rows = -(-(tall // SUB) // 2) * SUB
    sends = (struct(FIELDS, half_rows, LANES), struct(tall, LANES), struct(tall, LANES))

    def device(row, ax, az):
        return (row * n_ax + ax) * n_az + az

    every = [(row, ax, az) for row in range(2) for ax in range(n_ax) for az in range(n_az)]

    def along_ax(by):
        return [
            (device(r, x, z), device(r, x + by, z)) for r, x, z in every if 0 <= x + by < n_ax
        ]

    def turned(by):
        pairs = []
        for x in range(n_ax):
            for z in range(n_az):
                pairs.append((device(1, x, (z + by) % n_az), device(0, x, z)))
                pairs.append((device(0, x, z), device(1, x, (z + by) % n_az)))
        return pairs

    def call(kernel, outs, n_smem, n_vmem, scratch=()):
        return pl.pallas_call(
            kernel,
            out_shape=outs,
            in_specs=[smem] * n_smem + [vmem] * n_vmem,
            out_specs=jax.tree.map(lambda _: vmem, outs),
            scratch_shapes=list(scratch),
            cost_estimate=pl.CostEstimate(
                flops=8_000_000, bytes_accessed=3_000_000, transcendentals=0
            ),
        )

    kernel_of = lambda kernel: functools.partial(kernel, cycle_cells)
    taller = pltpu.VMEM((FIELDS, tall + SUB, LANES), jnp.float32)
    whole = pltpu.VMEM(block.shape, jnp.float32)

    chunks = call(pack_kernel, own, 0, 3)(density[0], velocity[0], pressure[0])
    whole_tile = lax.all_to_all(chunks, "ax", 0, 0, tiled=True)

    segment = lax.axis_index("ax")
    flags, turns, weights = [], [], []
    for step, (old_w, now_w) in enumerate(((0.0, 1.0), (0.75, 0.25), (1.0 / 3.0, 2.0 / 3.0))):
        rest = offsets[step] % tile
        turns.append(offsets[step] // tile)
        flags.append(jnp.stack([
            segment,
            jnp.full_like(segment, n_ax),
            jnp.where(is_rotor, tile + EDGE - rest, EDGE + rest),
            jnp.where(is_rotor, 1, 0),
            jnp.where(is_rotor, (tall - rest) % tall, rest),
            jnp.where(is_rotor, tile - rest, rest + tall - tile),
            jnp.where(is_rotor, 1, 0),
        ]).astype(jnp.int32))
        weights.append(jnp.array([old_w, now_w, now_w * TIME_STEP], dtype=jnp.float32))
    up_rows, down_rows = call(edge_kernel, (outer_rows, outer_rows), 1, 1)(flags[0], whole_tile)
    up_rows = lax.ppermute(up_rows, AXES, turned(1))
    down_rows = lax.ppermute(down_rows, AXES, turned(n_az - 1))
    up_rows = lax.ppermute(up_rows, AXES, turned(0))
    down_rows = lax.ppermute(down_rows, AXES, turned(0))
    start, *first = call(kernel_of(first_kernel), (block, *sends), 1, 3)(
        flags[0], whole_tile, up_rows, down_rows
    )
    carry = (start, whole_tile, *first)

    def local(flag, weight, now):
        return call(kernel_of(local_kernel), block, 2, 2, (taller, taller, whole, whole))(
            flag, weight, start, now
        )

    def around(out, inn):
        return (
            lax.ppermute(out, AXES, along_ax(1)),
            lax.ppermute(inn, AXES, along_ax(-1)),
        )

    def branch(by):
        def run(flag, weight, now, up, *edges):
            ghosts = (
                lax.ppermute(up, AXES, turned(by)),
                lax.ppermute(up, AXES, turned((by + 1) % n_az)),
            )
            if IN_BRANCH:
                ghosts += around(*edges)
                ghosts += (local(flag, weight, now),)
            return ghosts
        return run

    def substep(_, carry):
        now, _, up, *edges = carry[:5]
        turns, flags, weights = carry[5:]
        flag, weight = flags[0], weights[0]
        if not IN_BRANCH:
            halos = around(*edges)
        ghosts = lax.switch(
            turns[0], [branch(by) for by in range(n_az)], flag, weight, now, up, *edges
        )
        if IN_BRANCH:
            *ghosts, base = ghosts
        else:
            ghosts = (*ghosts, *halos)
            base = local(flag, weight, now)
        state = call(kernel_of(join_kernel), (block, own, *sends), 2, 5)(
            flag, weight, base, *ghosts
        )
        later = lambda kept: (*kept[1:], kept[0])
        return (*state, later(turns), later(flags), later(weights))

    carry = (*carry, tuple(turns), tuple(flags), tuple(weights))
    if LOOP:
        carry = lax.fori_loop(0, 3, substep, carry)
    else:
        for step in range(3):
            carry = substep(step, carry)
    chunks = lax.all_to_all(carry[1], "ax", 0, 0, tiled=True)
    return call(unpack_kernel, struct(FIELDS, planes, tile, cells), 0, 1)(chunks)[None]


def solution(mesh):
    placed = (
        P("row", "ax", "az", None),
        P("row", None, "ax", "az", None),
        P("row", "ax", "az", None),
        P(),
    )
    return jax.shard_map(
        body,
        mesh=mesh,
        in_specs=placed,
        out_specs=P("row", None, "ax", "az", None),
        check_vma=False,
    )
```

profile of v0, /device:TPU:16, one launch (start us, length us, event | category | flops | bytes accessed | tf_op | source)
XLA Modules:
  0.0 133.9 jit_solution(6522222726762442384)
XLA Ops:
  0.0 2.2 %shard_map.73 = f32[8,5,32,128]{3,2,1,0:T(8,128)} custom-call(f32[2,32,512]{2,1,0:T(8,128)} %bitcast.19, f32[3,2,32,512]{3,2,1,0:T(8,128)} %bitcast.18, f32[2,32,512]{2,1,0:T(8,128)} %bitcast.20), custom_call_target="tpu_custom_call" | custom-call | flops 8000000 | bytes 3000000 | tf_op jit(solution)/shard_map/pallas_call | solution.py:400
  2.2 6.1 %all-to-all-start = ((f32[8,5,32,128]{3,2,1,0:T(8,128)}), f32[8,5,32,128]{3,2,1,0:T(8,128)S(1)}, u32[]{:S(2)}, u32[]{:S(2)}) async-start(f32[8,5,32,128]{3,2,1,0:T(8,128)} %shard_map.73), calls=%async_computation | async-start | bytes 1310720 | tf_op jit(solution)/shard_map/all_to_all | solution.py:401
  8.3 0.6 copy-done.4
  8.9 0.6 fusion
  11.3 0.1 stack.54.flag_ref
  11.4 8.4 %all-to-all-done.in_ref = f32[8,5,32,128]{3,2,1,0:T(8,128)S(1)} async-done(((f32[8,5,32,128]{3,2,1,0:T(8,128)}), f32[8,5,32,128]{3,2,1,0:T(8,128)S(1)}, u32[]{:S(2)}, u32[]{:S(2)}) %all-to-all-start) | async-done | bytes 655392 | tf_op jit(solution)/shard_map/all_to_all | solution.py:401
  19.8 1.2 shard_map.74
  21.0 1.9 %collective-permute-start.128 = (f32[20,8,128]{2,1,0:T(8,128)}, f32[20,8,128]{2,1,0:T(8,128)S(1)}, u32[]{:S(2)}, u32[]{:S(2)}) collective-permute-start(f32[20,8,128]{2,1,0:T(8,128)} %get-tuple-element.774), channel_id=1, source_target_pairs={{257,0},{0,257},{258,1},{1,258},{259,2},{2,259},{260,3},{3,260},{2... | collective-permute-start | bytes 245768 | tf_op jit(solution)/shard_map/ppermute | solution.py:419
  22.9 3.1 %collective-permute-start.130 = (f32[20,8,128]{2,1,0:T(8,128)}, f32[20,8,128]{2,1,0:T(8,128)S(1)}, u32[]{:S(2)}, u32[]{:S(2)}) collective-permute-start(f32[20,8,128]{2,1,0:T(8,128)} %get-tuple-element.775), channel_id=1, source_target_pairs={{287,0},{0,287},{256,1},{1,256},{257,2},{2,257},{258,3},{3,258},{2... | collective-permute-start | bytes 245768 | tf_op jit(solution)/shard_map/ppermute | solution.py:420
  26.0 0.9 collective-permute-done.128
  26.9 2.3 %collective-permute-start.129 = (f32[20,8,128]{2,1,0:T(8,128)S(1)}, f32[20,8,128]{2,1,0:T(8,128)S(1)}, u32[]{:S(2)}, u32[]{:S(2)}) collective-permute-start(f32[20,8,128]{2,1,0:T(8,128)S(1)} %collective-permute-done.128), channel_id=1, source_target_pairs={{256,0},{0,256},{257,1},{1,257},{258,2},{2,258},{259,3},{3,259},{2... | collective-permute-start | bytes 245768 | tf_op jit(solution)/shard_map/ppermute | solution.py:421
  29.2 0.0 collective-permute-done.130
  29.2 2.3 %collective-permute-start.131 = (f32[20,8,128]{2,1,0:T(8,128)S(1)}, f32[20,8,128]{2,1,0:T(8,128)S(1)}, u32[]{:S(2)}, u32[]{:S(2)}) collective-permute-start(f32[20,8,128]{2,1,0:T(8,128)S(1)} %collective-permute-done.130), channel_id=1, source_target_pairs={{256,0},{0,256},{257,1},{1,257},{258,2},{2,258},{259,3},{3,259},{2... | collective-permute-start | bytes 245768 | tf_op jit(solution)/shard_map/ppermute | solution.py:422
  37.4 0.1 stack.62
  37.5 0.1 stack.58
  37.6 0.0 collective-permute-done.129.one_ref
  37.6 0.0 collective-permute-done.131.two_ref
  37.6 0.6 copy-done.2
  38.2 0.6 copy-done.3
  38.8 1.5 %shard_map.75 = (f32[8,5,40,128]{3,2,1,0:T(8,128)S(1)}, f32[5,24,128]{2,1,0:T(8,128)S(1)}, f32[40,128]{1,0:T(8,128)S(1)}, f32[40,128]{1,0:T(8,128)S(1)}) custom-call(s32[7]{0:T(128)S(1)} %stack.54.flag_ref, f32[8,5,32,128]{3,2,1,0:T(8,128)S(1)} %all-to-all-done.in_ref, f32[20,8,128]{2,1,0:T(8,128)} %copy-done.2, f32[20,8,128]{2,1,0:T(8,128)} %copy-done.3), custom_call_target="tpu_custom_call" | custom-call | flops 8000000 | bytes 3000000 | tf_op jit(solution)/shard_map/pallas_call | solution.py:423
  40.3 0.0 copy-done.1
  40.3 0.1 copy.169
  40.4 0.0 copy-start
  40.4 0.0 copy-start.5
  40.4 0.0 copy-start.6
  40.4 0.6 copy-done
  41.0 0.0 copy-done.5
  41.1 0.0 copy-done.6
  41.1 76.7 %while.36 = (s32[]{:T(128)}, f32[8,5,40,128]{3,2,1,0:T(8,128)S(1)}, f32[8,5,32,128]{3,2,1,0:T(8,128)}, f32[5,24,128]{2,1,0:T(8,128)S(1)}, f32[40,128]{1,0:T(8,12...) while((s32[]{:T(128)}, f32[8,5,40,128]{3,2,1,0:T(8,128)S(1)}, ...), condition=%wide.region_33.34_spmd, body=%wide.region_0.33_spmd.sunk | while | flops 16000003 | bytes 6656157 | solution.py:473
  41.1 29.5 %conditional.2 = (f32[5,24,128]{2,1,0:T(8,128)}, f32[5,24,128]{2,1,0:T(8,128)}, f32[40,128]{1,0:T(8,128)}, f32[40,128]{1,0:T(8,128)}, f32[8,5,40,128]{3,2,1,0:T(8,128)S(1)}) conditional(s32[]{:T(128)} %clamp.4, (f32[5,24,128]{2,1,0:T(8,128)S(1)}, f32[40,128]{1,0:T(8,128)S(1)}, f32[40,128]{1,0:T(8,128)S(1)}, ...), branch_computations={%region_1.1_spmd, %region_2.2_spmd, %region_3.3_spmd, %region_4.4_... | conditional | flops 8000000 | bytes 3655560 | solution.py:457
  41.2 13.8 %collective-permute-start.109 = (f32[5,24,128]{2,1,0:T(8,128)S(1)}, f32[5,24,128]{2,1,0:T(8,128)}, u32[]{:S(2)}, u32[]{:S(2)}) collective-permute-start(f32[5,24,128]{2,1,0:T(8,128)S(1)} %get-tuple-element.706), channel_id=1, source_target_pairs={{284,0},{0,284},{285,1},{1,285},{286,2},{2,286},{287,3},{3,287},{2... | collective-permute-start | bytes 184328 | tf_op jit(solution)/shard_map/while/body/eval_jaxpr/cond/branch_27_fun/ppermute | solution.py:443
  55.0 6.5 %collective-permute-start.108 = (f32[5,24,128]{2,1,0:T(8,128)S(1)}, f32[5,24,128]{2,1,0:T(8,128)}, u32[]{:S(2)}, u32[]{:S(2)}) collective-permute-start(f32[5,24,128]{2,1,0:T(8,128)S(1)} %get-tuple-element.706), channel_id=1, source_target_pairs={{283,0},{0,283},{284,1},{1,284},{285,2},{2,285},{286,3},{3,286},{2... | collective-permute-start | bytes 184328 | tf_op jit(solution)/shard_map/while/body/eval_jaxpr/cond/branch_27_fun/ppermute | solution.py:442
  61.5 3.4 %collective-permute-start.110 = (f32[40,128]{1,0:T(8,128)S(1)}, f32[40,128]{1,0:T(8,128)}, u32[]{:S(2)}, u32[]{:S(2)}) collective-permute-start(f32[40,128]{1,0:T(8,128)S(1)} %get-tuple-element.707), channel_id=1, source_target_pairs={{0,32},{1,33},{2,34},{3,35},{4,36},{5,37},{6,38},{7,39},{8,40},{9,... | collective-permute-start | bytes 61448 | tf_op jit(solution)/shard_map/while/body/eval_jaxpr/cond/branch_27_fun/ppermute | solution.py:435
  64.9 1.3 collective-permute-start.111
  66.1 2.9 %branch_27_fun.1 = f32[8,5,40,128]{3,2,1,0:T(8,128)S(1)} custom-call(s32[7]{0:T(128)S(1)} %get-tuple-element.709.flag_ref, f32[3]{0:T(128)S(1)} %get-tuple-element.710.weight_ref, f32[8,5,40,128]{3,2,1,0:T(8,128)S(1)} %get-tuple-element.711.old_ref, f32[8,5,40,128]{3,2,1,0:T(8,128)S(1)} %get-tuple-element.712.now_ref), custom_call_target="tpu_custom_call" | custom-call | flops 8000000 | bytes 3000000 | tf_op jit(solution)/shard_map/while/body/eval_jaxpr/cond/branch_27_fun/pallas_call | solution.py:429
  69.0 0.0 collective-permute-done.110
  69.0 1.6 %collective-permute-done.111 = f32[40,128]{1,0:T(8,128)} collective-permute-done((f32[40,128]{1,0:T(8,128)S(1)}, f32[40,128]{1,0:T(8,128)}, u32[]{:S(2)}, u32[]{:S(2)}) %collective-permute-start.111) | collective-permute-done | bytes 20512 | tf_op jit(solution)/shard_map/while/body/eval_jaxpr/cond/branch_27_fun/ppermute | solution.py:436
  70.6 0.0 collective-permute-done.109
  70.6 0.0 collective-permute-done.108
  70.6 2.7 %eval_jaxpr.1 = (f32[8,5,40,128]{3,2,1,0:T(8,128)S(1)}, f32[8,5,32,128]{3,2,1,0:T(8,128)}, f32[5,24,128]{2,1,0:T(8,128)S(1)}, f32[40,128]{1,0:T(8,128)S(1)}, f32[40,128]{1,0:T(8,128)S(1)}) custom-call(s32[7]{0:T(128)S(1)} %get-tuple-element.1119.flag_ref, f32[3]{0:T(128)S(1)} %get-tuple-element.1122.weight_ref, ...), custom_call_target="tpu_custom_call" | custom-call | flops 8000000 | bytes 3000000 | tf_op jit(solution)/shard_map/while/body/eval_jaxpr/pallas_call | solution.py:465
  73.5 20.3 %conditional.2 = (f32[5,24,128]{2,1,0:T(8,128)}, f32[5,24,128]{2,1,0:T(8,128)}, f32[40,128]{1,0:T(8,128)}, f32[40,128]{1,0:T(8,128)}, f32[8,5,40,128]{3,2,1,0:T(8,128)S(1)}) conditional(s32[]{:T(128)} %clamp.4, (f32[5,24,128]{2,1,0:T(8,128)S(1)}, f32[40,128]{1,0:T(8,128)S(1)}, f32[40,128]{1,0:T(8,128)S(1)}, ...), branch_computations={%region_1.1_spmd, %region_2.2_spmd, %region_3.3_spmd, %region_4.4_... | conditional | flops 8000000 | bytes 3655560 | solution.py:457
  73.5 1.9 %collective-permute-start.53 = (f32[5,24,128]{2,1,0:T(8,128)S(1)}, f32[5,24,128]{2,1,0:T(8,128)}, u32[]{:S(2)}, u32[]{:S(2)}) collective-permute-start(f32[5,24,128]{2,1,0:T(8,128)S(1)} %get-tuple-element.608), channel_id=1, source_target_pairs={{270,0},{0,270},{271,1},{1,271},{272,2},{2,272},{273,3},{3,273},{2... | collective-permute-start | bytes 184328 | tf_op jit(solution)/shard_map/while/body/eval_jaxpr/cond/branch_13_fun/ppermute | solution.py:443
  75.4 9.0 %collective-permute-start.52 = (f32[5,24,128]{2,1,0:T(8,128)S(1)}, f32[5,24,128]{2,1,0:T(8,128)}, u32[]{:S(2)}, u32[]{:S(2)}) collective-permute-start(f32[5,24,128]{2,1,0:T(8,128)S(1)} %get-tuple-element.608), channel_id=1, source_target_pairs={{269,0},{0,269},{270,1},{1,270},{271,2},{2,271},{272,3},{3,272},{2... | collective-permute-start | bytes 184328 | tf_op jit(solution)/shard_map/while/body/eval_jaxpr/cond/branch_13_fun/ppermute | solution.py:442
  84.4 3.6 %collective-permute-start.54 = (f32[40,128]{1,0:T(8,128)S(1)}, f32[40,128]{1,0:T(8,128)}, u32[]{:S(2)}, u32[]{:S(2)}) collective-permute-start(f32[40,128]{1,0:T(8,128)S(1)} %get-tuple-element.609), channel_id=1, source_target_pairs={{0,32},{1,33},{2,34},{3,35},{4,36},{5,37},{6,38},{7,39},{8,40},{9,... | collective-permute-start | bytes 61448 | tf_op jit(solution)/shard_map/while/body/eval_jaxpr/cond/branch_13_fun/ppermute | solution.py:435
  88.0 1.3 collective-permute-start.55
  89.3 2.9 %branch_13_fun.1 = f32[8,5,40,128]{3,2,1,0:T(8,128)S(1)} custom-call(s32[7]{0:T(128)S(1)} %get-tuple-element.611.flag_ref, f32[3]{0:T(128)S(1)} %get-tuple-element.612.weight_ref, f32[8,5,40,128]{3,2,1,0:T(8,128)S(1)} %get-tuple-element.613.old_ref, f32[8,5,40,128]{3,2,1,0:T(8,128)S(1)} %get-tuple-element.614.now_ref), custom_call_target="tpu_custom_call" | custom-call | flops 8000000 | bytes 3000000 | tf_op jit(solution)/shard_map/while/body/eval_jaxpr/cond/branch_13_fun/pallas_call | solution.py:429
  92.1 0.0 collective-permute-done.54
  92.2 1.6 %collective-permute-done.55 = f32[40,128]{1,0:T(8,128)} collective-permute-done((f32[40,128]{1,0:T(8,128)S(1)}, f32[40,128]{1,0:T(8,128)}, u32[]{:S(2)}, u32[]{:S(2)}) %collective-permute-start.55) | collective-permute-done | bytes 20512 | tf_op jit(solution)/shard_map/while/body/eval_jaxpr/cond/branch_13_fun/ppermute | solution.py:436
  93.8 0.0 collective-permute-done.53
  93.8 0.0 collective-permute-done.52
  93.8 2.7 %eval_jaxpr.1 = (f32[8,5,40,128]{3,2,1,0:T(8,128)S(1)}, f32[8,5,32,128]{3,2,1,0:T(8,128)}, f32[5,24,128]{2,1,0:T(8,128)S(1)}, f32[40,128]{1,0:T(8,128)S(1)}, f32[40,128]{1,0:T(8,128)S(1)}) custom-call(s32[7]{0:T(128)S(1)} %get-tuple-element.1119.flag_ref, f32[3]{0:T(128)S(1)} %get-tuple-element.1122.weight_ref, ...), custom_call_target="tpu_custom_call" | custom-call | flops 8000000 | bytes 3000000 | tf_op jit(solution)/shard_map/while/body/eval_jaxpr/pallas_call | solution.py:465
  96.6 18.5 %conditional.2 = (f32[5,24,128]{2,1,0:T(8,128)}, f32[5,24,128]{2,1,0:T(8,128)}, f32[40,128]{1,0:T(8,128)}, f32[40,128]{1,0:T(8,128)}, f32[8,5,40,128]{3,2,1,0:T(8,128)S(1)}) conditional(s32[]{:T(128)} %clamp.4, (f32[5,24,128]{2,1,0:T(8,128)S(1)}, f32[40,128]{1,0:T(8,128)S(1)}, f32[40,128]{1,0:T(8,128)S(1)}, ...), branch_computations={%region_1.1_spmd, %region_2.2_spmd, %region_3.3_spmd, %region_4.4_... | conditional | flops 8000000 | bytes 3655560 | solution.py:457
  96.6 3.4 %collective-permute-start.97 = (f32[5,24,128]{2,1,0:T(8,128)S(1)}, f32[5,24,128]{2,1,0:T(8,128)}, u32[]{:S(2)}, u32[]{:S(2)}) collective-permute-start(f32[5,24,128]{2,1,0:T(8,128)S(1)} %get-tuple-element.685), channel_id=1, source_target_pairs={{281,0},{0,281},{282,1},{1,282},{283,2},{2,283},{284,3},{3,284},{2... | collective-permute-start | bytes 184328 | tf_op jit(solution)/shard_map/while/body/eval_jaxpr/cond/branch_24_fun/ppermute | solution.py:443
  100.0 5.7 %collective-permute-start.96 = (f32[5,24,128]{2,1,0:T(8,128)S(1)}, f32[5,24,128]{2,1,0:T(8,128)}, u32[]{:S(2)}, u32[]{:S(2)}) collective-permute-start(f32[5,24,128]{2,1,0:T(8,128)S(1)} %get-tuple-element.685), channel_id=1, source_target_pairs={{280,0},{0,280},{281,1},{1,281},{282,2},{2,282},{283,3},{3,283},{2... | collective-permute-start | bytes 184328 | tf_op jit(solution)/shard_map/while/body/eval_jaxpr/cond/branch_24_fun/ppermute | solution.py:442
  105.7 3.6 %collective-permute-start.98 = (f32[40,128]{1,0:T(8,128)S(1)}, f32[40,128]{1,0:T(8,128)}, u32[]{:S(2)}, u32[]{:S(2)}) collective-permute-start(f32[40,128]{1,0:T(8,128)S(1)} %get-tuple-element.686), channel_id=1, source_target_pairs={{0,32},{1,33},{2,34},{3,35},{4,36},{5,37},{6,38},{7,39},{8,40},{9,... | collective-permute-start | bytes 61448 | tf_op jit(solution)/shard_map/while/body/eval_jaxpr/cond/branch_24_fun/ppermute | solution.py:435
  109.3 1.3 collective-permute-start.99
  110.6 2.9 %branch_24_fun.1 = f32[8,5,40,128]{3,2,1,0:T(8,128)S(1)} custom-call(s32[7]{0:T(128)S(1)} %get-tuple-element.688.flag_ref, f32[3]{0:T(128)S(1)} %get-tuple-element.689.weight_ref, f32[8,5,40,128]{3,2,1,0:T(8,128)S(1)} %get-tuple-element.690.old_ref, f32[8,5,40,128]{3,2,1,0:T(8,128)S(1)} %get-tuple-element.691.now_ref), custom_call_target="tpu_custom_call" | custom-call | flops 8000000 | bytes 3000000 | tf_op jit(solution)/shard_map/while/body/eval_jaxpr/cond/branch_24_fun/pallas_call | solution.py:429
  113.4 0.0 collective-permute-done.98
  113.4 1.6 %collective-permute-done.99 = f32[40,128]{1,0:T(8,128)} collective-permute-done((f32[40,128]{1,0:T(8,128)S(1)}, f32[40,128]{1,0:T(8,128)}, u32[]{:S(2)}, u32[]{:S(2)}) %collective-permute-start.99) | collective-permute-done | bytes 20512 | tf_op jit(solution)/shard_map/while/body/eval_jaxpr/cond/branch_24_fun/ppermute | solution.py:436
  115.1 0.0 collective-permute-done.97
  115.1 0.0 collective-permute-done.96
  115.1 2.7 %eval_jaxpr.1 = (f32[8,5,40,128]{3,2,1,0:T(8,128)S(1)}, f32[8,5,32,128]{3,2,1,0:T(8,128)}, f32[5,24,128]{2,1,0:T(8,128)S(1)}, f32[40,128]{1,0:T(8,128)S(1)}, f32[40,128]{1,0:T(8,128)S(1)}) custom-call(s32[7]{0:T(128)S(1)} %get-tuple-element.1119.flag_ref, f32[3]{0:T(128)S(1)} %get-tuple-element.1122.weight_ref, ...), custom_call_target="tpu_custom_call" | custom-call | flops 8000000 | bytes 3000000 | tf_op jit(solution)/shard_map/while/body/eval_jaxpr/pallas_call | solution.py:465
  117.8 13.9 %all_to_all.10.in_ref = f32[8,5,32,128]{3,2,1,0:T(8,128)} all-to-all(f32[8,5,32,128]{3,2,1,0:T(8,128)} %get-tuple-element.780), channel_id=1, replica_groups=mesh['row'=2,'ax'=8,'az'=32] {'ax'}, dimensions={0} | all-to-all | bytes 1310720 | tf_op jit(solution)/shard_map/all_to_all | solution.py:477
  131.7 2.2 %shard_map.76 = f32[5,2,32,512]{3,2,1,0:T(8,128)} custom-call(f32[8,5,32,128]{3,2,1,0:T(8,128)} %all_to_all.10.in_ref), custom_call_target="tpu_custom_call" | custom-call | flops 8000000 | bytes 3000000 | tf_op jit(solution)/shard_map/pallas_call | solution.py:478
  (28 shorter events, 0.1 us)
Async XLA Ops:
  2.2 17.6 %all-to-all-start = ((f32[8,5,32,128]{3,2,1,0:T(8,128)}), f32[8,5,32,128]{3,2,1,0:T(8,128)S(1)}, u32[]{:S(2)}, u32[]{:S(2)}) async-start(f32[8,5,32,128]{3,2,1,0:T(8,128)} %shard_map.73), calls=%async_computation | async-start | bytes 1310720 | tf_op jit(solution)/shard_map/all_to_all | solution.py:401
  8.3 0.7 copy-start.4
  19.8 20.6 %copy-start.1 = (f32[8,5,32,128]{3,2,1,0:T(8,128)}, f32[8,5,32,128]{3,2,1,0:T(8,128)S(1)}, u32[]{:S(2)}) copy-start(f32[8,5,32,128]{3,2,1,0:T(8,128)S(1)} %all-to-all-done.in_ref) | copy-start | bytes 1966084
  21.0 6.0 %collective-permute-start.128 = (f32[20,8,128]{2,1,0:T(8,128)}, f32[20,8,128]{2,1,0:T(8,128)S(1)}, u32[]{:S(2)}, u32[]{:S(2)}) collective-permute-start(f32[20,8,128]{2,1,0:T(8,128)} %get-tuple-element.774), channel_id=1, source_target_pairs={{257,0},{0,257},{258,1},{1,258},{259,2},{2,259},{260,3},{3,260},{2... | collective-permute-start | bytes 245768 | tf_op jit(solution)/shard_map/ppermute | solution.py:419
  22.9 6.3 %collective-permute-start.130 = (f32[20,8,128]{2,1,0:T(8,128)}, f32[20,8,128]{2,1,0:T(8,128)S(1)}, u32[]{:S(2)}, u32[]{:S(2)}) collective-permute-start(f32[20,8,128]{2,1,0:T(8,128)} %get-tuple-element.775), channel_id=1, source_target_pairs={{287,0},{0,287},{256,1},{1,256},{257,2},{2,257},{258,3},{3,258},{2... | collective-permute-start | bytes 245768 | tf_op jit(solution)/shard_map/ppermute | solution.py:420
  26.9 10.6 %collective-permute-start.129 = (f32[20,8,128]{2,1,0:T(8,128)S(1)}, f32[20,8,128]{2,1,0:T(8,128)S(1)}, u32[]{:S(2)}, u32[]{:S(2)}) collective-permute-start(f32[20,8,128]{2,1,0:T(8,128)S(1)} %collective-permute-done.128), channel_id=1, source_target_pairs={{256,0},{0,256},{257,1},{1,257},{258,2},{2,258},{259,3},{3,259},{2... | collective-permute-start | bytes 245768 | tf_op jit(solution)/shard_map/ppermute | solution.py:421
  29.2 8.4 %collective-permute-start.131 = (f32[20,8,128]{2,1,0:T(8,128)S(1)}, f32[20,8,128]{2,1,0:T(8,128)S(1)}, u32[]{:S(2)}, u32[]{:S(2)}) collective-permute-start(f32[20,8,128]{2,1,0:T(8,128)S(1)} %collective-permute-done.130), channel_id=1, source_target_pairs={{256,0},{0,256},{257,1},{1,257},{258,2},{2,258},{259,3},{3,259},{2... | collective-permute-start | bytes 245768 | tf_op jit(solution)/shard_map/ppermute | solution.py:422
  37.6 0.6 copy-start.2
  38.2 0.6 copy-start.3
  40.4 0.7 copy-start
  40.4 0.7 copy-start.5
  40.4 0.7 copy-start.6
  41.2 29.5 %collective-permute-start.109 = (f32[5,24,128]{2,1,0:T(8,128)S(1)}, f32[5,24,128]{2,1,0:T(8,128)}, u32[]{:S(2)}, u32[]{:S(2)}) collective-permute-start(f32[5,24,128]{2,1,0:T(8,128)S(1)} %get-tuple-element.706), channel_id=1, source_target_pairs={{284,0},{0,284},{285,1},{1,285},{286,2},{2,286},{287,3},{3,287},{2... | collective-permute-start | bytes 184328 | tf_op jit(solution)/shard_map/while/body/eval_jaxpr/cond/branch_27_fun/ppermute | solution.py:443
  55.0 15.6 %collective-permute-start.108 = (f32[5,24,128]{2,1,0:T(8,128)S(1)}, f32[5,24,128]{2,1,0:T(8,128)}, u32[]{:S(2)}, u32[]{:S(2)}) collective-permute-start(f32[5,24,128]{2,1,0:T(8,128)S(1)} %get-tuple-element.706), channel_id=1, source_target_pairs={{283,0},{0,283},{284,1},{1,284},{285,2},{2,285},{286,3},{3,286},{2... | collective-permute-start | bytes 184328 | tf_op jit(solution)/shard_map/while/body/eval_jaxpr/cond/branch_27_fun/ppermute | solution.py:442
  61.5 7.5 %collective-permute-start.110 = (f32[40,128]{1,0:T(8,128)S(1)}, f32[40,128]{1,0:T(8,128)}, u32[]{:S(2)}, u32[]{:S(2)}) collective-permute-start(f32[40,128]{1,0:T(8,128)S(1)} %get-tuple-element.707), channel_id=1, source_target_pairs={{0,32},{1,33},{2,34},{3,35},{4,36},{5,37},{6,38},{7,39},{8,40},{9,... | collective-permute-start | bytes 61448 | tf_op jit(solution)/shard_map/while/body/eval_jaxpr/cond/branch_27_fun/ppermute | solution.py:435
  64.9 5.8 %collective-permute-start.111 = (f32[40,128]{1,0:T(8,128)S(1)}, f32[40,128]{1,0:T(8,128)}, u32[]{:S(2)}, u32[]{:S(2)}) collective-permute-start(f32[40,128]{1,0:T(8,128)S(1)} %get-tuple-element.708), channel_id=1, source_target_pairs={{32,0},{33,1},{34,2},{35,3},{36,4},{37,5},{38,6},{39,7},{40,8},{41... | collective-permute-start | bytes 61448 | tf_op jit(solution)/shard_map/while/body/eval_jaxpr/cond/branch_27_fun/ppermute | solution.py:436
  73.5 20.3 %collective-permute-start.53 = (f32[5,24,128]{2,1,0:T(8,128)S(1)}, f32[5,24,128]{2,1,0:T(8,128)}, u32[]{:S(2)}, u32[]{:S(2)}) collective-permute-start(f32[5,24,128]{2,1,0:T(8,128)S(1)} %get-tuple-element.608), channel_id=1, source_target_pairs={{270,0},{0,270},{271,1},{1,271},{272,2},{2,272},{273,3},{3,273},{2... | collective-permute-start | bytes 184328 | tf_op jit(solution)/shard_map/while/body/eval_jaxpr/cond/branch_13_fun/ppermute | solution.py:443
  75.4 18.3 %collective-permute-start.52 = (f32[5,24,128]{2,1,0:T(8,128)S(1)}, f32[5,24,128]{2,1,0:T(8,128)}, u32[]{:S(2)}, u32[]{:S(2)}) collective-permute-start(f32[5,24,128]{2,1,0:T(8,128)S(1)} %get-tuple-element.608), channel_id=1, source_target_pairs={{269,0},{0,269},{270,1},{1,270},{271,2},{2,271},{272,3},{3,272},{2... | collective-permute-start | bytes 184328 | tf_op jit(solution)/shard_map/while/body/eval_jaxpr/cond/branch_13_fun/ppermute | solution.py:442
  84.4 7.7 %collective-permute-start.54 = (f32[40,128]{1,0:T(8,128)S(1)}, f32[40,128]{1,0:T(8,128)}, u32[]{:S(2)}, u32[]{:S(2)}) collective-permute-start(f32[40,128]{1,0:T(8,128)S(1)} %get-tuple-element.609), channel_id=1, source_target_pairs={{0,32},{1,33},{2,34},{3,35},{4,36},{5,37},{6,38},{7,39},{8,40},{9,... | collective-permute-start | bytes 61448 | tf_op jit(solution)/shard_map/while/body/eval_jaxpr/cond/branch_13_fun/ppermute | solution.py:435
  88.0 5.8 %collective-permute-start.55 = (f32[40,128]{1,0:T(8,128)S(1)}, f32[40,128]{1,0:T(8,128)}, u32[]{:S(2)}, u32[]{:S(2)}) collective-permute-start(f32[40,128]{1,0:T(8,128)S(1)} %get-tuple-element.610), channel_id=1, source_target_pairs={{32,0},{33,1},{34,2},{35,3},{36,4},{37,5},{38,6},{39,7},{40,8},{41... | collective-permute-start | bytes 61448 | tf_op jit(solution)/shard_map/while/body/eval_jaxpr/cond/branch_13_fun/ppermute | solution.py:436
  96.6 18.4 %collective-permute-start.97 = (f32[5,24,128]{2,1,0:T(8,128)S(1)}, f32[5,24,128]{2,1,0:T(8,128)}, u32[]{:S(2)}, u32[]{:S(2)}) collective-permute-start(f32[5,24,128]{2,1,0:T(8,128)S(1)} %get-tuple-element.685), channel_id=1, source_target_pairs={{281,0},{0,281},{282,1},{1,282},{283,2},{2,283},{284,3},{3,284},{2... | collective-permute-start | bytes 184328 | tf_op jit(solution)/shard_map/while/body/eval_jaxpr/cond/branch_24_fun/ppermute | solution.py:443
  100.0 15.1 %collective-permute-start.96 = (f32[5,24,128]{2,1,0:T(8,128)S(1)}, f32[5,24,128]{2,1,0:T(8,128)}, u32[]{:S(2)}, u32[]{:S(2)}) collective-permute-start(f32[5,24,128]{2,1,0:T(8,128)S(1)} %get-tuple-element.685), channel_id=1, source_target_pairs={{280,0},{0,280},{281,1},{1,281},{282,2},{2,282},{283,3},{3,283},{2... | collective-permute-start | bytes 184328 | tf_op jit(solution)/shard_map/while/body/eval_jaxpr/cond/branch_24_fun/ppermute | solution.py:442
  105.7 7.7 %collective-permute-start.98 = (f32[40,128]{1,0:T(8,128)S(1)}, f32[40,128]{1,0:T(8,128)}, u32[]{:S(2)}, u32[]{:S(2)}) collective-permute-start(f32[40,128]{1,0:T(8,128)S(1)} %get-tuple-element.686), channel_id=1, source_target_pairs={{0,32},{1,33},{2,34},{3,35},{4,36},{5,37},{6,38},{7,39},{8,40},{9,... | collective-permute-start | bytes 61448 | tf_op jit(solution)/shard_map/while/body/eval_jaxpr/cond/branch_24_fun/ppermute | solution.py:435
  109.3 5.8 %collective-permute-start.99 = (f32[40,128]{1,0:T(8,128)S(1)}, f32[40,128]{1,0:T(8,128)}, u32[]{:S(2)}, u32[]{:S(2)}) collective-permute-start(f32[40,128]{1,0:T(8,128)S(1)} %get-tuple-element.687), channel_id=1, source_target_pairs={{32,0},{33,1},{34,2},{35,3},{36,4},{37,5},{38,6},{39,7},{40,8},{41... | collective-permute-start | bytes 61448 | tf_op jit(solution)/shard_map/while/body/eval_jaxpr/cond/branch_24_fun/ppermute | solution.py:436
where the time goes:
time: 136 us; the launch traced here: 134 us
  starting transfers between devices  70.3 us (52%)
  Pallas kernels  23.8 us (18%)
  waiting for transfers between devices  14.1 us (10%)
  blocking collectives  13.9 us (10%)
  between operations  7.74 us (6%)
  local copies, waits for them, and re-layouts  3.58 us (3%)
    ppermute x3, starting transfers between devices, run(): lax.ppermute(up, AXES, turned(by))  21.2 us
    ppermute x3, starting transfers between devices, run(): lax.ppermute(up, AXES, turned((by + 1) % n_az))  19.1 us
    all_to_all x1, blocking collectives, body(): chunks = lax.all_to_all(carry[1], 'ax', 0, 0, tiled=True)  13.9 us
    ppermute x3, starting transfers between devices, around(): lax.ppermute(out, AXES, along_ax(1))  10.5 us
    pallas_call x3, Pallas kernels, local(): call(kernel_of(local_kernel), block, 2, 2, (taller, taller, whole, whole))  8.55 us
    all_to_all x1, waiting for transfers between devices, body(): whole_tile = lax.all_to_all(chunks, 'ax', 0, 0, tiled=True)  8.36 us
    pallas_call x3, Pallas kernels, substep(): call(kernel_of(join_kernel), (block, own, *sends), 2, 5)  8.21 us
    all_to_all x1, starting transfers between devices, body(): whole_tile = lax.all_to_all(chunks, 'ax', 0, 0, tiled=True)  6.11 us
  transfers between devices with their start and end apart: 17, of which 5 were waited for; matrix products, arithmetic and copies ran while one was open for 1% of the time, Pallas kernels for 6%

commit v1 on v0

--- a/solution.py
+++ b/solution.py
@@ -19,8 +19,6 @@
 LANES = 128
 HALF = 64
 EDGE = 4
-IN_BRANCH = True
-LOOP = True
 
 
 def cell(state):
@@ -128,6 +126,19 @@
         r=r, half_r=0.5 * r, inv_r=inv_r, half_arc=1.0 / (2.0 * r * dtheta), arc2=arc2,
         cross=1.0 / (r * r * dtheta), centre=2.0 * arc2 + 2.0 + 2.0 * AXIAL_CURVE,
     )
+
+
+def weights_of(step):
+    first, second = step == 0, step == 1
+    old = jnp.where(first, 0.0, jnp.where(second, 0.75, 1.0 / 3.0))
+    now = jnp.where(first, 1.0, jnp.where(second, 0.25, 2.0 / 3.0))
+    return old, now, now * TIME_STEP
+
+
+def decode(code_ref, segments):
+    code = code_ref[0]
+    place = lax.div(code, 4)
+    return lax.rem(code, 4), lax.rem(place, segments), lax.div(place, segments) == 1
 
 
 def pack_kernel(rho_ref, vel_ref, press_ref, out_ref):
@@ -150,9 +161,9 @@
                 out_ref[2 * w + 1, k, rows, :] = jnp.where(low, pltpu.roll(first, HALF, 1), second)
 
 
-def edge_kernel(flag_ref, in_ref, up_ref, down_ref):
+def edge_kernel(code_ref, in_ref, up_ref, down_ref):
     front = lax.broadcasted_iota(jnp.int32, (SUB, LANES), 0) < EDGE
-    rotor = flag_ref[6] == 1
+    _, _, rotor = decode(code_ref, in_ref.shape[0])
     end = pl.ds(in_ref.shape[2] - SUB, SUB)
     for i in range(up_ref.shape[0]):
         one, two = divmod(2 * i, FIELDS), divmod(2 * i + 1, FIELDS)
@@ -209,8 +220,8 @@
             up_ref[k, pl.ds(b * SUB, SUB), :] = value
 
 
-def first_kernel(cycle_cells, flag_ref, in_ref, one_ref, two_ref, state_ref, *sends):
-    rotor = flag_ref[6] == 1
+def first_kernel(cycle_cells, code_ref, in_ref, one_ref, two_ref, state_ref, *sends):
+    _, segment, rotor = decode(code_ref, in_ref.shape[0])
     rows = in_ref.shape[2]
     for a in range(in_ref.shape[0]):
         for k in range(FIELDS):
@@ -220,12 +231,13 @@
             state_ref[a, k, pl.ds(0, EDGE), :] = jnp.where(rotor, one, two)
             state_ref[a, k, pl.ds(EDGE, rows), :] = in_ref[a, k]
             state_ref[a, k, pl.ds(EDGE + rows, EDGE), :] = jnp.where(rotor, two, one)
-    co = coefficients(flag_ref[0], cycle_cells)
+    co = coefficients(segment, cycle_cells)
     write_sends(state_ref, co, *sends)
 
 
-def local_kernel(cycle_cells, flag_ref, weight_ref, old_ref, now_ref, base_ref, nxt_s, prv_s, up_s, dn_s):
-    segment, segments = flag_ref[0], flag_ref[1]
+def local_kernel(cycle_cells, code_ref, old_ref, now_ref, base_ref, nxt_s, prv_s, up_s, dn_s):
+    segments = now_ref.shape[0]
+    step, segment, _ = decode(code_ref, segments)
     co = coefficients(segment, cycle_cells)
     lane, place = lanes_of()
     low = lane < HALF
@@ -280,7 +292,7 @@
         return carry
 
     lax.fori_loop(0, pairs, pair, 0)
-    old_w, now_w, rate_w = weight_ref[0], weight_ref[1], weight_ref[2]
+    old_w, now_w, rate_w = weights_of(step)
 
     def finish(a, carry):
         lower = jnp.maximum(a - 1, 0)
@@ -302,17 +314,22 @@
     lax.fori_loop(0, pairs, finish, 0)
 
 
-def join_kernel(cycle_cells, flag_ref, weight_ref, base_ref, turn_ref, turn2_ref, inside_ref,
+def join_kernel(cycle_cells, code_ref, offsets_ref, base_ref, turn_ref, turn2_ref, inside_ref,
                 outside_ref, state_ref, own_ref, *sends):
-    co = coefficients(flag_ref[0], cycle_cells)
-    split, flip, shift, shift2 = flag_ref[2], flag_ref[3], flag_ref[4], flag_ref[5]
-    rate_w = weight_ref[2]
+    step, segment, rotor = decode(code_ref, base_ref.shape[0])
+    co = coefficients(segment, cycle_cells)
+    _, _, rate_w = weights_of(step)
     lane, place = lanes_of()
     pairs = base_ref.shape[0]
     blocks = base_ref.shape[2] // SUB
     rows_all = blocks * SUB
+    tile = own_ref.shape[2]
+    rest = lax.rem(offsets_ref[0], tile)
+    split = jnp.where(rotor, tile + EDGE - rest, EDGE + rest)
+    shift = jnp.where(rotor, lax.rem(rows_all - rest, rows_all), rest)
+    shift2 = jnp.where(rotor, tile - rest, rest + rows_all - tile)
     row_id = lax.broadcasted_iota(jnp.int32, (rows_all, LANES), 0)
-    from_first = (row_id >= split) != (flip == 1)
+    from_first = (row_id >= split) != rotor
     upper_half = lax.broadcasted_iota(jnp.int32, (rows_all, LANES), 1) >= HALF
     weight_r = rate_w * co["inv_r"]
     at_low = jnp.where(place == 0, weight_r, 0.0)
@@ -341,17 +358,22 @@
         turned = jnp.where(upper_half, mixed, 0.0)
         signed = -rate_w if k == 3 else rate_w
         state_ref[pairs - 1, k] = state_ref[pairs - 1, k] + signed * turned
-    for a in range(pairs):
-        for k in range(FIELDS):
-            own_ref[a, k] = state_ref[a, k, pl.ds(EDGE, own_ref.shape[2]), :]
-    write_sends(state_ref, co, *sends)
+
+    @pl.when(step < 2)
+    def _():
+        write_sends(state_ref, co, *sends)
+
+    @pl.when(step == 2)
+    def _():
+        for a in range(pairs):
+            for k in range(FIELDS):
+                own_ref[a, k] = state_ref[a, k, pl.ds(EDGE, tile), :]
 
 
 def body(density, velocity, pressure, offsets):
     n_ax, n_az = lax.axis_size("ax"), lax.axis_size("az")
     planes, tile, cells = density.shape[1:]
     cycle_cells = tile * n_az
-    is_rotor = lax.axis_index("row") == 0
 
     vmem = pl.BlockSpec(memory_space=pltpu.VMEM)
     smem = pl.BlockSpec(memory_space=pltpu.SMEM)
@@ -380,6 +402,8 @@
                 pairs.append((device(1, x, (z + by) % n_az), device(0, x, z)))
                 pairs.append((device(0, x, z), device(1, x, (z + by) % n_az)))
         return pairs
+
+    near = [(device(r, x, z), device(r, x, (z + (1 if r else -1)) % n_az)) for r, x, z in every]
 
     def call(kernel, outs, n_smem, n_vmem, scratch=()):
         return pl.pallas_call(
@@ -400,80 +424,45 @@
     chunks = call(pack_kernel, own, 0, 3)(density[0], velocity[0], pressure[0])
     whole_tile = lax.all_to_all(chunks, "ax", 0, 0, tiled=True)
 
-    segment = lax.axis_index("ax")
-    flags, turns, weights = [], [], []
-    for step, (old_w, now_w) in enumerate(((0.0, 1.0), (0.75, 0.25), (1.0 / 3.0, 2.0 / 3.0))):
-        rest = offsets[step] % tile
-        turns.append(offsets[step] // tile)
-        flags.append(jnp.stack([
-            segment,
-            jnp.full_like(segment, n_ax),
-            jnp.where(is_rotor, tile + EDGE - rest, EDGE + rest),
-            jnp.where(is_rotor, 1, 0),
-            jnp.where(is_rotor, (tall - rest) % tall, rest),
-            jnp.where(is_rotor, tile - rest, rest + tall - tile),
-            jnp.where(is_rotor, 1, 0),
-        ]).astype(jnp.int32))
-        weights.append(jnp.array([old_w, now_w, now_w * TIME_STEP], dtype=jnp.float32))
-    up_rows, down_rows = call(edge_kernel, (outer_rows, outer_rows), 1, 1)(flags[0], whole_tile)
+    code = 4 * ((1 - lax.axis_index("row")) * n_ax + lax.axis_index("ax"))
+    code_1 = jnp.reshape(code, (1,))
+    packed = offsets[0] + cycle_cells * (offsets[1] + cycle_cells * offsets[2])
+    up_rows, down_rows = call(edge_kernel, (outer_rows, outer_rows), 1, 1)(code_1, whole_tile)
     up_rows = lax.ppermute(up_rows, AXES, turned(1))
-    down_rows = lax.ppermute(down_rows, AXES, turned(n_az - 1))
+    down_rows = lax.ppermute(down_rows, AXES, near)
     up_rows = lax.ppermute(up_rows, AXES, turned(0))
-    down_rows = lax.ppermute(down_rows, AXES, turned(0))
     start, *first = call(kernel_of(first_kernel), (block, *sends), 1, 3)(
-        flags[0], whole_tile, up_rows, down_rows
+        code_1, whole_tile, up_rows, down_rows
     )
     carry = (start, whole_tile, *first)
 
-    def local(flag, weight, now):
-        return call(kernel_of(local_kernel), block, 2, 2, (taller, taller, whole, whole))(
-            flag, weight, start, now
-        )
-
-    def around(out, inn):
-        return (
-            lax.ppermute(out, AXES, along_ax(1)),
-            lax.ppermute(inn, AXES, along_ax(-1)),
-        )
-
     def branch(by):
-        def run(flag, weight, now, up, *edges):
-            ghosts = (
+        def run(up, out, inn):
+            return (
                 lax.ppermute(up, AXES, turned(by)),
-                lax.ppermute(up, AXES, turned((by + 1) % n_az)),
+                lax.ppermute(out, AXES, along_ax(1)),
+                lax.ppermute(inn, AXES, along_ax(-1)),
             )
-            if IN_BRANCH:
-                ghosts += around(*edges)
-                ghosts += (local(flag, weight, now),)
-            return ghosts
         return run
 
     def substep(_, carry):
-        now, _, up, *edges = carry[:5]
-        turns, flags, weights = carry[5:]
-        flag, weight = flags[0], weights[0]
-        if not IN_BRANCH:
-            halos = around(*edges)
-        ghosts = lax.switch(
-            turns[0], [branch(by) for by in range(n_az)], flag, weight, now, up, *edges
-        )
-        if IN_BRANCH:
-            *ghosts, base = ghosts
-        else:
-            ghosts = (*ghosts, *halos)
-            base = local(flag, weight, now)
+        now, _, *edges, code, packed = carry
+        index = lax.div(lax.rem(packed, cycle_cells), tile)
+        code_1, left = jnp.reshape(code, (1,)), jnp.reshape(packed, (1,))
+        turn1, inside, outside = lax.switch(
+            index, [branch(by) for by in range(n_az)], *edges
+        )
+        turn2 = lax.ppermute(turn1, AXES, near)
+        base = call(kernel_of(local_kernel), block, 1, 2, (taller, taller, whole, whole))(
+            code_1, start, now
+        )
         state = call(kernel_of(join_kernel), (block, own, *sends), 2, 5)(
-            flag, weight, base, *ghosts
-        )
-        later = lambda kept: (*kept[1:], kept[0])
-        return (*state, later(turns), later(flags), later(weights))
-
-    carry = (*carry, tuple(turns), tuple(flags), tuple(weights))
-    if LOOP:
-        carry = lax.fori_loop(0, 3, substep, carry)
-    else:
-        for step in range(3):
-            carry = substep(step, carry)
+            code_1, left, base, turn1, turn2, inside, outside
+        )
+        return (*state, code + 1, lax.div(packed, cycle_cells))
+
+    carry = (*carry, code, packed)
+    carry = lax.fori_loop(0, 3, substep, carry)
     chunks = lax.all_to_all(carry[1], "ax", 0, 0, tiled=True)
     return call(unpack_kernel, struct(FIELDS, planes, tile, cells), 0, 1)(chunks)[None]
 

time: 136 us -> 138 us (1.015)
  the two profiles are of different devices: /device:TPU:16 before, /device:TPU:2 now
where the time goes in v1:
time: 138 us
  starting transfers between devices  76.1 us (55%)
  Pallas kernels  25 us (18%)
  waiting for transfers between devices  16.4 us (12%)
  blocking collectives  14.6 us (11%)
  local copies, waits for them, and re-layouts  3.81 us (3%)
  between operations  1.94 us (1%)
    ppermute x3, starting transfers between devices, substep(): turn2 = lax.ppermute(turn1, AXES, near)  19.9 us
    all_to_all x1, blocking collectives, body(): chunks = lax.all_to_all(carry[1], 'ax', 0, 0, tiled=True)  14.6 us
    ppermute x1, starting transfers between devices, body(): down_rows = lax.ppermute(down_rows, AXES, near)  12.3 us
    ppermute x3, starting transfers between devices, run(): lax.ppermute(out, AXES, along_ax(1))  10.7 us
    pallas_call x3, Pallas kernels, substep(): call(kernel_of(local_kernel), block, 1, 2, (taller, taller, whole, whole))  9.64 us
    ppermute x3, starting transfers between devices, run(): lax.ppermute(inn, AXES, along_ax(-1))  9.56 us
    all_to_all x1, starting transfers between devices, body(): whole_tile = lax.all_to_all(chunks, 'ax', 0, 0, tiled=True)  9.33 us
    ppermute x3, starting transfers between devices, run(): lax.ppermute(up, AXES, turned(by))  9.17 us
  transfers between devices with their start and end apart: 16, of which 5 were waited for; matrix products, arithmetic and copies ran while one was open for 0% of the time, Pallas kernels for 7%

profile of v1, /device:TPU:2, one launch (start us, length us, event | category | flops | bytes accessed | tf_op | source)
XLA Modules:
  0.0 137.9 jit_solution(15250664227205232707)
XLA Ops:
  0.0 2.2 %shard_map.46 = f32[8,5,32,128]{3,2,1,0:T(8,128)} custom-call(f32[2,32,512]{2,1,0:T(8,128)} %bitcast.13, f32[3,2,32,512]{3,2,1,0:T(8,128)} %bitcast.12, f32[2,32,512]{2,1,0:T(8,128)} %bitcast.14), custom_call_target="tpu_custom_call" | custom-call | flops 8000000 | bytes 3000000 | tf_op jit(solution)/shard_map/pallas_call | solution.py:424
  2.2 9.3 %all-to-all-start = ((f32[8,5,32,128]{3,2,1,0:T(8,128)}), f32[8,5,32,128]{3,2,1,0:T(8,128)S(1)}, u32[]{:S(2)}, u32[]{:S(2)}) async-start(f32[8,5,32,128]{3,2,1,0:T(8,128)} %shard_map.46), calls=%async_computation | async-start | bytes 1310720 | tf_op jit(solution)/shard_map/all_to_all | solution.py:425
  11.5 7.4 %all-to-all-done.in_ref = f32[8,5,32,128]{3,2,1,0:T(8,128)S(1)} async-done(((f32[8,5,32,128]{3,2,1,0:T(8,128)}), f32[8,5,32,128]{3,2,1,0:T(8,128)S(1)}, u32[]{:S(2)}, u32[]{:S(2)}) %all-to-all-start) | async-done | bytes 655392 | tf_op jit(solution)/shard_map/all_to_all | solution.py:425
  18.9 0.0 copy-start
  18.9 0.7 shard_map.47
  19.6 1.9 %collective-permute-start.97 = (f32[20,8,128]{2,1,0:T(8,128)}, f32[20,8,128]{2,1,0:T(8,128)S(1)}, u32[]{:S(2)}, u32[]{:S(2)}) collective-permute-start(f32[20,8,128]{2,1,0:T(8,128)} %get-tuple-element.415), channel_id=1, source_target_pairs={{257,0},{0,257},{258,1},{1,258},{259,2},{2,259},{260,3},{3,260},{2... | collective-permute-start | bytes 245768 | tf_op jit(solution)/shard_map/ppermute | solution.py:431
  21.5 0.0 copy-start.4
  21.5 12.3 %collective-permute-start.99 = (f32[20,8,128]{2,1,0:T(8,128)}, f32[20,8,128]{2,1,0:T(8,128)S(1)}, u32[]{:S(2)}, u32[]{:S(2)}) collective-permute-start(f32[20,8,128]{2,1,0:T(8,128)} %get-tuple-element.416), channel_id=1, source_target_pairs={{0,31},{1,0},{2,1},{3,2},{4,3},{5,4},{6,5},{7,6},{8,7},{9,8},{10,9... | collective-permute-start | bytes 245768 | tf_op jit(solution)/shard_map/ppermute | solution.py:432
  33.8 0.0 collective-permute-done.97
  33.9 3.3 %collective-permute-start.98 = (f32[20,8,128]{2,1,0:T(8,128)S(1)}, f32[20,8,128]{2,1,0:T(8,128)S(1)}, u32[]{:S(2)}, u32[]{:S(2)}) collective-permute-start(f32[20,8,128]{2,1,0:T(8,128)S(1)} %collective-permute-done.97), channel_id=1, source_target_pairs={{256,0},{0,256},{257,1},{1,257},{258,2},{2,258},{259,3},{3,259},{2... | collective-permute-start | bytes 245768 | tf_op jit(solution)/shard_map/ppermute | solution.py:433
  37.1 0.0 copy-done.4
  37.1 0.7 fusion
  39.6 0.0 collective-permute-done.99.two_ref
  39.6 0.0 copy-start.2
  39.6 0.0 collective-permute-done.98.one_ref
  39.6 0.6 copy-done.2
  40.3 0.0 copy-start.3
  40.3 0.6 copy-done.3
  40.9 1.5 %shard_map.48 = (f32[8,5,40,128]{3,2,1,0:T(8,128)S(1)}, f32[5,24,128]{2,1,0:T(8,128)S(1)}, f32[40,128]{1,0:T(8,128)S(1)}, f32[40,128]{1,0:T(8,128)S(1)}) custom-call(s32[1]{0:T(128)} %bitcast.2.code_ref, f32[8,5,32,128]{3,2,1,0:T(8,128)S(1)} %all-to-all-done.in_ref, f32[20,8,128]{2,1,0:T(8,128)} %copy-done.3, f32[20,8,128]{2,1,0:T(8,128)} %copy-done.2), custom_call_target="tpu_custom_call" | custom-call | flops 8000000 | bytes 3000000 | tf_op jit(solution)/shard_map/pallas_call | solution.py:434
  42.4 0.0 copy-done
  42.4 0.1 copy.102
  42.4 78.8 %while.22 = (s32[]{:T(128)}, f32[8,5,40,128]{3,2,1,0:T(8,128)S(1)}, f32[8,5,32,128]{3,2,1,0:T(8,128)}, f32[5,24,128]{2,1,0:T(8,128)S(1)}, f32[40,128]{1,0:T(8,12...) while((s32[]{:T(128)}, f32[8,5,40,128]{3,2,1,0:T(8,128)S(1)}, ...), condition=%wide.region_33.0_spmd, body=%wide.region_0.0_spmd.sunk | while | flops 16000019 | bytes 6901700 | solution.py:465
  42.5 13.5 %conditional.2 = (f32[5,24,128]{2,1,0:T(8,128)}, f32[40,128]{1,0:T(8,128)}, f32[40,128]{1,0:T(8,128)}) conditional(s32[]{:T(128)} %clamp.6, (f32[5,24,128]{2,1,0:T(8,128)S(1)}, f32[40,128]{1,0:T(8,128)S(1)}, f32[40,128]{1,0:T(8,128)S(1)}) %tuple.155, (f32[5,24,128]{2,1,0:T(8,128)S(1)}, f32[40,128]{1,0:T(8,128)S(1)}, ...), branch_computations={%region_1.0_spmd, %region_2.0_spmd, %region_3.0_spmd, %region_4.0_... | conditional | bytes 409744 | solution.py:452
  42.5 4.1 %collective-permute-start.57 = (f32[5,24,128]{2,1,0:T(8,128)S(1)}, f32[5,24,128]{2,1,0:T(8,128)}, u32[]{:S(2)}, u32[]{:S(2)}) collective-permute-start(f32[5,24,128]{2,1,0:T(8,128)S(1)} %get-tuple-element.352), channel_id=1, source_target_pairs={{275,0},{0,275},{276,1},{1,276},{277,2},{2,277},{278,3},{3,278},{2... | collective-permute-start | bytes 184328 | tf_op jit(solution)/shard_map/while/body/eval_jaxpr/cond/branch_19_fun/ppermute | solution.py:442
  46.6 3.4 %collective-permute-start.58 = (f32[40,128]{1,0:T(8,128)S(1)}, f32[40,128]{1,0:T(8,128)}, u32[]{:S(2)}, u32[]{:S(2)}) collective-permute-start(f32[40,128]{1,0:T(8,128)S(1)} %get-tuple-element.353), channel_id=1, source_target_pairs={{0,32},{1,33},{2,34},{3,35},{4,36},{5,37},{6,38},{7,39},{8,40},{9,... | collective-permute-start | bytes 61448 | tf_op jit(solution)/shard_map/while/body/eval_jaxpr/cond/branch_19_fun/ppermute | solution.py:443
  50.0 3.4 %collective-permute-start.59 = (f32[40,128]{1,0:T(8,128)S(1)}, f32[40,128]{1,0:T(8,128)}, u32[]{:S(2)}, u32[]{:S(2)}) collective-permute-start(f32[40,128]{1,0:T(8,128)S(1)} %get-tuple-element.354), channel_id=1, source_target_pairs={{32,0},{33,1},{34,2},{35,3},{36,4},{37,5},{38,6},{39,7},{40,8},{41... | collective-permute-start | bytes 61448 | tf_op jit(solution)/shard_map/while/body/eval_jaxpr/cond/branch_19_fun/ppermute | solution.py:444
  53.3 1.2 collective-permute-done.58
  54.6 1.4 %collective-permute-done.59 = f32[40,128]{1,0:T(8,128)} collective-permute-done((f32[40,128]{1,0:T(8,128)S(1)}, f32[40,128]{1,0:T(8,128)}, u32[]{:S(2)}, u32[]{:S(2)}) %collective-permute-start.59) | collective-permute-done | bytes 20512 | tf_op jit(solution)/shard_map/while/body/eval_jaxpr/cond/branch_19_fun/ppermute | solution.py:444
  56.0 0.0 collective-permute-done.57
  56.0 4.8 %collective-permute-start.96 = (f32[5,24,128]{2,1,0:T(8,128)}, f32[5,24,128]{2,1,0:T(8,128)S(1)}, u32[]{:S(2)}, u32[]{:S(2)}) collective-permute-start(f32[5,24,128]{2,1,0:T(8,128)} %get-tuple-element.504.turn_ref), channel_id=1, source_target_pairs={{0,31},{1,0},{2,1},{3,2},{4,3},{5,4},{6,5},{7,6},{8,7},{9,8},{10,9... | collective-permute-start | bytes 184328 | tf_op jit(solution)/shard_map/while/body/eval_jaxpr/ppermute | solution.py:455
  60.8 3.2 %eval_jaxpr.4.base_ref = f32[8,5,40,128]{3,2,1,0:T(8,128)} custom-call(s32[1]{0:T(128)} %bitcast.10.code_ref, f32[8,5,40,128]{3,2,1,0:T(8,128)S(1)} %get-tuple-element.646.old_ref, f32[8,5,40,128]{3,2,1,0:T(8,128)S(1)} %get-tuple-element.624.now_ref), custom_call_target="tpu_custom_call" | custom-call | flops 8000000 | bytes 3000000 | tf_op jit(solution)/shard_map/while/body/eval_jaxpr/pallas_call | solution.py:456
  64.0 0.0 collective-permute-done.96.turn2_ref
  64.0 0.0 copy-start.1
  64.1 0.6 copy-done.1
  64.7 3.1 %eval_jaxpr.5 = (f32[8,5,40,128]{3,2,1,0:T(8,128)S(1)}, f32[8,5,32,128]{3,2,1,0:T(8,128)}, f32[5,24,128]{2,1,0:T(8,128)S(1)}, f32[40,128]{1,0:T(8,128)S(1)}, f32[40,128]{1,0:T(8,128)S(1)}) custom-call(s32[1]{0:T(128)} %bitcast.10.code_ref, s32[1]{0:T(128)} %bitcast.11.offsets_ref, f32[8,5,40,128]{3,2,1,0:T(8,128)} %eval_jaxpr.4.base_ref, ...), custom_call_target="tpu_custom_call" | custom-call | flops 8000000 | bytes 3000000 | tf_op jit(solution)/shard_map/while/body/eval_jaxpr/pallas_call | solution.py:459
  67.8 12.9 %conditional.2 = (f32[5,24,128]{2,1,0:T(8,128)}, f32[40,128]{1,0:T(8,128)}, f32[40,128]{1,0:T(8,128)}) conditional(s32[]{:T(128)} %clamp.6, (f32[5,24,128]{2,1,0:T(8,128)S(1)}, f32[40,128]{1,0:T(8,128)S(1)}, f32[40,128]{1,0:T(8,128)S(1)}) %tuple.155, (f32[5,24,128]{2,1,0:T(8,128)S(1)}, f32[40,128]{1,0:T(8,128)S(1)}, ...), branch_computations={%region_1.0_spmd, %region_2.0_spmd, %region_3.0_spmd, %region_4.0_... | conditional | bytes 409744 | solution.py:452
  67.8 1.9 %collective-permute-start.33 = (f32[5,24,128]{2,1,0:T(8,128)S(1)}, f32[5,24,128]{2,1,0:T(8,128)}, u32[]{:S(2)}, u32[]{:S(2)}) collective-permute-start(f32[5,24,128]{2,1,0:T(8,128)S(1)} %get-tuple-element.328), channel_id=1, source_target_pairs={{267,0},{0,267},{268,1},{1,268},{269,2},{2,269},{270,3},{3,270},{2... | collective-permute-start | bytes 184328 | tf_op jit(solution)/shard_map/while/body/eval_jaxpr/cond/branch_11_fun/ppermute | solution.py:442
  69.7 4.2 %collective-permute-start.34 = (f32[40,128]{1,0:T(8,128)S(1)}, f32[40,128]{1,0:T(8,128)}, u32[]{:S(2)}, u32[]{:S(2)}) collective-permute-start(f32[40,128]{1,0:T(8,128)S(1)} %get-tuple-element.329), channel_id=1, source_target_pairs={{0,32},{1,33},{2,34},{3,35},{4,36},{5,37},{6,38},{7,39},{8,40},{9,... | collective-permute-start | bytes 61448 | tf_op jit(solution)/shard_map/while/body/eval_jaxpr/cond/branch_11_fun/ppermute | solution.py:443
  73.9 2.6 %collective-permute-start.35 = (f32[40,128]{1,0:T(8,128)S(1)}, f32[40,128]{1,0:T(8,128)}, u32[]{:S(2)}, u32[]{:S(2)}) collective-permute-start(f32[40,128]{1,0:T(8,128)S(1)} %get-tuple-element.330), channel_id=1, source_target_pairs={{32,0},{33,1},{34,2},{35,3},{36,4},{37,5},{38,6},{39,7},{40,8},{41... | collective-permute-start | bytes 61448 | tf_op jit(solution)/shard_map/while/body/eval_jaxpr/cond/branch_11_fun/ppermute | solution.py:444
  76.4 0.0 collective-permute-done.34
  76.4 4.2 %collective-permute-done.35 = f32[40,128]{1,0:T(8,128)} collective-permute-done((f32[40,128]{1,0:T(8,128)S(1)}, f32[40,128]{1,0:T(8,128)}, u32[]{:S(2)}, u32[]{:S(2)}) %collective-permute-start.35) | collective-permute-done | bytes 20512 | tf_op jit(solution)/shard_map/while/body/eval_jaxpr/cond/branch_11_fun/ppermute | solution.py:444
  80.6 0.0 collective-permute-done.33
  80.6 7.9 %collective-permute-start.96 = (f32[5,24,128]{2,1,0:T(8,128)}, f32[5,24,128]{2,1,0:T(8,128)S(1)}, u32[]{:S(2)}, u32[]{:S(2)}) collective-permute-start(f32[5,24,128]{2,1,0:T(8,128)} %get-tuple-element.504.turn_ref), channel_id=1, source_target_pairs={{0,31},{1,0},{2,1},{3,2},{4,3},{5,4},{6,5},{7,6},{8,7},{9,8},{10,9... | collective-permute-start | bytes 184328 | tf_op jit(solution)/shard_map/while/body/eval_jaxpr/ppermute | solution.py:455
  88.6 3.2 %eval_jaxpr.4.base_ref = f32[8,5,40,128]{3,2,1,0:T(8,128)} custom-call(s32[1]{0:T(128)} %bitcast.10.code_ref, f32[8,5,40,128]{3,2,1,0:T(8,128)S(1)} %get-tuple-element.646.old_ref, f32[8,5,40,128]{3,2,1,0:T(8,128)S(1)} %get-tuple-element.624.now_ref), custom_call_target="tpu_custom_call" | custom-call | flops 8000000 | bytes 3000000 | tf_op jit(solution)/shard_map/while/body/eval_jaxpr/pallas_call | solution.py:456
  91.8 0.0 collective-permute-done.96.turn2_ref
  91.8 0.0 copy-start.1
  91.8 0.6 copy-done.1
  92.4 3.1 %eval_jaxpr.5 = (f32[8,5,40,128]{3,2,1,0:T(8,128)S(1)}, f32[8,5,32,128]{3,2,1,0:T(8,128)}, f32[5,24,128]{2,1,0:T(8,128)S(1)}, f32[40,128]{1,0:T(8,128)S(1)}, f32[40,128]{1,0:T(8,128)S(1)}) custom-call(s32[1]{0:T(128)} %bitcast.10.code_ref, s32[1]{0:T(128)} %bitcast.11.offsets_ref, f32[8,5,40,128]{3,2,1,0:T(8,128)} %eval_jaxpr.4.base_ref, ...), custom_call_target="tpu_custom_call" | custom-call | flops 8000000 | bytes 3000000 | tf_op jit(solution)/shard_map/while/body/eval_jaxpr/pallas_call | solution.py:459
  95.5 12.1 %conditional.2 = (f32[5,24,128]{2,1,0:T(8,128)}, f32[40,128]{1,0:T(8,128)}, f32[40,128]{1,0:T(8,128)}) conditional(s32[]{:T(128)} %clamp.6, (f32[5,24,128]{2,1,0:T(8,128)S(1)}, f32[40,128]{1,0:T(8,128)S(1)}, f32[40,128]{1,0:T(8,128)S(1)}) %tuple.155, (f32[5,24,128]{2,1,0:T(8,128)S(1)}, f32[40,128]{1,0:T(8,128)S(1)}, ...), branch_computations={%region_1.0_spmd, %region_2.0_spmd, %region_3.0_spmd, %region_4.0_... | conditional | bytes 409744 | solution.py:452
  95.5 3.2 %collective-permute-start = (f32[5,24,128]{2,1,0:T(8,128)S(1)}, f32[5,24,128]{2,1,0:T(8,128)}, u32[]{:S(2)}, u32[]{:S(2)}) collective-permute-start(f32[5,24,128]{2,1,0:T(8,128)S(1)} %get-tuple-element.295), channel_id=1, source_target_pairs={{256,0},{0,256},{257,1},{1,257},{258,2},{2,258},{259,3},{3,259},{2... | collective-permute-start | bytes 184328 | tf_op jit(solution)/shard_map/while/body/eval_jaxpr/cond/branch_0_fun/ppermute | solution.py:442
  98.7 3.1 %collective-permute-start.1 = (f32[40,128]{1,0:T(8,128)S(1)}, f32[40,128]{1,0:T(8,128)}, u32[]{:S(2)}, u32[]{:S(2)}) collective-permute-start(f32[40,128]{1,0:T(8,128)S(1)} %get-tuple-element.296), channel_id=1, source_target_pairs={{0,32},{1,33},{2,34},{3,35},{4,36},{5,37},{6,38},{7,39},{8,40},{9,... | collective-permute-start | bytes 61448 | tf_op jit(solution)/shard_map/while/body/eval_jaxpr/cond/branch_0_fun/ppermute | solution.py:443
  101.8 3.6 %collective-permute-start.2 = (f32[40,128]{1,0:T(8,128)S(1)}, f32[40,128]{1,0:T(8,128)}, u32[]{:S(2)}, u32[]{:S(2)}) collective-permute-start(f32[40,128]{1,0:T(8,128)S(1)} %get-tuple-element.297), channel_id=1, source_target_pairs={{32,0},{33,1},{34,2},{35,3},{36,4},{37,5},{38,6},{39,7},{40,8},{41... | collective-permute-start | bytes 61448 | tf_op jit(solution)/shard_map/while/body/eval_jaxpr/cond/branch_0_fun/ppermute | solution.py:444
  105.4 0.0 collective-permute-done.1
  105.5 2.1 %collective-permute-done.2 = f32[40,128]{1,0:T(8,128)} collective-permute-done((f32[40,128]{1,0:T(8,128)S(1)}, f32[40,128]{1,0:T(8,128)}, u32[]{:S(2)}, u32[]{:S(2)}) %collective-permute-start.2) | collective-permute-done | bytes 20512 | tf_op jit(solution)/shard_map/while/body/eval_jaxpr/cond/branch_0_fun/ppermute | solution.py:444
  107.6 0.0 collective-permute-done
  107.6 7.1 %collective-permute-start.96 = (f32[5,24,128]{2,1,0:T(8,128)}, f32[5,24,128]{2,1,0:T(8,128)S(1)}, u32[]{:S(2)}, u32[]{:S(2)}) collective-permute-start(f32[5,24,128]{2,1,0:T(8,128)} %get-tuple-element.504.turn_ref), channel_id=1, source_target_pairs={{0,31},{1,0},{2,1},{3,2},{4,3},{5,4},{6,5},{7,6},{8,7},{9,8},{10,9... | collective-permute-start | bytes 184328 | tf_op jit(solution)/shard_map/while/body/eval_jaxpr/ppermute | solution.py:455
  114.8 3.2 %eval_jaxpr.4.base_ref = f32[8,5,40,128]{3,2,1,0:T(8,128)} custom-call(s32[1]{0:T(128)} %bitcast.10.code_ref, f32[8,5,40,128]{3,2,1,0:T(8,128)S(1)} %get-tuple-element.646.old_ref, f32[8,5,40,128]{3,2,1,0:T(8,128)S(1)} %get-tuple-element.624.now_ref), custom_call_target="tpu_custom_call" | custom-call | flops 8000000 | bytes 3000000 | tf_op jit(solution)/shard_map/while/body/eval_jaxpr/pallas_call | solution.py:456
  118.0 0.0 collective-permute-done.96.turn2_ref
  118.0 0.0 copy-start.1
  118.0 0.6 copy-done.1
  118.6 2.6 %eval_jaxpr.5 = (f32[8,5,40,128]{3,2,1,0:T(8,128)S(1)}, f32[8,5,32,128]{3,2,1,0:T(8,128)}, f32[5,24,128]{2,1,0:T(8,128)S(1)}, f32[40,128]{1,0:T(8,128)S(1)}, f32[40,128]{1,0:T(8,128)S(1)}) custom-call(s32[1]{0:T(128)} %bitcast.10.code_ref, s32[1]{0:T(128)} %bitcast.11.offsets_ref, f32[8,5,40,128]{3,2,1,0:T(8,128)} %eval_jaxpr.4.base_ref, ...), custom_call_target="tpu_custom_call" | custom-call | flops 8000000 | bytes 3000000 | tf_op jit(solution)/shard_map/while/body/eval_jaxpr/pallas_call | solution.py:459
  121.2 14.6 %all_to_all.10.in_ref = f32[8,5,32,128]{3,2,1,0:T(8,128)} all-to-all(f32[8,5,32,128]{3,2,1,0:T(8,128)} %get-tuple-element.421), channel_id=1, replica_groups=mesh['row'=2,'ax'=8,'az'=32] {'ax'}, dimensions={0} | all-to-all | bytes 1310720 | tf_op jit(solution)/shard_map/all_to_all | solution.py:466
  135.8 2.2 %shard_map.49 = f32[5,2,32,512]{3,2,1,0:T(8,128)} custom-call(f32[8,5,32,128]{3,2,1,0:T(8,128)} %all_to_all.10.in_ref), custom_call_target="tpu_custom_call" | custom-call | flops 8000000 | bytes 3000000 | tf_op jit(solution)/shard_map/pallas_call | solution.py:467
Async XLA Ops:
  2.2 16.7 %all-to-all-start = ((f32[8,5,32,128]{3,2,1,0:T(8,128)}), f32[8,5,32,128]{3,2,1,0:T(8,128)S(1)}, u32[]{:S(2)}, u32[]{:S(2)}) async-start(f32[8,5,32,128]{3,2,1,0:T(8,128)} %shard_map.46), calls=%async_computation | async-start | bytes 1310720 | tf_op jit(solution)/shard_map/all_to_all | solution.py:425
  18.9 23.5 %copy-start = (f32[8,5,32,128]{3,2,1,0:T(8,128)}, f32[8,5,32,128]{3,2,1,0:T(8,128)S(1)}, u32[]{:S(2)}) copy-start(f32[8,5,32,128]{3,2,1,0:T(8,128)S(1)} %all-to-all-done.in_ref) | copy-start | bytes 1966084
  19.6 14.2 %collective-permute-start.97 = (f32[20,8,128]{2,1,0:T(8,128)}, f32[20,8,128]{2,1,0:T(8,128)S(1)}, u32[]{:S(2)}, u32[]{:S(2)}) collective-permute-start(f32[20,8,128]{2,1,0:T(8,128)} %get-tuple-element.415), channel_id=1, source_target_pairs={{257,0},{0,257},{258,1},{1,258},{259,2},{2,259},{260,3},{3,260},{2... | collective-permute-start | bytes 245768 | tf_op jit(solution)/shard_map/ppermute | solution.py:431
  21.5 15.6 %copy-start.4 = (s32[3]{0:T(128)S(1)}, s32[3]{0:T(128)}, u32[]{:S(2)}) copy-start(s32[3]{0:T(128)} %param.41) | copy-start | bytes 40
  21.5 18.1 %collective-permute-start.99 = (f32[20,8,128]{2,1,0:T(8,128)}, f32[20,8,128]{2,1,0:T(8,128)S(1)}, u32[]{:S(2)}, u32[]{:S(2)}) collective-permute-start(f32[20,8,128]{2,1,0:T(8,128)} %get-tuple-element.416), channel_id=1, source_target_pairs={{0,31},{1,0},{2,1},{3,2},{4,3},{5,4},{6,5},{7,6},{8,7},{9,8},{10,9... | collective-permute-start | bytes 245768 | tf_op jit(solution)/shard_map/ppermute | solution.py:432
  33.9 5.8 %collective-permute-start.98 = (f32[20,8,128]{2,1,0:T(8,128)S(1)}, f32[20,8,128]{2,1,0:T(8,128)S(1)}, u32[]{:S(2)}, u32[]{:S(2)}) collective-permute-start(f32[20,8,128]{2,1,0:T(8,128)S(1)} %collective-permute-done.97), channel_id=1, source_target_pairs={{256,0},{0,256},{257,1},{1,257},{258,2},{2,258},{259,3},{3,259},{2... | collective-permute-start | bytes 245768 | tf_op jit(solution)/shard_map/ppermute | solution.py:433
  39.6 0.6 copy-start.2
  40.3 0.6 copy-start.3
  42.5 13.5 %collective-permute-start.57 = (f32[5,24,128]{2,1,0:T(8,128)S(1)}, f32[5,24,128]{2,1,0:T(8,128)}, u32[]{:S(2)}, u32[]{:S(2)}) collective-permute-start(f32[5,24,128]{2,1,0:T(8,128)S(1)} %get-tuple-element.352), channel_id=1, source_target_pairs={{275,0},{0,275},{276,1},{1,276},{277,2},{2,277},{278,3},{3,278},{2... | collective-permute-start | bytes 184328 | tf_op jit(solution)/shard_map/while/body/eval_jaxpr/cond/branch_19_fun/ppermute | solution.py:442
  46.6 8.0 %collective-permute-start.58 = (f32[40,128]{1,0:T(8,128)S(1)}, f32[40,128]{1,0:T(8,128)}, u32[]{:S(2)}, u32[]{:S(2)}) collective-permute-start(f32[40,128]{1,0:T(8,128)S(1)} %get-tuple-element.353), channel_id=1, source_target_pairs={{0,32},{1,33},{2,34},{3,35},{4,36},{5,37},{6,38},{7,39},{8,40},{9,... | collective-permute-start | bytes 61448 | tf_op jit(solution)/shard_map/while/body/eval_jaxpr/cond/branch_19_fun/ppermute | solution.py:443
  50.0 6.0 %collective-permute-start.59 = (f32[40,128]{1,0:T(8,128)S(1)}, f32[40,128]{1,0:T(8,128)}, u32[]{:S(2)}, u32[]{:S(2)}) collective-permute-start(f32[40,128]{1,0:T(8,128)S(1)} %get-tuple-element.354), channel_id=1, source_target_pairs={{32,0},{33,1},{34,2},{35,3},{36,4},{37,5},{38,6},{39,7},{40,8},{41... | collective-permute-start | bytes 61448 | tf_op jit(solution)/shard_map/while/body/eval_jaxpr/cond/branch_19_fun/ppermute | solution.py:444
  56.0 8.1 %collective-permute-start.96 = (f32[5,24,128]{2,1,0:T(8,128)}, f32[5,24,128]{2,1,0:T(8,128)S(1)}, u32[]{:S(2)}, u32[]{:S(2)}) collective-permute-start(f32[5,24,128]{2,1,0:T(8,128)} %get-tuple-element.504.turn_ref), channel_id=1, source_target_pairs={{0,31},{1,0},{2,1},{3,2},{4,3},{5,4},{6,5},{7,6},{8,7},{9,8},{10,9... | collective-permute-start | bytes 184328 | tf_op jit(solution)/shard_map/while/body/eval_jaxpr/ppermute | solution.py:455
  64.0 0.6 copy-start.1
  67.8 12.9 %collective-permute-start.33 = (f32[5,24,128]{2,1,0:T(8,128)S(1)}, f32[5,24,128]{2,1,0:T(8,128)}, u32[]{:S(2)}, u32[]{:S(2)}) collective-permute-start(f32[5,24,128]{2,1,0:T(8,128)S(1)} %get-tuple-element.328), channel_id=1, source_target_pairs={{267,0},{0,267},{268,1},{1,268},{269,2},{2,269},{270,3},{3,270},{2... | collective-permute-start | bytes 184328 | tf_op jit(solution)/shard_map/while/body/eval_jaxpr/cond/branch_11_fun/ppermute | solution.py:442
  69.7 6.8 %collective-permute-start.34 = (f32[40,128]{1,0:T(8,128)S(1)}, f32[40,128]{1,0:T(8,128)}, u32[]{:S(2)}, u32[]{:S(2)}) collective-permute-start(f32[40,128]{1,0:T(8,128)S(1)} %get-tuple-element.329), channel_id=1, source_target_pairs={{0,32},{1,33},{2,34},{3,35},{4,36},{5,37},{6,38},{7,39},{8,40},{9,... | collective-permute-start | bytes 61448 | tf_op jit(solution)/shard_map/while/body/eval_jaxpr/cond/branch_11_fun/ppermute | solution.py:443
  73.9 6.8 %collective-permute-start.35 = (f32[40,128]{1,0:T(8,128)S(1)}, f32[40,128]{1,0:T(8,128)}, u32[]{:S(2)}, u32[]{:S(2)}) collective-permute-start(f32[40,128]{1,0:T(8,128)S(1)} %get-tuple-element.330), channel_id=1, source_target_pairs={{32,0},{33,1},{34,2},{35,3},{36,4},{37,5},{38,6},{39,7},{40,8},{41... | collective-permute-start | bytes 61448 | tf_op jit(solution)/shard_map/while/body/eval_jaxpr/cond/branch_11_fun/ppermute | solution.py:444
  80.6 11.2 %collective-permute-start.96 = (f32[5,24,128]{2,1,0:T(8,128)}, f32[5,24,128]{2,1,0:T(8,128)S(1)}, u32[]{:S(2)}, u32[]{:S(2)}) collective-permute-start(f32[5,24,128]{2,1,0:T(8,128)} %get-tuple-element.504.turn_ref), channel_id=1, source_target_pairs={{0,31},{1,0},{2,1},{3,2},{4,3},{5,4},{6,5},{7,6},{8,7},{9,8},{10,9... | collective-permute-start | bytes 184328 | tf_op jit(solution)/shard_map/while/body/eval_jaxpr/ppermute | solution.py:455
  91.8 0.6 copy-start.1
  95.5 12.1 %collective-permute-start = (f32[5,24,128]{2,1,0:T(8,128)S(1)}, f32[5,24,128]{2,1,0:T(8,128)}, u32[]{:S(2)}, u32[]{:S(2)}) collective-permute-start(f32[5,24,128]{2,1,0:T(8,128)S(1)} %get-tuple-element.295), channel_id=1, source_target_pairs={{256,0},{0,256},{257,1},{1,257},{258,2},{2,258},{259,3},{3,259},{2... | collective-permute-start | bytes 184328 | tf_op jit(solution)/shard_map/while/body/eval_jaxpr/cond/branch_0_fun/ppermute | solution.py:442
  98.7 6.8 %collective-permute-start.1 = (f32[40,128]{1,0:T(8,128)S(1)}, f32[40,128]{1,0:T(8,128)}, u32[]{:S(2)}, u32[]{:S(2)}) collective-permute-start(f32[40,128]{1,0:T(8,128)S(1)} %get-tuple-element.296), channel_id=1, source_target_pairs={{0,32},{1,33},{2,34},{3,35},{4,36},{5,37},{6,38},{7,39},{8,40},{9,... | collective-permute-start | bytes 61448 | tf_op jit(solution)/shard_map/while/body/eval_jaxpr/cond/branch_0_fun/ppermute | solution.py:443
  101.8 5.8 %collective-permute-start.2 = (f32[40,128]{1,0:T(8,128)S(1)}, f32[40,128]{1,0:T(8,128)}, u32[]{:S(2)}, u32[]{:S(2)}) collective-permute-start(f32[40,128]{1,0:T(8,128)S(1)} %get-tuple-element.297), channel_id=1, source_target_pairs={{32,0},{33,1},{34,2},{35,3},{36,4},{37,5},{38,6},{39,7},{40,8},{41... | collective-permute-start | bytes 61448 | tf_op jit(solution)/shard_map/while/body/eval_jaxpr/cond/branch_0_fun/ppermute | solution.py:444
  107.6 10.4 %collective-permute-start.96 = (f32[5,24,128]{2,1,0:T(8,128)}, f32[5,24,128]{2,1,0:T(8,128)S(1)}, u32[]{:S(2)}, u32[]{:S(2)}) collective-permute-start(f32[5,24,128]{2,1,0:T(8,128)} %get-tuple-element.504.turn_ref), channel_id=1, source_target_pairs={{0,31},{1,0},{2,1},{3,2},{4,3},{5,4},{6,5},{7,6},{8,7},{9,8},{10,9... | collective-permute-start | bytes 184328 | tf_op jit(solution)/shard_map/while/body/eval_jaxpr/ppermute | solution.py:455
  118.0 0.6 copy-start.1

commit v2 on v1

--- a/solution.py
+++ b/solution.py
@@ -315,7 +315,7 @@
 
 
 def join_kernel(cycle_cells, code_ref, offsets_ref, base_ref, turn_ref, turn2_ref, inside_ref,
-                outside_ref, state_ref, own_ref, *sends):
+                outside_ref, state_ref, *sends):
     step, segment, rotor = decode(code_ref, base_ref.shape[0])
     co = coefficients(segment, cycle_cells)
     _, _, rate_w = weights_of(step)
@@ -323,7 +323,7 @@
     pairs = base_ref.shape[0]
     blocks = base_ref.shape[2] // SUB
     rows_all = blocks * SUB
-    tile = own_ref.shape[2]
+    tile = rows_all - 2 * EDGE
     rest = lax.rem(offsets_ref[0], tile)
     split = jnp.where(rotor, tile + EDGE - rest, EDGE + rest)
     shift = jnp.where(rotor, lax.rem(rows_all - rest, rows_all), rest)
@@ -358,16 +358,7 @@
         turned = jnp.where(upper_half, mixed, 0.0)
         signed = -rate_w if k == 3 else rate_w
         state_ref[pairs - 1, k] = state_ref[pairs - 1, k] + signed * turned
-
-    @pl.when(step < 2)
-    def _():
-        write_sends(state_ref, co, *sends)
-
-    @pl.when(step == 2)
-    def _():
-        for a in range(pairs):
-            for k in range(FIELDS):
-                own_ref[a, k] = state_ref[a, k, pl.ds(EDGE, tile), :]
+    write_sends(state_ref, co, *sends)
 
 
 def body(density, velocity, pressure, offsets):
@@ -434,36 +425,33 @@
     start, *first = call(kernel_of(first_kernel), (block, *sends), 1, 3)(
         code_1, whole_tile, up_rows, down_rows
     )
-    carry = (start, whole_tile, *first)
+    carry = (start, *first)
 
     def branch(by):
-        def run(up, out, inn):
-            return (
-                lax.ppermute(up, AXES, turned(by)),
-                lax.ppermute(out, AXES, along_ax(1)),
-                lax.ppermute(inn, AXES, along_ax(-1)),
+        def run(code, now, up, out, inn):
+            turn1 = lax.ppermute(up, AXES, turned(by))
+            turn2 = lax.ppermute(up, AXES, turned((by + 1) % n_az))
+            inside = lax.ppermute(out, AXES, along_ax(1))
+            outside = lax.ppermute(inn, AXES, along_ax(-1))
+            base = call(kernel_of(local_kernel), block, 1, 2, (taller, taller, whole, whole))(
+                code, start, now
             )
+            return base, turn1, turn2, inside, outside
         return run
 
     def substep(_, carry):
-        now, _, *edges, code, packed = carry
+        *cells_and_edges, code, packed = carry
         index = lax.div(lax.rem(packed, cycle_cells), tile)
         code_1, left = jnp.reshape(code, (1,)), jnp.reshape(packed, (1,))
-        turn1, inside, outside = lax.switch(
-            index, [branch(by) for by in range(n_az)], *edges
+        terms = lax.switch(
+            index, [branch(by) for by in range(n_az)], code_1, *cells_and_edges
         )
-        turn2 = lax.ppermute(turn1, AXES, near)
-        base = call(kernel_of(local_kernel), block, 1, 2, (taller, taller, whole, whole))(
-            code_1, start, now
-        )
-        state = call(kernel_of(join_kernel), (block, own, *sends), 2, 5)(
-            code_1, left, base, turn1, turn2, inside, outside
-        )
+        state = call(kernel_of(join_kernel), (block, *sends), 2, 5)(code_1, left, *terms)
         return (*state, code + 1, lax.div(packed, cycle_cells))
 
     carry = (*carry, code, packed)
     carry = lax.fori_loop(0, 3, substep, carry)
-    chunks = lax.all_to_all(carry[1], "ax", 0, 0, tiled=True)
+    chunks = lax.all_to_all(carry[0][:, :, EDGE : EDGE + tile], "ax", 0, 0, tiled=True)
     return call(unpack_kernel, struct(FIELDS, planes, tile, cells), 0, 1)(chunks)[None]
 
 

time: 138 us -> 126 us (0.913)
  the two profiles are of different devices: /device:TPU:2 before, /device:TPU:16 now
where the time goes in v2:
time: 126 us; the launch traced here: 124 us
  starting transfers between devices  65.3 us (52%)
  Pallas kernels  20.3 us (16%)
  waiting for transfers between devices  19.6 us (16%)
  blocking collectives  13.6 us (11%)
  local copies, waits for them, and re-layouts  2.79 us (2%)
  between operations  1.86 us (1%)
    ppermute x3, starting transfers between devices, run(): turn1 = lax.ppermute(up, AXES, turned(by))  20.6 us
    ppermute x3, starting transfers between devices, run(): turn2 = lax.ppermute(up, AXES, turned((by + 1) % n_az))  17.9 us
    all_to_all x1, blocking collectives, body(): lax.all_to_all(carry[0][:, :, EDGE:EDGE + tile], 'ax', 0, 0, tiled=True)  13.6 us
    all_to_all x1, waiting for transfers between devices, body(): whole_tile = lax.all_to_all(chunks, 'ax', 0, 0, tiled=True)  11.5 us
    ppermute x3, starting transfers between devices, run(): inside = lax.ppermute(out, AXES, along_ax(1))  10.6 us
    pallas_call x3, Pallas kernels, run(): call(kernel_of(local_kernel), block, 1, 2, (taller, taller, whole, whole))  6.94 us
    ppermute x3, waiting for transfers between devices, run(): outside = lax.ppermute(inn, AXES, along_ax(-1))  6.45 us
    all_to_all x1, starting transfers between devices, body(): whole_tile = lax.all_to_all(chunks, 'ax', 0, 0, tiled=True)  6.11 us
  transfers between devices with their start and end apart: 16, of which 5 were waited for; matrix products, arithmetic and copies ran while one was open for 0% of the time, Pallas kernels for 6%

profile of v2, /device:TPU:16, one launch (start us, length us, event | category | flops | bytes accessed | tf_op | source)
XLA Modules:
  0.0 123.8 jit_solution(5198001878985185397)
XLA Ops:
  0.0 2.2 %shard_map.46 = f32[8,5,32,128]{3,2,1,0:T(8,128)} custom-call(f32[2,32,512]{2,1,0:T(8,128)} %bitcast.13, f32[3,2,32,512]{3,2,1,0:T(8,128)} %bitcast.12, f32[2,32,512]{2,1,0:T(8,128)} %bitcast.14), custom_call_target="tpu_custom_call" | custom-call | flops 8000000 | bytes 3000000 | tf_op jit(solution)/shard_map/pallas_call | solution.py:415
  2.2 6.1 %all-to-all-start = ((f32[8,5,32,128]{3,2,1,0:T(8,128)}), f32[8,5,32,128]{3,2,1,0:T(8,128)S(1)}, u32[]{:S(2)}, u32[]{:S(2)}) async-start(f32[8,5,32,128]{3,2,1,0:T(8,128)} %shard_map.46), calls=%async_computation | async-start | bytes 1310720 | tf_op jit(solution)/shard_map/all_to_all | solution.py:416
  8.3 11.5 %all-to-all-done.in_ref = f32[8,5,32,128]{3,2,1,0:T(8,128)S(1)} async-done(((f32[8,5,32,128]{3,2,1,0:T(8,128)}), f32[8,5,32,128]{3,2,1,0:T(8,128)S(1)}, u32[]{:S(2)}, u32[]{:S(2)}) %all-to-all-start) | async-done | bytes 655392 | tf_op jit(solution)/shard_map/all_to_all | solution.py:416
  19.8 0.0 copy-start
  19.8 0.8 copy-done
  20.6 1.8 %shard_map.47 = (f32[20,8,128]{2,1,0:T(8,128)}, f32[20,8,128]{2,1,0:T(8,128)}) custom-call(s32[1]{0:T(128)} %bitcast.2.code_ref, f32[8,5,32,128]{3,2,1,0:T(8,128)} %copy-done), custom_call_target="tpu_custom_call" | custom-call | flops 8000000 | bytes 3000000 | tf_op jit(solution)/shard_map/pallas_call | solution.py:421
  22.4 1.9 %collective-permute-start.128 = (f32[20,8,128]{2,1,0:T(8,128)}, f32[20,8,128]{2,1,0:T(8,128)S(1)}, u32[]{:S(2)}, u32[]{:S(2)}) collective-permute-start(f32[20,8,128]{2,1,0:T(8,128)} %get-tuple-element.699), channel_id=1, source_target_pairs={{257,0},{0,257},{258,1},{1,258},{259,2},{2,259},{260,3},{3,260},{2... | collective-permute-start | bytes 245768 | tf_op jit(solution)/shard_map/ppermute | solution.py:422
  24.3 0.0 copy-start.3
  24.3 2.4 %collective-permute-start.130 = (f32[20,8,128]{2,1,0:T(8,128)}, f32[20,8,128]{2,1,0:T(8,128)S(1)}, u32[]{:S(2)}, u32[]{:S(2)}) collective-permute-start(f32[20,8,128]{2,1,0:T(8,128)} %get-tuple-element.700), channel_id=1, source_target_pairs={{0,31},{1,0},{2,1},{3,2},{4,3},{5,4},{6,5},{7,6},{8,7},{9,8},{10,9... | collective-permute-start | bytes 245768 | tf_op jit(solution)/shard_map/ppermute | solution.py:423
  26.7 1.7 %collective-permute-done.128 = f32[20,8,128]{2,1,0:T(8,128)S(1)} collective-permute-done((f32[20,8,128]{2,1,0:T(8,128)}, f32[20,8,128]{2,1,0:T(8,128)S(1)}, u32[]{:S(2)}, u32[]{:S(2)}) %collective-permute-start.128) | collective-permute-done | bytes 81952 | tf_op jit(solution)/shard_map/ppermute | solution.py:422
  28.3 1.9 %collective-permute-start.129 = (f32[20,8,128]{2,1,0:T(8,128)S(1)}, f32[20,8,128]{2,1,0:T(8,128)S(1)}, u32[]{:S(2)}, u32[]{:S(2)}) collective-permute-start(f32[20,8,128]{2,1,0:T(8,128)S(1)} %collective-permute-done.128), channel_id=1, source_target_pairs={{256,0},{0,256},{257,1},{1,257},{258,2},{2,258},{259,3},{3,259},{2... | collective-permute-start | bytes 245768 | tf_op jit(solution)/shard_map/ppermute | solution.py:424
  30.2 0.0 copy-done.3
  30.2 0.6 fusion
  32.6 0.0 collective-permute-done.130.two_ref
  32.6 0.0 copy-start.1
  32.6 0.0 collective-permute-done.129.one_ref
  32.6 0.6 copy-done.1
  33.2 0.0 copy-start.2
  33.2 0.6 copy-done.2
  33.8 1.7 %shard_map.48 = (f32[8,5,40,128]{3,2,1,0:T(8,128)S(1)}, f32[5,24,128]{2,1,0:T(8,128)S(1)}, f32[40,128]{1,0:T(8,128)S(1)}, f32[40,128]{1,0:T(8,128)S(1)}) custom-call(s32[1]{0:T(128)} %bitcast.2.code_ref, f32[8,5,32,128]{3,2,1,0:T(8,128)} %copy-done, f32[20,8,128]{2,1,0:T(8,128)} %copy-done.2, f32[20,8,128]{2,1,0:T(8,128)} %copy-done.1), custom_call_target="tpu_custom_call" | custom-call | flops 8000000 | bytes 3000000 | tf_op jit(solution)/shard_map/pallas_call | solution.py:425
  35.5 0.1 copy.166
  35.6 72.3 %while.20 = (s32[]{:T(128)}, f32[8,5,40,128]{3,2,1,0:T(8,128)S(1)}, f32[5,24,128]{2,1,0:T(8,128)S(1)}, f32[40,128]{1,0:T(8,128)S(1)}, f32[40,128]{1,0:T(8,128)S(...) while((s32[]{:T(128)}, f32[8,5,40,128]{3,2,1,0:T(8,128)S(1)}, ...), condition=%wide.region_33.0_spmd, body=%wide.region_0.0_spmd.sunk | while | flops 16000019 | bytes 6655944 | solution.py:453
  35.6 16.9 %conditional.2 = (f32[8,5,40,128]{3,2,1,0:T(8,128)S(1)}, f32[5,24,128]{2,1,0:T(8,128)}, f32[5,24,128]{2,1,0:T(8,128)}, f32[40,128]{1,0:T(8,128)}, f32[40,128]{1,0:T(8,128)}) conditional(s32[]{:T(128)} %clamp.6, (s32[1]{0:T(128)}, f32[8,5,40,128]{3,2,1,0:T(8,128)S(1)}, f32[8,5,40,128]{3,2,1,0:T(8,128)S(1)}, ...), branch_computations={%region_1.0_spmd, %region_2.0_spmd, %region_3.0_spmd, %region_4.0_... | conditional | flops 8000000 | bytes 3655560 | solution.py:446
  35.7 5.8 %collective-permute-start.5 = (f32[5,24,128]{2,1,0:T(8,128)S(1)}, f32[5,24,128]{2,1,0:T(8,128)}, u32[]{:S(2)}, u32[]{:S(2)}) collective-permute-start(f32[5,24,128]{2,1,0:T(8,128)S(1)} %get-tuple-element.491), channel_id=1, source_target_pairs={{258,0},{0,258},{259,1},{1,259},{260,2},{2,260},{261,3},{3,261},{2... | collective-permute-start | bytes 184328 | tf_op jit(solution)/shard_map/while/body/eval_jaxpr/cond/branch_1_fun/ppermute | solution.py:433
  41.5 1.9 %collective-permute-start.4 = (f32[5,24,128]{2,1,0:T(8,128)S(1)}, f32[5,24,128]{2,1,0:T(8,128)}, u32[]{:S(2)}, u32[]{:S(2)}) collective-permute-start(f32[5,24,128]{2,1,0:T(8,128)S(1)} %get-tuple-element.491), channel_id=1, source_target_pairs={{257,0},{0,257},{258,1},{1,258},{259,2},{2,259},{260,3},{3,260},{2... | collective-permute-start | bytes 184328 | tf_op jit(solution)/shard_map/while/body/eval_jaxpr/cond/branch_1_fun/ppermute | solution.py:432
  43.4 3.4 %collective-permute-start.6 = (f32[40,128]{1,0:T(8,128)S(1)}, f32[40,128]{1,0:T(8,128)}, u32[]{:S(2)}, u32[]{:S(2)}) collective-permute-start(f32[40,128]{1,0:T(8,128)S(1)} %get-tuple-element.492), channel_id=1, source_target_pairs={{0,32},{1,33},{2,34},{3,35},{4,36},{5,37},{6,38},{7,39},{8,40},{9,... | collective-permute-start | bytes 61448 | tf_op jit(solution)/shard_map/while/body/eval_jaxpr/cond/branch_1_fun/ppermute | solution.py:434
  46.8 1.3 %collective-permute-start.7 = (f32[40,128]{1,0:T(8,128)S(1)}, f32[40,128]{1,0:T(8,128)}, u32[]{:S(2)}, u32[]{:S(2)}) collective-permute-start(f32[40,128]{1,0:T(8,128)S(1)} %get-tuple-element.493), channel_id=1, source_target_pairs={{32,0},{33,1},{34,2},{35,3},{36,4},{37,5},{38,6},{39,7},{40,8},{41... | collective-permute-start | bytes 61448 | tf_op jit(solution)/shard_map/while/body/eval_jaxpr/cond/branch_1_fun/ppermute | solution.py:435
  48.1 2.3 %branch_1_fun.1 = f32[8,5,40,128]{3,2,1,0:T(8,128)S(1)} custom-call(s32[1]{0:T(128)} %get-tuple-element.488.code_ref, f32[8,5,40,128]{3,2,1,0:T(8,128)S(1)} %get-tuple-element.489.old_ref, f32[8,5,40,128]{3,2,1,0:T(8,128)S(1)} %get-tuple-element.490.now_ref), custom_call_target="tpu_custom_call" | custom-call | flops 8000000 | bytes 3000000 | tf_op jit(solution)/shard_map/while/body/eval_jaxpr/cond/branch_1_fun/pallas_call | solution.py:436
  50.4 0.0 collective-permute-done.6
  50.4 2.2 %collective-permute-done.7 = f32[40,128]{1,0:T(8,128)} collective-permute-done((f32[40,128]{1,0:T(8,128)S(1)}, f32[40,128]{1,0:T(8,128)}, u32[]{:S(2)}, u32[]{:S(2)}) %collective-permute-start.7) | collective-permute-done | bytes 20512 | tf_op jit(solution)/shard_map/while/body/eval_jaxpr/cond/branch_1_fun/ppermute | solution.py:435
  52.5 0.0 collective-permute-done.5
  52.6 0.0 collective-permute-done.4
  52.6 1.9 %eval_jaxpr.3 = (f32[8,5,40,128]{3,2,1,0:T(8,128)S(1)}, f32[5,24,128]{2,1,0:T(8,128)S(1)}, f32[40,128]{1,0:T(8,128)S(1)}, f32[40,128]{1,0:T(8,128)S(1)}) custom-call(s32[1]{0:T(128)} %bitcast.10.code_ref, s32[1]{0:T(128)} %bitcast.11.offsets_ref, f32[8,5,40,128]{3,2,1,0:T(8,128)S(1)} %get-tuple-element.783.base_ref, ...), custom_call_target="tpu_custom_call" | custom-call | flops 8000000 | bytes 3000000 | tf_op jit(solution)/shard_map/while/body/eval_jaxpr/pallas_call | solution.py:449
  54.5 29.6 %conditional.2 = (f32[8,5,40,128]{3,2,1,0:T(8,128)S(1)}, f32[5,24,128]{2,1,0:T(8,128)}, f32[5,24,128]{2,1,0:T(8,128)}, f32[40,128]{1,0:T(8,128)}, f32[40,128]{1,0:T(8,128)}) conditional(s32[]{:T(128)} %clamp.6, (s32[1]{0:T(128)}, f32[8,5,40,128]{3,2,1,0:T(8,128)S(1)}, f32[8,5,40,128]{3,2,1,0:T(8,128)S(1)}, ...), branch_computations={%region_1.0_spmd, %region_2.0_spmd, %region_3.0_spmd, %region_4.0_... | conditional | flops 8000000 | bytes 3655560 | solution.py:446
  54.5 10.2 %collective-permute-start.73 = (f32[5,24,128]{2,1,0:T(8,128)S(1)}, f32[5,24,128]{2,1,0:T(8,128)}, u32[]{:S(2)}, u32[]{:S(2)}) collective-permute-start(f32[5,24,128]{2,1,0:T(8,128)S(1)} %get-tuple-element.593), channel_id=1, source_target_pairs={{275,0},{0,275},{276,1},{1,276},{277,2},{2,277},{278,3},{3,278},{2... | collective-permute-start | bytes 184328 | tf_op jit(solution)/shard_map/while/body/eval_jaxpr/cond/branch_18_fun/ppermute | solution.py:433
  64.7 9.5 %collective-permute-start.72 = (f32[5,24,128]{2,1,0:T(8,128)S(1)}, f32[5,24,128]{2,1,0:T(8,128)}, u32[]{:S(2)}, u32[]{:S(2)}) collective-permute-start(f32[5,24,128]{2,1,0:T(8,128)S(1)} %get-tuple-element.593), channel_id=1, source_target_pairs={{274,0},{0,274},{275,1},{1,275},{276,2},{2,276},{277,3},{3,277},{2... | collective-permute-start | bytes 184328 | tf_op jit(solution)/shard_map/while/body/eval_jaxpr/cond/branch_18_fun/ppermute | solution.py:432
  74.2 4.1 %collective-permute-start.74 = (f32[40,128]{1,0:T(8,128)S(1)}, f32[40,128]{1,0:T(8,128)}, u32[]{:S(2)}, u32[]{:S(2)}) collective-permute-start(f32[40,128]{1,0:T(8,128)S(1)} %get-tuple-element.594), channel_id=1, source_target_pairs={{0,32},{1,33},{2,34},{3,35},{4,36},{5,37},{6,38},{7,39},{8,40},{9,... | collective-permute-start | bytes 61448 | tf_op jit(solution)/shard_map/while/body/eval_jaxpr/cond/branch_18_fun/ppermute | solution.py:434
  78.3 1.3 %collective-permute-start.75 = (f32[40,128]{1,0:T(8,128)S(1)}, f32[40,128]{1,0:T(8,128)}, u32[]{:S(2)}, u32[]{:S(2)}) collective-permute-start(f32[40,128]{1,0:T(8,128)S(1)} %get-tuple-element.595), channel_id=1, source_target_pairs={{32,0},{33,1},{34,2},{35,3},{36,4},{37,5},{38,6},{39,7},{40,8},{41... | collective-permute-start | bytes 61448 | tf_op jit(solution)/shard_map/while/body/eval_jaxpr/cond/branch_18_fun/ppermute | solution.py:435
  79.6 2.3 %branch_18_fun.1 = f32[8,5,40,128]{3,2,1,0:T(8,128)S(1)} custom-call(s32[1]{0:T(128)} %get-tuple-element.590.code_ref, f32[8,5,40,128]{3,2,1,0:T(8,128)S(1)} %get-tuple-element.591.old_ref, f32[8,5,40,128]{3,2,1,0:T(8,128)S(1)} %get-tuple-element.592.now_ref), custom_call_target="tpu_custom_call" | custom-call | flops 8000000 | bytes 3000000 | tf_op jit(solution)/shard_map/while/body/eval_jaxpr/cond/branch_18_fun/pallas_call | solution.py:436
  81.9 0.0 collective-permute-done.74
  81.9 2.2 %collective-permute-done.75 = f32[40,128]{1,0:T(8,128)} collective-permute-done((f32[40,128]{1,0:T(8,128)S(1)}, f32[40,128]{1,0:T(8,128)}, u32[]{:S(2)}, u32[]{:S(2)}) %collective-permute-start.75) | collective-permute-done | bytes 20512 | tf_op jit(solution)/shard_map/while/body/eval_jaxpr/cond/branch_18_fun/ppermute | solution.py:435
  84.0 0.0 collective-permute-done.73
  84.0 0.0 collective-permute-done.72
  84.1 1.9 %eval_jaxpr.3 = (f32[8,5,40,128]{3,2,1,0:T(8,128)S(1)}, f32[5,24,128]{2,1,0:T(8,128)S(1)}, f32[40,128]{1,0:T(8,128)S(1)}, f32[40,128]{1,0:T(8,128)S(1)}) custom-call(s32[1]{0:T(128)} %bitcast.10.code_ref, s32[1]{0:T(128)} %bitcast.11.offsets_ref, f32[8,5,40,128]{3,2,1,0:T(8,128)S(1)} %get-tuple-element.783.base_ref, ...), custom_call_target="tpu_custom_call" | custom-call | flops 8000000 | bytes 3000000 | tf_op jit(solution)/shard_map/while/body/eval_jaxpr/pallas_call | solution.py:449
  85.9 20.1 %conditional.2 = (f32[8,5,40,128]{3,2,1,0:T(8,128)S(1)}, f32[5,24,128]{2,1,0:T(8,128)}, f32[5,24,128]{2,1,0:T(8,128)}, f32[40,128]{1,0:T(8,128)}, f32[40,128]{1,0:T(8,128)}) conditional(s32[]{:T(128)} %clamp.6, (s32[1]{0:T(128)}, f32[8,5,40,128]{3,2,1,0:T(8,128)S(1)}, f32[8,5,40,128]{3,2,1,0:T(8,128)S(1)}, ...), branch_computations={%region_1.0_spmd, %region_2.0_spmd, %region_3.0_spmd, %region_4.0_... | conditional | flops 8000000 | bytes 3655560 | solution.py:446
  86.0 1.9 %collective-permute-start.9 = (f32[5,24,128]{2,1,0:T(8,128)S(1)}, f32[5,24,128]{2,1,0:T(8,128)}, u32[]{:S(2)}, u32[]{:S(2)}) collective-permute-start(f32[5,24,128]{2,1,0:T(8,128)S(1)} %get-tuple-element.497), channel_id=1, source_target_pairs={{259,0},{0,259},{260,1},{1,260},{261,2},{2,261},{262,3},{3,262},{2... | collective-permute-start | bytes 184328 | tf_op jit(solution)/shard_map/while/body/eval_jaxpr/cond/branch_2_fun/ppermute | solution.py:433
  87.9 9.2 %collective-permute-start.8 = (f32[5,24,128]{2,1,0:T(8,128)S(1)}, f32[5,24,128]{2,1,0:T(8,128)}, u32[]{:S(2)}, u32[]{:S(2)}) collective-permute-start(f32[5,24,128]{2,1,0:T(8,128)S(1)} %get-tuple-element.497), channel_id=1, source_target_pairs={{258,0},{0,258},{259,1},{1,259},{260,2},{2,260},{261,3},{3,261},{2... | collective-permute-start | bytes 184328 | tf_op jit(solution)/shard_map/while/body/eval_jaxpr/cond/branch_2_fun/ppermute | solution.py:432
  97.1 3.2 %collective-permute-start.10 = (f32[40,128]{1,0:T(8,128)S(1)}, f32[40,128]{1,0:T(8,128)}, u32[]{:S(2)}, u32[]{:S(2)}) collective-permute-start(f32[40,128]{1,0:T(8,128)S(1)} %get-tuple-element.498), channel_id=1, source_target_pairs={{0,32},{1,33},{2,34},{3,35},{4,36},{5,37},{6,38},{7,39},{8,40},{9,... | collective-permute-start | bytes 61448 | tf_op jit(solution)/shard_map/while/body/eval_jaxpr/cond/branch_2_fun/ppermute | solution.py:434
  100.3 1.3 %collective-permute-start.11 = (f32[40,128]{1,0:T(8,128)S(1)}, f32[40,128]{1,0:T(8,128)}, u32[]{:S(2)}, u32[]{:S(2)}) collective-permute-start(f32[40,128]{1,0:T(8,128)S(1)} %get-tuple-element.499), channel_id=1, source_target_pairs={{32,0},{33,1},{34,2},{35,3},{36,4},{37,5},{38,6},{39,7},{40,8},{41... | collective-permute-start | bytes 61448 | tf_op jit(solution)/shard_map/while/body/eval_jaxpr/cond/branch_2_fun/ppermute | solution.py:435
  101.6 2.3 %branch_2_fun.1 = f32[8,5,40,128]{3,2,1,0:T(8,128)S(1)} custom-call(s32[1]{0:T(128)} %get-tuple-element.494.code_ref, f32[8,5,40,128]{3,2,1,0:T(8,128)S(1)} %get-tuple-element.495.old_ref, f32[8,5,40,128]{3,2,1,0:T(8,128)S(1)} %get-tuple-element.496.now_ref), custom_call_target="tpu_custom_call" | custom-call | flops 8000000 | bytes 3000000 | tf_op jit(solution)/shard_map/while/body/eval_jaxpr/cond/branch_2_fun/pallas_call | solution.py:436
  103.9 0.0 collective-permute-done.10
  103.9 2.2 %collective-permute-done.11 = f32[40,128]{1,0:T(8,128)} collective-permute-done((f32[40,128]{1,0:T(8,128)S(1)}, f32[40,128]{1,0:T(8,128)}, u32[]{:S(2)}, u32[]{:S(2)}) %collective-permute-start.11) | collective-permute-done | bytes 20512 | tf_op jit(solution)/shard_map/while/body/eval_jaxpr/cond/branch_2_fun/ppermute | solution.py:435
  106.1 0.0 collective-permute-done.9
  106.1 0.0 collective-permute-done.8
  106.1 1.9 %eval_jaxpr.3 = (f32[8,5,40,128]{3,2,1,0:T(8,128)S(1)}, f32[5,24,128]{2,1,0:T(8,128)S(1)}, f32[40,128]{1,0:T(8,128)S(1)}, f32[40,128]{1,0:T(8,128)S(1)}) custom-call(s32[1]{0:T(128)} %bitcast.10.code_ref, s32[1]{0:T(128)} %bitcast.11.offsets_ref, f32[8,5,40,128]{3,2,1,0:T(8,128)S(1)} %get-tuple-element.783.base_ref, ...), custom_call_target="tpu_custom_call" | custom-call | flops 8000000 | bytes 3000000 | tf_op jit(solution)/shard_map/while/body/eval_jaxpr/pallas_call | solution.py:449
  107.9 0.1 slice.15
  108.0 13.6 %all_to_all.10.in_ref = f32[8,5,32,128]{3,2,1,0:T(8,128)} all-to-all(f32[8,5,32,128]{3,2,1,0:T(8,128)S(1)} %slice.15), channel_id=1, replica_groups=mesh['row'=2,'ax'=8,'az'=32] {'ax'}, dimensions={0} | all-to-all | bytes 1310720 | tf_op jit(solution)/shard_map/all_to_all | solution.py:454
  121.6 2.2 %shard_map.49 = f32[5,2,32,512]{3,2,1,0:T(8,128)} custom-call(f32[8,5,32,128]{3,2,1,0:T(8,128)} %all_to_all.10.in_ref), custom_call_target="tpu_custom_call" | custom-call | flops 8000000 | bytes 3000000 | tf_op jit(solution)/shard_map/pallas_call | solution.py:455
Async XLA Ops:
  2.2 17.6 %all-to-all-start = ((f32[8,5,32,128]{3,2,1,0:T(8,128)}), f32[8,5,32,128]{3,2,1,0:T(8,128)S(1)}, u32[]{:S(2)}, u32[]{:S(2)}) async-start(f32[8,5,32,128]{3,2,1,0:T(8,128)} %shard_map.46), calls=%async_computation | async-start | bytes 1310720 | tf_op jit(solution)/shard_map/all_to_all | solution.py:416
  19.8 0.8 copy-start
  22.4 6.0 %collective-permute-start.128 = (f32[20,8,128]{2,1,0:T(8,128)}, f32[20,8,128]{2,1,0:T(8,128)S(1)}, u32[]{:S(2)}, u32[]{:S(2)}) collective-permute-start(f32[20,8,128]{2,1,0:T(8,128)} %get-tuple-element.699), channel_id=1, source_target_pairs={{257,0},{0,257},{258,1},{1,258},{259,2},{2,259},{260,3},{3,260},{2... | collective-permute-start | bytes 245768 | tf_op jit(solution)/shard_map/ppermute | solution.py:422
  24.3 6.0 %copy-start.3 = (s32[3]{0:T(128)S(1)}, s32[3]{0:T(128)}, u32[]{:S(2)}) copy-start(s32[3]{0:T(128)} %param.41) | copy-start | bytes 40
  24.3 8.3 %collective-permute-start.130 = (f32[20,8,128]{2,1,0:T(8,128)}, f32[20,8,128]{2,1,0:T(8,128)S(1)}, u32[]{:S(2)}, u32[]{:S(2)}) collective-permute-start(f32[20,8,128]{2,1,0:T(8,128)} %get-tuple-element.700), channel_id=1, source_target_pairs={{0,31},{1,0},{2,1},{3,2},{4,3},{5,4},{6,5},{7,6},{8,7},{9,8},{10,9... | collective-permute-start | bytes 245768 | tf_op jit(solution)/shard_map/ppermute | solution.py:423
  28.3 4.3 %collective-permute-start.129 = (f32[20,8,128]{2,1,0:T(8,128)S(1)}, f32[20,8,128]{2,1,0:T(8,128)S(1)}, u32[]{:S(2)}, u32[]{:S(2)}) collective-permute-start(f32[20,8,128]{2,1,0:T(8,128)S(1)} %collective-permute-done.128), channel_id=1, source_target_pairs={{256,0},{0,256},{257,1},{1,257},{258,2},{2,258},{259,3},{3,259},{2... | collective-permute-start | bytes 245768 | tf_op jit(solution)/shard_map/ppermute | solution.py:424
  32.6 0.6 copy-start.1
  33.2 0.6 copy-start.2
  35.7 16.9 %collective-permute-start.5 = (f32[5,24,128]{2,1,0:T(8,128)S(1)}, f32[5,24,128]{2,1,0:T(8,128)}, u32[]{:S(2)}, u32[]{:S(2)}) collective-permute-start(f32[5,24,128]{2,1,0:T(8,128)S(1)} %get-tuple-element.491), channel_id=1, source_target_pairs={{258,0},{0,258},{259,1},{1,259},{260,2},{2,260},{261,3},{3,261},{2... | collective-permute-start | bytes 184328 | tf_op jit(solution)/shard_map/while/body/eval_jaxpr/cond/branch_1_fun/ppermute | solution.py:433
  41.5 11.1 %collective-permute-start.4 = (f32[5,24,128]{2,1,0:T(8,128)S(1)}, f32[5,24,128]{2,1,0:T(8,128)}, u32[]{:S(2)}, u32[]{:S(2)}) collective-permute-start(f32[5,24,128]{2,1,0:T(8,128)S(1)} %get-tuple-element.491), channel_id=1, source_target_pairs={{257,0},{0,257},{258,1},{1,258},{259,2},{2,259},{260,3},{3,260},{2... | collective-permute-start | bytes 184328 | tf_op jit(solution)/shard_map/while/body/eval_jaxpr/cond/branch_1_fun/ppermute | solution.py:432
  43.4 7.0 %collective-permute-start.6 = (f32[40,128]{1,0:T(8,128)S(1)}, f32[40,128]{1,0:T(8,128)}, u32[]{:S(2)}, u32[]{:S(2)}) collective-permute-start(f32[40,128]{1,0:T(8,128)S(1)} %get-tuple-element.492), channel_id=1, source_target_pairs={{0,32},{1,33},{2,34},{3,35},{4,36},{5,37},{6,38},{7,39},{8,40},{9,... | collective-permute-start | bytes 61448 | tf_op jit(solution)/shard_map/while/body/eval_jaxpr/cond/branch_1_fun/ppermute | solution.py:434
  46.8 5.8 %collective-permute-start.7 = (f32[40,128]{1,0:T(8,128)S(1)}, f32[40,128]{1,0:T(8,128)}, u32[]{:S(2)}, u32[]{:S(2)}) collective-permute-start(f32[40,128]{1,0:T(8,128)S(1)} %get-tuple-element.493), channel_id=1, source_target_pairs={{32,0},{33,1},{34,2},{35,3},{36,4},{37,5},{38,6},{39,7},{40,8},{41... | collective-permute-start | bytes 61448 | tf_op jit(solution)/shard_map/while/body/eval_jaxpr/cond/branch_1_fun/ppermute | solution.py:435
  54.5 29.5 %collective-permute-start.73 = (f32[5,24,128]{2,1,0:T(8,128)S(1)}, f32[5,24,128]{2,1,0:T(8,128)}, u32[]{:S(2)}, u32[]{:S(2)}) collective-permute-start(f32[5,24,128]{2,1,0:T(8,128)S(1)} %get-tuple-element.593), channel_id=1, source_target_pairs={{275,0},{0,275},{276,1},{1,276},{277,2},{2,277},{278,3},{3,278},{2... | collective-permute-start | bytes 184328 | tf_op jit(solution)/shard_map/while/body/eval_jaxpr/cond/branch_18_fun/ppermute | solution.py:433
  64.7 19.3 %collective-permute-start.72 = (f32[5,24,128]{2,1,0:T(8,128)S(1)}, f32[5,24,128]{2,1,0:T(8,128)}, u32[]{:S(2)}, u32[]{:S(2)}) collective-permute-start(f32[5,24,128]{2,1,0:T(8,128)S(1)} %get-tuple-element.593), channel_id=1, source_target_pairs={{274,0},{0,274},{275,1},{1,275},{276,2},{2,276},{277,3},{3,277},{2... | collective-permute-start | bytes 184328 | tf_op jit(solution)/shard_map/while/body/eval_jaxpr/cond/branch_18_fun/ppermute | solution.py:432
  74.2 7.7 %collective-permute-start.74 = (f32[40,128]{1,0:T(8,128)S(1)}, f32[40,128]{1,0:T(8,128)}, u32[]{:S(2)}, u32[]{:S(2)}) collective-permute-start(f32[40,128]{1,0:T(8,128)S(1)} %get-tuple-element.594), channel_id=1, source_target_pairs={{0,32},{1,33},{2,34},{3,35},{4,36},{5,37},{6,38},{7,39},{8,40},{9,... | collective-permute-start | bytes 61448 | tf_op jit(solution)/shard_map/while/body/eval_jaxpr/cond/branch_18_fun/ppermute | solution.py:434
  78.3 5.8 %collective-permute-start.75 = (f32[40,128]{1,0:T(8,128)S(1)}, f32[40,128]{1,0:T(8,128)}, u32[]{:S(2)}, u32[]{:S(2)}) collective-permute-start(f32[40,128]{1,0:T(8,128)S(1)} %get-tuple-element.595), channel_id=1, source_target_pairs={{32,0},{33,1},{34,2},{35,3},{36,4},{37,5},{38,6},{39,7},{40,8},{41... | collective-permute-start | bytes 61448 | tf_op jit(solution)/shard_map/while/body/eval_jaxpr/cond/branch_18_fun/ppermute | solution.py:435
  86.0 20.1 %collective-permute-start.9 = (f32[5,24,128]{2,1,0:T(8,128)S(1)}, f32[5,24,128]{2,1,0:T(8,128)}, u32[]{:S(2)}, u32[]{:S(2)}) collective-permute-start(f32[5,24,128]{2,1,0:T(8,128)S(1)} %get-tuple-element.497), channel_id=1, source_target_pairs={{259,0},{0,259},{260,1},{1,260},{261,2},{2,261},{262,3},{3,262},{2... | collective-permute-start | bytes 184328 | tf_op jit(solution)/shard_map/while/body/eval_jaxpr/cond/branch_2_fun/ppermute | solution.py:433
  87.9 18.2 %collective-permute-start.8 = (f32[5,24,128]{2,1,0:T(8,128)S(1)}, f32[5,24,128]{2,1,0:T(8,128)}, u32[]{:S(2)}, u32[]{:S(2)}) collective-permute-start(f32[5,24,128]{2,1,0:T(8,128)S(1)} %get-tuple-element.497), channel_id=1, source_target_pairs={{258,0},{0,258},{259,1},{1,259},{260,2},{2,260},{261,3},{3,261},{2... | collective-permute-start | bytes 184328 | tf_op jit(solution)/shard_map/while/body/eval_jaxpr/cond/branch_2_fun/ppermute | solution.py:432
  97.1 6.8 %collective-permute-start.10 = (f32[40,128]{1,0:T(8,128)S(1)}, f32[40,128]{1,0:T(8,128)}, u32[]{:S(2)}, u32[]{:S(2)}) collective-permute-start(f32[40,128]{1,0:T(8,128)S(1)} %get-tuple-element.498), channel_id=1, source_target_pairs={{0,32},{1,33},{2,34},{3,35},{4,36},{5,37},{6,38},{7,39},{8,40},{9,... | collective-permute-start | bytes 61448 | tf_op jit(solution)/shard_map/while/body/eval_jaxpr/cond/branch_2_fun/ppermute | solution.py:434
  100.3 5.8 %collective-permute-start.11 = (f32[40,128]{1,0:T(8,128)S(1)}, f32[40,128]{1,0:T(8,128)}, u32[]{:S(2)}, u32[]{:S(2)}) collective-permute-start(f32[40,128]{1,0:T(8,128)S(1)} %get-tuple-element.499), channel_id=1, source_target_pairs={{32,0},{33,1},{34,2},{35,3},{36,4},{37,5},{38,6},{39,7},{40,8},{41... | collective-permute-start | bytes 61448 | tf_op jit(solution)/shard_map/while/body/eval_jaxpr/cond/branch_2_fun/ppermute | solution.py:435

commit v3 on v2

--- a/solution.py
+++ b/solution.py
@@ -18,6 +18,7 @@
 SUB = 8
 LANES = 128
 HALF = 64
+KERNEL_VMEM = 12 * 2**20
 EDGE = 4
 
 
@@ -188,7 +189,8 @@
                 out_ref[k, 1, rows, cols] = jnp.where(low, pltpu.roll(inner, HALF, 1), outer)
 
 
-def write_sends(state_ref, co, up_ref, out_ref, inn_ref):
+def write_sends(state_ref, co, segment, up_ref, one_ref, two_ref):
+    odd = lax.rem(segment, 2) == 1
     lane, place = lanes_of()
     pairs = state_ref.shape[0]
     blocks = state_ref.shape[2] // SUB
@@ -209,8 +211,8 @@
                 packed_in = jnp.where(here, moved, packed_in)
             if a == pairs - 1:
                 top.append(axial_terms(c)[0])
-        out_ref[rows, :] = packed_out
-        inn_ref[rows, :] = packed_in
+        one_ref[rows, :] = jnp.where(odd, packed_in, packed_out)
+        two_ref[rows, :] = jnp.where(odd, packed_out, packed_in)
     half = up_ref.shape[1] // SUB
     for b in range(half):
         for k in range(FIELDS):
@@ -232,7 +234,7 @@
             state_ref[a, k, pl.ds(EDGE, rows), :] = in_ref[a, k]
             state_ref[a, k, pl.ds(EDGE + rows, EDGE), :] = jnp.where(rotor, two, one)
     co = coefficients(segment, cycle_cells)
-    write_sends(state_ref, co, *sends)
+    write_sends(state_ref, co, segment, *sends)
 
 
 def local_kernel(cycle_cells, code_ref, old_ref, now_ref, base_ref, nxt_s, prv_s, up_s, dn_s):
@@ -314,11 +316,12 @@
     lax.fori_loop(0, pairs, finish, 0)
 
 
-def join_kernel(cycle_cells, code_ref, offsets_ref, base_ref, turn_ref, turn2_ref, inside_ref,
-                outside_ref, state_ref, *sends):
+def join_kernel(cycle_cells, code_ref, offsets_ref, base_ref, turn_ref, turn2_ref, one_ref,
+                two_ref, state_ref, *sends):
     step, segment, rotor = decode(code_ref, base_ref.shape[0])
     co = coefficients(segment, cycle_cells)
     _, _, rate_w = weights_of(step)
+    odd = lax.rem(segment, 2) == 1
     lane, place = lanes_of()
     pairs = base_ref.shape[0]
     blocks = base_ref.shape[2] // SUB
@@ -341,7 +344,8 @@
 
     for b in range(blocks):
         rows = pl.ds(b * SUB, SUB)
-        inside, outside = inside_ref[rows, :], outside_ref[rows, :]
+        inside = jnp.where(odd, one_ref[rows, :], two_ref[rows, :])
+        outside = jnp.where(odd, two_ref[rows, :], one_ref[rows, :])
         for a in range(pairs):
             for k in range(FIELDS):
                 j = a * FIELDS + k
@@ -358,7 +362,7 @@
         turned = jnp.where(upper_half, mixed, 0.0)
         signed = -rate_w if k == 3 else rate_w
         state_ref[pairs - 1, k] = state_ref[pairs - 1, k] + signed * turned
-    write_sends(state_ref, co, *sends)
+    write_sends(state_ref, co, segment, *sends)
 
 
 def body(density, velocity, pressure, offsets):
@@ -381,9 +385,11 @@
 
     every = [(row, ax, az) for row in range(2) for ax in range(n_ax) for az in range(n_az)]
 
-    def along_ax(by):
+    def swapped(first):
+        partner = lambda x: x + 1 if (x - first) % 2 == 0 else x - 1
         return [
-            (device(r, x, z), device(r, x + by, z)) for r, x, z in every if 0 <= x + by < n_ax
+            (device(r, x, z), device(r, partner(x), z)) for r, x, z in every
+            if 0 <= partner(x) < n_ax
         ]
 
     def turned(by):
@@ -403,6 +409,7 @@
             in_specs=[smem] * n_smem + [vmem] * n_vmem,
             out_specs=jax.tree.map(lambda _: vmem, outs),
             scratch_shapes=list(scratch),
+            compiler_params=pltpu.CompilerParams(vmem_limit_bytes=KERNEL_VMEM),
             cost_estimate=pl.CostEstimate(
                 flops=8_000_000, bytes_accessed=3_000_000, transcendentals=0
             ),
@@ -428,15 +435,15 @@
     carry = (start, *first)
 
     def branch(by):
-        def run(code, now, up, out, inn):
+        def run(code, now, up, one, two):
             turn1 = lax.ppermute(up, AXES, turned(by))
             turn2 = lax.ppermute(up, AXES, turned((by + 1) % n_az))
-            inside = lax.ppermute(out, AXES, along_ax(1))
-            outside = lax.ppermute(inn, AXES, along_ax(-1))
+            one = lax.ppermute(one, AXES, swapped(0))
+            two = lax.ppermute(two, AXES, swapped(1))
             base = call(kernel_of(local_kernel), block, 1, 2, (taller, taller, whole, whole))(
                 code, start, now
             )
-            return base, turn1, turn2, inside, outside
+            return base, turn1, turn2, one, two
         return run
 
     def substep(_, carry):

time: 126 us -> 122 us (0.968); the launches traced: 124 us -> 122 us
  waiting for transfers between devices: 19.6 us -> 13 us
  starting transfers between devices: 65.3 us -> 71.7 us
  Pallas kernels: 20.3 us -> 15.2 us
  blocking collectives: 13.6 us -> 16.4 us
    ppermute x3, starting transfers between devices: 17.9 us -> 25.4 us  [run(): turn2 = lax.ppermute(up, AXES, turned((by + 1) % n_az))]
    ppermute x6, waiting for transfers between devices: 6.46 us -> 0.02 us  [the longest x3 0.01 us: run(): one = lax.ppermute(one, AXES, swapped(0))]
    ppermute x3, starting transfers between devices: 20.6 us -> 16.3 us  [run(): turn1 = lax.ppermute(up, AXES, turned(by))]
    ppermute x6, starting transfers between devices: 14.4 us -> 17.7 us  [the longest x3 13.9 us: run(): one = lax.ppermute(one, AXES, swapped(0))]
    all_to_all x1, blocking collectives: 13.6 us -> 16.4 us  [body(): lax.all_to_all(carry[0][:, :, EDGE:EDGE + tile], 'ax', 0, 0, tiled=True)]
    pallas_call x1, Pallas kernels: 1.77 us -> 0.02 us  [body(): call(edge_kernel, (outer_rows, outer_rows), 1, 1)(code_1, whole_tile)]
  transfers between devices with their start and end apart: 16 -> 16, of which waited for: 5 -> 2; matrix products, arithmetic and copies ran while one was open for 0% -> 1% of each run, Pallas kernels for 6% -> 6%
where the time goes in v3:
time: 122 us
  starting transfers between devices  71.7 us (59%)
  blocking collectives  16.4 us (13%)
  Pallas kernels  15.2 us (12%)
  waiting for transfers between devices  13 us (11%)
  local copies, waits for them, and re-layouts  3.6 us (3%)
  between operations  1.97 us (2%)
    ppermute x3, starting transfers between devices, run(): turn2 = lax.ppermute(up, AXES, turned((by + 1) % n_az))  25.4 us
    all_to_all x1, blocking collectives, body(): lax.all_to_all(carry[0][:, :, EDGE:EDGE + tile], 'ax', 0, 0, tiled=True)  16.4 us
    ppermute x3, starting transfers between devices, run(): turn1 = lax.ppermute(up, AXES, turned(by))  16.3 us
    ppermute x3, starting transfers between devices, run(): one = lax.ppermute(one, AXES, swapped(0))  13.9 us
    all_to_all x1, waiting for transfers between devices, body(): whole_tile = lax.all_to_all(chunks, 'ax', 0, 0, tiled=True)  11.5 us
    pallas_call x3, Pallas kernels, run(): call(kernel_of(local_kernel), block, 1, 2, (taller, taller, whole, whole))  6.93 us
    all_to_all x1, starting transfers between devices, body(): whole_tile = lax.all_to_all(chunks, 'ax', 0, 0, tiled=True)  6.11 us
    pallas_call x3, Pallas kernels, substep(): call(kernel_of(join_kernel), (block, *sends), 2, 5)(code_1, left, *terms)  5.59 us
  transfers between devices with their start and end apart: 16, of which 2 were waited for; matrix products, arithmetic and copies ran while one was open for 1% of the time, Pallas kernels for 6%

profile of v3, /device:TPU:16, one launch (start us, length us, event | category | flops | bytes accessed | tf_op | source)
XLA Modules:
  0.0 122.3 jit_solution(12458198155349425137)
XLA Ops:
  0.0 0.0 copy-start
  0.0 1.0 copy-done
  1.0 0.0 copy-start.1
  1.0 0.9 copy-done.1
  1.9 0.0 copy-start.2
  1.9 0.9 copy-done.2
  2.8 1.1 shard_map.46
  3.9 6.1 %all-to-all-start = ((f32[8,5,32,128]{3,2,1,0:T(8,128)}), f32[8,5,32,128]{3,2,1,0:T(8,128)S(1)}, u32[]{:S(2)}, u32[]{:S(2)}) async-start(f32[8,5,32,128]{3,2,1,0:T(8,128)} %shard_map.46), calls=%async_computation | async-start | bytes 1310720 | tf_op jit(solution)/shard_map/all_to_all | solution.py:423
  10.0 11.5 %all-to-all-done.in_ref = f32[8,5,32,128]{3,2,1,0:T(8,128)S(1)} async-done(((f32[8,5,32,128]{3,2,1,0:T(8,128)}), f32[8,5,32,128]{3,2,1,0:T(8,128)S(1)}, u32[]{:S(2)}, u32[]{:S(2)}) %all-to-all-start) | async-done | bytes 655392 | tf_op jit(solution)/shard_map/all_to_all | solution.py:423
  21.5 1.9 %collective-permute-start.128 = (f32[20,8,128]{2,1,0:T(8,128)S(1)}, f32[20,8,128]{2,1,0:T(8,128)S(1)}, u32[]{:S(2)}, u32[]{:S(2)}) collective-permute-start(f32[20,8,128]{2,1,0:T(8,128)S(1)} %get-tuple-element.699), channel_id=1, source_target_pairs={{257,0},{0,257},{258,1},{1,258},{259,2},{2,259},{260,3},{3,260},{2... | collective-permute-start | bytes 245768 | tf_op jit(solution)/shard_map/ppermute | solution.py:429
  23.4 0.0 copy-start.3
  23.4 2.4 %collective-permute-start.130 = (f32[20,8,128]{2,1,0:T(8,128)S(1)}, f32[20,8,128]{2,1,0:T(8,128)S(1)}, u32[]{:S(2)}, u32[]{:S(2)}) collective-permute-start(f32[20,8,128]{2,1,0:T(8,128)S(1)} %get-tuple-element.700), channel_id=1, source_target_pairs={{0,31},{1,0},{2,1},{3,2},{4,3},{5,4},{6,5},{7,6},{8,7},{9,8},{10,9... | collective-permute-start | bytes 245768 | tf_op jit(solution)/shard_map/ppermute | solution.py:430
  25.8 1.5 %collective-permute-done.128 = f32[20,8,128]{2,1,0:T(8,128)S(1)} collective-permute-done((f32[20,8,128]{2,1,0:T(8,128)S(1)}, f32[20,8,128]{2,1,0:T(8,128)S(1)}, u32[]{:S(2)}, u32[]{:S(2)}) %collective-permute-start.128) | collective-permute-done | bytes 81952 | tf_op jit(solution)/shard_map/ppermute | solution.py:429
  27.3 1.9 %collective-permute-start.129 = (f32[20,8,128]{2,1,0:T(8,128)S(1)}, f32[20,8,128]{2,1,0:T(8,128)S(1)}, u32[]{:S(2)}, u32[]{:S(2)}) collective-permute-start(f32[20,8,128]{2,1,0:T(8,128)S(1)} %collective-permute-done.128), channel_id=1, source_target_pairs={{256,0},{0,256},{257,1},{1,257},{258,2},{2,258},{259,3},{3,259},{2... | collective-permute-start | bytes 245768 | tf_op jit(solution)/shard_map/ppermute | solution.py:431
  29.2 0.0 copy-done.3
  29.2 0.7 fusion
  31.7 0.0 collective-permute-done.130.two_ref
  31.7 0.0 collective-permute-done.129.one_ref
  31.7 0.5 shard_map.48
  32.3 0.1 copy.166
  32.4 72.4 %while.20 = (s32[]{:T(128)}, f32[8,5,40,128]{3,2,1,0:T(8,128)S(1)}, f32[5,24,128]{2,1,0:T(8,128)S(1)}, f32[40,128]{1,0:T(8,128)S(1)}, f32[40,128]{1,0:T(8,128)S(...) while((s32[]{:T(128)}, f32[8,5,40,128]{3,2,1,0:T(8,128)S(1)}, ...), condition=%wide.region_33.0_spmd, body=%wide.region_0.0_spmd.sunk | while | flops 16000019 | bytes 6655944 | solution.py:460
  32.4 14.2 %conditional.2 = (f32[8,5,40,128]{3,2,1,0:T(8,128)S(1)}, f32[5,24,128]{2,1,0:T(8,128)}, f32[5,24,128]{2,1,0:T(8,128)}, f32[40,128]{1,0:T(8,128)}, f32[40,128]{1,0:T(8,128)}) conditional(s32[]{:T(128)} %clamp.6, (s32[1]{0:T(128)}, f32[8,5,40,128]{3,2,1,0:T(8,128)S(1)}, f32[8,5,40,128]{3,2,1,0:T(8,128)S(1)}, ...), branch_computations={%region_1.0_spmd, %region_2.0_spmd, %region_3.0_spmd, %region_4.0_... | conditional | flops 8000000 | bytes 3655560 | solution.py:453
  32.4 5.8 %collective-permute-start.5 = (f32[5,24,128]{2,1,0:T(8,128)S(1)}, f32[5,24,128]{2,1,0:T(8,128)}, u32[]{:S(2)}, u32[]{:S(2)}) collective-permute-start(f32[5,24,128]{2,1,0:T(8,128)S(1)} %get-tuple-element.491), channel_id=1, source_target_pairs={{258,0},{0,258},{259,1},{1,259},{260,2},{2,260},{261,3},{3,261},{2... | collective-permute-start | bytes 184328 | tf_op jit(solution)/shard_map/while/body/eval_jaxpr/cond/branch_1_fun/ppermute | solution.py:440
  38.3 1.9 %collective-permute-start.4 = (f32[5,24,128]{2,1,0:T(8,128)S(1)}, f32[5,24,128]{2,1,0:T(8,128)}, u32[]{:S(2)}, u32[]{:S(2)}) collective-permute-start(f32[5,24,128]{2,1,0:T(8,128)S(1)} %get-tuple-element.491), channel_id=1, source_target_pairs={{257,0},{0,257},{258,1},{1,258},{259,2},{2,259},{260,3},{3,260},{2... | collective-permute-start | bytes 184328 | tf_op jit(solution)/shard_map/while/body/eval_jaxpr/cond/branch_1_fun/ppermute | solution.py:439
  40.2 2.8 %collective-permute-start.6 = (f32[40,128]{1,0:T(8,128)S(1)}, f32[40,128]{1,0:T(8,128)}, u32[]{:S(2)}, u32[]{:S(2)}) collective-permute-start(f32[40,128]{1,0:T(8,128)S(1)} %get-tuple-element.492), channel_id=1, source_target_pairs={{0,32},{1,33},{2,34},{3,35},{4,36},{5,37},{6,38},{7,39},{8,40},{9,... | collective-permute-start | bytes 61448 | tf_op jit(solution)/shard_map/while/body/eval_jaxpr/cond/branch_1_fun/ppermute | solution.py:441
  43.0 1.3 %collective-permute-start.7 = (f32[40,128]{1,0:T(8,128)S(1)}, f32[40,128]{1,0:T(8,128)}, u32[]{:S(2)}, u32[]{:S(2)}) collective-permute-start(f32[40,128]{1,0:T(8,128)S(1)} %get-tuple-element.493), channel_id=1, source_target_pairs={{32,64},{33,65},{34,66},{35,67},{36,68},{37,69},{38,70},{39,71},{4... | collective-permute-start | bytes 61448 | tf_op jit(solution)/shard_map/while/body/eval_jaxpr/cond/branch_1_fun/ppermute | solution.py:442
  44.2 2.3 %branch_1_fun.1 = f32[8,5,40,128]{3,2,1,0:T(8,128)S(1)} custom-call(s32[1]{0:T(128)} %get-tuple-element.488.code_ref, f32[8,5,40,128]{3,2,1,0:T(8,128)S(1)} %get-tuple-element.489.old_ref, f32[8,5,40,128]{3,2,1,0:T(8,128)S(1)} %get-tuple-element.490.now_ref), custom_call_target="tpu_custom_call" | custom-call | flops 8000000 | bytes 3000000 | tf_op jit(solution)/shard_map/while/body/eval_jaxpr/cond/branch_1_fun/pallas_call | solution.py:443
  46.5 0.0 collective-permute-done.6
  46.5 0.0 collective-permute-done.7
  46.6 0.0 collective-permute-done.5
  46.6 0.0 collective-permute-done.4
  46.6 1.9 %eval_jaxpr.3 = (f32[8,5,40,128]{3,2,1,0:T(8,128)S(1)}, f32[5,24,128]{2,1,0:T(8,128)S(1)}, f32[40,128]{1,0:T(8,128)S(1)}, f32[40,128]{1,0:T(8,128)S(1)}) custom-call(s32[1]{0:T(128)} %bitcast.10.code_ref, s32[1]{0:T(128)} %bitcast.11.offsets_ref, f32[8,5,40,128]{3,2,1,0:T(8,128)S(1)} %get-tuple-element.783.base_ref, ...), custom_call_target="tpu_custom_call" | custom-call | flops 8000000 | bytes 3000000 | tf_op jit(solution)/shard_map/while/body/eval_jaxpr/pallas_call | solution.py:456
  48.5 27.5 %conditional.2 = (f32[8,5,40,128]{3,2,1,0:T(8,128)S(1)}, f32[5,24,128]{2,1,0:T(8,128)}, f32[5,24,128]{2,1,0:T(8,128)}, f32[40,128]{1,0:T(8,128)}, f32[40,128]{1,0:T(8,128)}) conditional(s32[]{:T(128)} %clamp.6, (s32[1]{0:T(128)}, f32[8,5,40,128]{3,2,1,0:T(8,128)S(1)}, f32[8,5,40,128]{3,2,1,0:T(8,128)S(1)}, ...), branch_computations={%region_1.0_spmd, %region_2.0_spmd, %region_3.0_spmd, %region_4.0_... | conditional | flops 8000000 | bytes 3655560 | solution.py:453
  48.6 12.1 %collective-permute-start.45 = (f32[5,24,128]{2,1,0:T(8,128)S(1)}, f32[5,24,128]{2,1,0:T(8,128)}, u32[]{:S(2)}, u32[]{:S(2)}) collective-permute-start(f32[5,24,128]{2,1,0:T(8,128)S(1)} %get-tuple-element.551), channel_id=1, source_target_pairs={{268,0},{0,268},{269,1},{1,269},{270,2},{2,270},{271,3},{3,271},{2... | collective-permute-start | bytes 184328 | tf_op jit(solution)/shard_map/while/body/eval_jaxpr/cond/branch_11_fun/ppermute | solution.py:440
  60.7 5.5 %collective-permute-start.44 = (f32[5,24,128]{2,1,0:T(8,128)S(1)}, f32[5,24,128]{2,1,0:T(8,128)}, u32[]{:S(2)}, u32[]{:S(2)}) collective-permute-start(f32[5,24,128]{2,1,0:T(8,128)S(1)} %get-tuple-element.551), channel_id=1, source_target_pairs={{267,0},{0,267},{268,1},{1,268},{269,2},{2,269},{270,3},{3,270},{2... | collective-permute-start | bytes 184328 | tf_op jit(solution)/shard_map/while/body/eval_jaxpr/cond/branch_11_fun/ppermute | solution.py:439
  66.2 6.2 %collective-permute-start.46 = (f32[40,128]{1,0:T(8,128)S(1)}, f32[40,128]{1,0:T(8,128)}, u32[]{:S(2)}, u32[]{:S(2)}) collective-permute-start(f32[40,128]{1,0:T(8,128)S(1)} %get-tuple-element.552), channel_id=1, source_target_pairs={{0,32},{1,33},{2,34},{3,35},{4,36},{5,37},{6,38},{7,39},{8,40},{9,... | collective-permute-start | bytes 61448 | tf_op jit(solution)/shard_map/while/body/eval_jaxpr/cond/branch_11_fun/ppermute | solution.py:441
  72.4 1.3 %collective-permute-start.47 = (f32[40,128]{1,0:T(8,128)S(1)}, f32[40,128]{1,0:T(8,128)}, u32[]{:S(2)}, u32[]{:S(2)}) collective-permute-start(f32[40,128]{1,0:T(8,128)S(1)} %get-tuple-element.553), channel_id=1, source_target_pairs={{32,64},{33,65},{34,66},{35,67},{36,68},{37,69},{38,70},{39,71},{4... | collective-permute-start | bytes 61448 | tf_op jit(solution)/shard_map/while/body/eval_jaxpr/cond/branch_11_fun/ppermute | solution.py:442
  73.6 2.3 %branch_11_fun.1 = f32[8,5,40,128]{3,2,1,0:T(8,128)S(1)} custom-call(s32[1]{0:T(128)} %get-tuple-element.548.code_ref, f32[8,5,40,128]{3,2,1,0:T(8,128)S(1)} %get-tuple-element.549.old_ref, f32[8,5,40,128]{3,2,1,0:T(8,128)S(1)} %get-tuple-element.550.now_ref), custom_call_target="tpu_custom_call" | custom-call | flops 8000000 | bytes 3000000 | tf_op jit(solution)/shard_map/while/body/eval_jaxpr/cond/branch_11_fun/pallas_call | solution.py:443
  75.9 0.0 collective-permute-done.46
  75.9 0.0 collective-permute-done.47
  76.0 0.0 collective-permute-done.45
  76.0 0.0 collective-permute-done.44
  76.0 1.9 %eval_jaxpr.3 = (f32[8,5,40,128]{3,2,1,0:T(8,128)S(1)}, f32[5,24,128]{2,1,0:T(8,128)S(1)}, f32[40,128]{1,0:T(8,128)S(1)}, f32[40,128]{1,0:T(8,128)S(1)}) custom-call(s32[1]{0:T(128)} %bitcast.10.code_ref, s32[1]{0:T(128)} %bitcast.11.offsets_ref, f32[8,5,40,128]{3,2,1,0:T(8,128)S(1)} %get-tuple-element.783.base_ref, ...), custom_call_target="tpu_custom_call" | custom-call | flops 8000000 | bytes 3000000 | tf_op jit(solution)/shard_map/while/body/eval_jaxpr/pallas_call | solution.py:456
  77.9 25.0 %conditional.2 = (f32[8,5,40,128]{3,2,1,0:T(8,128)S(1)}, f32[5,24,128]{2,1,0:T(8,128)}, f32[5,24,128]{2,1,0:T(8,128)}, f32[40,128]{1,0:T(8,128)}, f32[40,128]{1,0:T(8,128)}) conditional(s32[]{:T(128)} %clamp.6, (s32[1]{0:T(128)}, f32[8,5,40,128]{3,2,1,0:T(8,128)S(1)}, f32[8,5,40,128]{3,2,1,0:T(8,128)S(1)}, ...), branch_computations={%region_1.0_spmd, %region_2.0_spmd, %region_3.0_spmd, %region_4.0_... | conditional | flops 8000000 | bytes 3655560 | solution.py:453
  78.0 7.4 %collective-permute-start.105 = (f32[5,24,128]{2,1,0:T(8,128)S(1)}, f32[5,24,128]{2,1,0:T(8,128)}, u32[]{:S(2)}, u32[]{:S(2)}) collective-permute-start(f32[5,24,128]{2,1,0:T(8,128)S(1)} %get-tuple-element.641), channel_id=1, source_target_pairs={{283,0},{0,283},{284,1},{1,284},{285,2},{2,285},{286,3},{3,286},{2... | collective-permute-start | bytes 184328 | tf_op jit(solution)/shard_map/while/body/eval_jaxpr/cond/branch_26_fun/ppermute | solution.py:440
  85.4 8.9 %collective-permute-start.104 = (f32[5,24,128]{2,1,0:T(8,128)S(1)}, f32[5,24,128]{2,1,0:T(8,128)}, u32[]{:S(2)}, u32[]{:S(2)}) collective-permute-start(f32[5,24,128]{2,1,0:T(8,128)S(1)} %get-tuple-element.641), channel_id=1, source_target_pairs={{282,0},{0,282},{283,1},{1,283},{284,2},{2,284},{285,3},{3,285},{2... | collective-permute-start | bytes 184328 | tf_op jit(solution)/shard_map/while/body/eval_jaxpr/cond/branch_26_fun/ppermute | solution.py:439
  94.3 5.0 %collective-permute-start.106 = (f32[40,128]{1,0:T(8,128)S(1)}, f32[40,128]{1,0:T(8,128)}, u32[]{:S(2)}, u32[]{:S(2)}) collective-permute-start(f32[40,128]{1,0:T(8,128)S(1)} %get-tuple-element.642), channel_id=1, source_target_pairs={{0,32},{1,33},{2,34},{3,35},{4,36},{5,37},{6,38},{7,39},{8,40},{9,... | collective-permute-start | bytes 61448 | tf_op jit(solution)/shard_map/while/body/eval_jaxpr/cond/branch_26_fun/ppermute | solution.py:441
  99.3 1.3 %collective-permute-start.107 = (f32[40,128]{1,0:T(8,128)S(1)}, f32[40,128]{1,0:T(8,128)}, u32[]{:S(2)}, u32[]{:S(2)}) collective-permute-start(f32[40,128]{1,0:T(8,128)S(1)} %get-tuple-element.643), channel_id=1, source_target_pairs={{32,64},{33,65},{34,66},{35,67},{36,68},{37,69},{38,70},{39,71},{4... | collective-permute-start | bytes 61448 | tf_op jit(solution)/shard_map/while/body/eval_jaxpr/cond/branch_26_fun/ppermute | solution.py:442
  100.6 2.3 %branch_26_fun.1 = f32[8,5,40,128]{3,2,1,0:T(8,128)S(1)} custom-call(s32[1]{0:T(128)} %get-tuple-element.638.code_ref, f32[8,5,40,128]{3,2,1,0:T(8,128)S(1)} %get-tuple-element.639.old_ref, f32[8,5,40,128]{3,2,1,0:T(8,128)S(1)} %get-tuple-element.640.now_ref), custom_call_target="tpu_custom_call" | custom-call | flops 8000000 | bytes 3000000 | tf_op jit(solution)/shard_map/while/body/eval_jaxpr/cond/branch_26_fun/pallas_call | solution.py:443
  102.9 0.0 collective-permute-done.106
  102.9 0.0 collective-permute-done.107
  102.9 0.0 collective-permute-done.105
  102.9 0.0 collective-permute-done.104
  102.9 1.9 %eval_jaxpr.3 = (f32[8,5,40,128]{3,2,1,0:T(8,128)S(1)}, f32[5,24,128]{2,1,0:T(8,128)S(1)}, f32[40,128]{1,0:T(8,128)S(1)}, f32[40,128]{1,0:T(8,128)S(1)}) custom-call(s32[1]{0:T(128)} %bitcast.10.code_ref, s32[1]{0:T(128)} %bitcast.11.offsets_ref, f32[8,5,40,128]{3,2,1,0:T(8,128)S(1)} %get-tuple-element.783.base_ref, ...), custom_call_target="tpu_custom_call" | custom-call | flops 8000000 | bytes 3000000 | tf_op jit(solution)/shard_map/while/body/eval_jaxpr/pallas_call | solution.py:456
  104.8 0.1 slice.15
  104.9 16.4 %all_to_all.10.in_ref = f32[8,5,32,128]{3,2,1,0:T(8,128)S(1)} all-to-all(f32[8,5,32,128]{3,2,1,0:T(8,128)S(1)} %slice.15), channel_id=1, replica_groups=mesh['row'=2,'ax'=8,'az'=32] {'ax'}, dimensions={0} | all-to-all | bytes 1310720 | tf_op jit(solution)/shard_map/all_to_all | solution.py:461
  121.3 1.1 shard_map.49
  (1 shorter events, 0.0 us)
Async XLA Ops:
  0.0 1.0 copy-start
  1.0 0.9 copy-start.1
  1.9 0.9 copy-start.2
  3.9 17.6 %all-to-all-start = ((f32[8,5,32,128]{3,2,1,0:T(8,128)}), f32[8,5,32,128]{3,2,1,0:T(8,128)S(1)}, u32[]{:S(2)}, u32[]{:S(2)}) async-start(f32[8,5,32,128]{3,2,1,0:T(8,128)} %shard_map.46), calls=%async_computation | async-start | bytes 1310720 | tf_op jit(solution)/shard_map/all_to_all | solution.py:423
  21.5 5.8 %collective-permute-start.128 = (f32[20,8,128]{2,1,0:T(8,128)S(1)}, f32[20,8,128]{2,1,0:T(8,128)S(1)}, u32[]{:S(2)}, u32[]{:S(2)}) collective-permute-start(f32[20,8,128]{2,1,0:T(8,128)S(1)} %get-tuple-element.699), channel_id=1, source_target_pairs={{257,0},{0,257},{258,1},{1,258},{259,2},{2,259},{260,3},{3,260},{2... | collective-permute-start | bytes 245768 | tf_op jit(solution)/shard_map/ppermute | solution.py:429
  23.4 5.8 %copy-start.3 = (s32[3]{0:T(128)S(1)}, s32[3]{0:T(128)}, u32[]{:S(2)}) copy-start(s32[3]{0:T(128)} %param.41) | copy-start | bytes 40
  23.4 8.3 %collective-permute-start.130 = (f32[20,8,128]{2,1,0:T(8,128)S(1)}, f32[20,8,128]{2,1,0:T(8,128)S(1)}, u32[]{:S(2)}, u32[]{:S(2)}) collective-permute-start(f32[20,8,128]{2,1,0:T(8,128)S(1)} %get-tuple-element.700), channel_id=1, source_target_pairs={{0,31},{1,0},{2,1},{3,2},{4,3},{5,4},{6,5},{7,6},{8,7},{9,8},{10,9... | collective-permute-start | bytes 245768 | tf_op jit(solution)/shard_map/ppermute | solution.py:430
  27.3 4.5 %collective-permute-start.129 = (f32[20,8,128]{2,1,0:T(8,128)S(1)}, f32[20,8,128]{2,1,0:T(8,128)S(1)}, u32[]{:S(2)}, u32[]{:S(2)}) collective-permute-start(f32[20,8,128]{2,1,0:T(8,128)S(1)} %collective-permute-done.128), channel_id=1, source_target_pairs={{256,0},{0,256},{257,1},{1,257},{258,2},{2,258},{259,3},{3,259},{2... | collective-permute-start | bytes 245768 | tf_op jit(solution)/shard_map/ppermute | solution.py:431
  32.4 14.1 %collective-permute-start.5 = (f32[5,24,128]{2,1,0:T(8,128)S(1)}, f32[5,24,128]{2,1,0:T(8,128)}, u32[]{:S(2)}, u32[]{:S(2)}) collective-permute-start(f32[5,24,128]{2,1,0:T(8,128)S(1)} %get-tuple-element.491), channel_id=1, source_target_pairs={{258,0},{0,258},{259,1},{1,259},{260,2},{2,260},{261,3},{3,261},{2... | collective-permute-start | bytes 184328 | tf_op jit(solution)/shard_map/while/body/eval_jaxpr/cond/branch_1_fun/ppermute | solution.py:440
  38.3 8.3 %collective-permute-start.4 = (f32[5,24,128]{2,1,0:T(8,128)S(1)}, f32[5,24,128]{2,1,0:T(8,128)}, u32[]{:S(2)}, u32[]{:S(2)}) collective-permute-start(f32[5,24,128]{2,1,0:T(8,128)S(1)} %get-tuple-element.491), channel_id=1, source_target_pairs={{257,0},{0,257},{258,1},{1,258},{259,2},{2,259},{260,3},{3,260},{2... | collective-permute-start | bytes 184328 | tf_op jit(solution)/shard_map/while/body/eval_jaxpr/cond/branch_1_fun/ppermute | solution.py:439
  40.2 6.4 %collective-permute-start.6 = (f32[40,128]{1,0:T(8,128)S(1)}, f32[40,128]{1,0:T(8,128)}, u32[]{:S(2)}, u32[]{:S(2)}) collective-permute-start(f32[40,128]{1,0:T(8,128)S(1)} %get-tuple-element.492), channel_id=1, source_target_pairs={{0,32},{1,33},{2,34},{3,35},{4,36},{5,37},{6,38},{7,39},{8,40},{9,... | collective-permute-start | bytes 61448 | tf_op jit(solution)/shard_map/while/body/eval_jaxpr/cond/branch_1_fun/ppermute | solution.py:441
  43.0 3.6 %collective-permute-start.7 = (f32[40,128]{1,0:T(8,128)S(1)}, f32[40,128]{1,0:T(8,128)}, u32[]{:S(2)}, u32[]{:S(2)}) collective-permute-start(f32[40,128]{1,0:T(8,128)S(1)} %get-tuple-element.493), channel_id=1, source_target_pairs={{32,64},{33,65},{34,66},{35,67},{36,68},{37,69},{38,70},{39,71},{4... | collective-permute-start | bytes 61448 | tf_op jit(solution)/shard_map/while/body/eval_jaxpr/cond/branch_1_fun/ppermute | solution.py:442
  48.6 27.4 %collective-permute-start.45 = (f32[5,24,128]{2,1,0:T(8,128)S(1)}, f32[5,24,128]{2,1,0:T(8,128)}, u32[]{:S(2)}, u32[]{:S(2)}) collective-permute-start(f32[5,24,128]{2,1,0:T(8,128)S(1)} %get-tuple-element.551), channel_id=1, source_target_pairs={{268,0},{0,268},{269,1},{1,269},{270,2},{2,270},{271,3},{3,271},{2... | collective-permute-start | bytes 184328 | tf_op jit(solution)/shard_map/while/body/eval_jaxpr/cond/branch_11_fun/ppermute | solution.py:440
  60.7 15.3 %collective-permute-start.44 = (f32[5,24,128]{2,1,0:T(8,128)S(1)}, f32[5,24,128]{2,1,0:T(8,128)}, u32[]{:S(2)}, u32[]{:S(2)}) collective-permute-start(f32[5,24,128]{2,1,0:T(8,128)S(1)} %get-tuple-element.551), channel_id=1, source_target_pairs={{267,0},{0,267},{268,1},{1,268},{269,2},{2,269},{270,3},{3,270},{2... | collective-permute-start | bytes 184328 | tf_op jit(solution)/shard_map/while/body/eval_jaxpr/cond/branch_11_fun/ppermute | solution.py:439
  66.2 9.8 %collective-permute-start.46 = (f32[40,128]{1,0:T(8,128)S(1)}, f32[40,128]{1,0:T(8,128)}, u32[]{:S(2)}, u32[]{:S(2)}) collective-permute-start(f32[40,128]{1,0:T(8,128)S(1)} %get-tuple-element.552), channel_id=1, source_target_pairs={{0,32},{1,33},{2,34},{3,35},{4,36},{5,37},{6,38},{7,39},{8,40},{9,... | collective-permute-start | bytes 61448 | tf_op jit(solution)/shard_map/while/body/eval_jaxpr/cond/branch_11_fun/ppermute | solution.py:441
  72.4 3.6 %collective-permute-start.47 = (f32[40,128]{1,0:T(8,128)S(1)}, f32[40,128]{1,0:T(8,128)}, u32[]{:S(2)}, u32[]{:S(2)}) collective-permute-start(f32[40,128]{1,0:T(8,128)S(1)} %get-tuple-element.553), channel_id=1, source_target_pairs={{32,64},{33,65},{34,66},{35,67},{36,68},{37,69},{38,70},{39,71},{4... | collective-permute-start | bytes 61448 | tf_op jit(solution)/shard_map/while/body/eval_jaxpr/cond/branch_11_fun/ppermute | solution.py:442
  78.0 24.9 %collective-permute-start.105 = (f32[5,24,128]{2,1,0:T(8,128)S(1)}, f32[5,24,128]{2,1,0:T(8,128)}, u32[]{:S(2)}, u32[]{:S(2)}) collective-permute-start(f32[5,24,128]{2,1,0:T(8,128)S(1)} %get-tuple-element.641), channel_id=1, source_target_pairs={{283,0},{0,283},{284,1},{1,284},{285,2},{2,285},{286,3},{3,286},{2... | collective-permute-start | bytes 184328 | tf_op jit(solution)/shard_map/while/body/eval_jaxpr/cond/branch_26_fun/ppermute | solution.py:440
  85.4 17.5 %collective-permute-start.104 = (f32[5,24,128]{2,1,0:T(8,128)S(1)}, f32[5,24,128]{2,1,0:T(8,128)}, u32[]{:S(2)}, u32[]{:S(2)}) collective-permute-start(f32[5,24,128]{2,1,0:T(8,128)S(1)} %get-tuple-element.641), channel_id=1, source_target_pairs={{282,0},{0,282},{283,1},{1,283},{284,2},{2,284},{285,3},{3,285},{2... | collective-permute-start | bytes 184328 | tf_op jit(solution)/shard_map/while/body/eval_jaxpr/cond/branch_26_fun/ppermute | solution.py:439
  94.3 8.6 %collective-permute-start.106 = (f32[40,128]{1,0:T(8,128)S(1)}, f32[40,128]{1,0:T(8,128)}, u32[]{:S(2)}, u32[]{:S(2)}) collective-permute-start(f32[40,128]{1,0:T(8,128)S(1)} %get-tuple-element.642), channel_id=1, source_target_pairs={{0,32},{1,33},{2,34},{3,35},{4,36},{5,37},{6,38},{7,39},{8,40},{9,... | collective-permute-start | bytes 61448 | tf_op jit(solution)/shard_map/while/body/eval_jaxpr/cond/branch_26_fun/ppermute | solution.py:441
  99.3 3.6 %collective-permute-start.107 = (f32[40,128]{1,0:T(8,128)S(1)}, f32[40,128]{1,0:T(8,128)}, u32[]{:S(2)}, u32[]{:S(2)}) collective-permute-start(f32[40,128]{1,0:T(8,128)S(1)} %get-tuple-element.643), channel_id=1, source_target_pairs={{32,64},{33,65},{34,66},{35,67},{36,68},{37,69},{38,70},{39,71},{4... | collective-permute-start | bytes 61448 | tf_op jit(solution)/shard_map/while/body/eval_jaxpr/cond/branch_26_fun/ppermute | solution.py:442

commit v4 on v3

--- a/solution.py
+++ b/solution.py
@@ -213,13 +213,12 @@
                 top.append(axial_terms(c)[0])
         one_ref[rows, :] = jnp.where(odd, packed_in, packed_out)
         two_ref[rows, :] = jnp.where(odd, packed_out, packed_in)
-    half = up_ref.shape[1] // SUB
-    for b in range(half):
-        for k in range(FIELDS):
-            value = pltpu.roll(top[b][k], HALF, 1)
-            if b + half < blocks:
-                value = jnp.where(lane < HALF, value, top[b + half][k])
-            up_ref[k, pl.ds(b * SUB, SUB), :] = value
+    halves = [top[b][k] for k in range(FIELDS) for b in range(blocks)]
+    for h in range(up_ref.shape[0]):
+        value = pltpu.roll(halves[2 * h], HALF, 1)
+        if 2 * h + 1 < len(halves):
+            value = jnp.where(lane < HALF, value, halves[2 * h + 1])
+        up_ref[h] = value
 
 
 def first_kernel(cycle_cells, code_ref, in_ref, one_ref, two_ref, state_ref, *sends):
@@ -338,9 +337,11 @@
     at_low = jnp.where(place == 0, weight_r, 0.0)
     at_high = jnp.where(place == HALF - 1, weight_r, 0.0)
 
-    def opened(value):
-        both = jnp.concatenate([pltpu.roll(value, HALF, 1), value], axis=0)
-        return both[:rows_all]
+    def opened(ref, k):
+        halves = [divmod(k * blocks + b, 2) for b in range(blocks)]
+        return jnp.concatenate(
+            [ref[h] if odd_half else pltpu.roll(ref[h], HALF, 1) for h, odd_half in halves], axis=0
+        )
 
     for b in range(blocks):
         rows = pl.ds(b * SUB, SUB)
@@ -356,8 +357,8 @@
     for k in range(FIELDS):
         mixed = jnp.where(
             from_first,
-            pltpu.roll(opened(turn_ref[k]), shift, 0),
-            pltpu.roll(opened(turn2_ref[k]), shift2, 0),
+            pltpu.roll(opened(turn_ref, k), shift, 0),
+            pltpu.roll(opened(turn2_ref, k), shift2, 0),
         )
         turned = jnp.where(upper_half, mixed, 0.0)
         signed = -rate_w if k == 3 else rate_w
@@ -377,8 +378,8 @@
     block = struct(n_ax, FIELDS, tall, LANES)
     own = struct(n_ax, FIELDS, tile, LANES)
     outer_rows = struct(n_ax * FIELDS // 2, 2 * EDGE, LANES)
-    half_rows = -(-(tall // SUB) // 2) * SUB
-    sends = (struct(FIELDS, half_rows, LANES), struct(tall, LANES), struct(tall, LANES))
+    up_blocks = -(-FIELDS * (tall // SUB) // 2)
+    sends = (struct(up_blocks, SUB, LANES), struct(tall, LANES), struct(tall, LANES))
 
     def device(row, ax, az):
         return (row * n_ax + ax) * n_az + az
@@ -402,14 +403,14 @@
 
     near = [(device(r, x, z), device(r, x, (z + (1 if r else -1)) % n_az)) for r, x, z in every]
 
-    def call(kernel, outs, n_smem, n_vmem, scratch=()):
+    def call(kernel, outs, n_smem, n_vmem, scratch=(), grant=KERNEL_VMEM):
         return pl.pallas_call(
             kernel,
             out_shape=outs,
             in_specs=[smem] * n_smem + [vmem] * n_vmem,
             out_specs=jax.tree.map(lambda _: vmem, outs),
             scratch_shapes=list(scratch),
-            compiler_params=pltpu.CompilerParams(vmem_limit_bytes=KERNEL_VMEM),
+            compiler_params=pltpu.CompilerParams(vmem_limit_bytes=grant),
             cost_estimate=pl.CostEstimate(
                 flops=8_000_000, bytes_accessed=3_000_000, transcendentals=0
             ),
@@ -419,7 +420,7 @@
     taller = pltpu.VMEM((FIELDS, tall + SUB, LANES), jnp.float32)
     whole = pltpu.VMEM(block.shape, jnp.float32)
 
-    chunks = call(pack_kernel, own, 0, 3)(density[0], velocity[0], pressure[0])
+    chunks = call(pack_kernel, own, 0, 3, grant=None)(density[0], velocity[0], pressure[0])
     whole_tile = lax.all_to_all(chunks, "ax", 0, 0, tiled=True)
 
     code = 4 * ((1 - lax.axis_index("row")) * n_ax + lax.axis_index("ax"))

time: 122 us -> 125 us (1.025); the launches traced: 122 us -> 123 us
  waiting for transfers between devices: 13 us -> 18.3 us
  local copies, waits for them, and re-layouts: 3.6 us -> 0.75 us
  starting transfers between devices: 71.7 us -> 69.1 us
    ppermute x3, starting transfers between devices: 25.4 us -> 19.1 us  [run(): turn2 = lax.ppermute(up, AXES, turned((by + 1) % n_az))]
    ppermute x3, waiting for transfers between devices: 0.01 us -> 5.29 us  [run(): turn1 = lax.ppermute(up, AXES, turned(by))]
    ppermute x3, starting transfers between devices: 16.3 us -> 20 us  [run(): turn1 = lax.ppermute(up, AXES, turned(by))]
    unnamed x9 -> x3, local copies, waits for them, and re-layouts: 2.86 us -> 0.06 us
  transfers between devices with their start and end apart: 16 -> 16, of which waited for: 2 -> 3; matrix products, arithmetic and copies ran while one was open for 1% -> 0% of each run, Pallas kernels for 6% -> 6%
where the time goes in v4:
time: 125 us; the launch traced here: 123 us
  starting transfers between devices  69.1 us (55%)
  waiting for transfers between devices  18.3 us (15%)
  blocking collectives  16.3 us (13%)
  Pallas kernels  16.2 us (13%)
  between operations  1.88 us (2%)
    ppermute x3, starting transfers between devices, run(): turn1 = lax.ppermute(up, AXES, turned(by))  20 us
    ppermute x3, starting transfers between devices, run(): turn2 = lax.ppermute(up, AXES, turned((by + 1) % n_az))  19.1 us
    all_to_all x1, blocking collectives, body(): lax.all_to_all(carry[0][:, :, EDGE:EDGE + tile], 'ax', 0, 0, tiled=True)  16.3 us
    ppermute x3, starting transfers between devices, run(): one = lax.ppermute(one, AXES, swapped(0))  13.9 us
    all_to_all x1, waiting for transfers between devices, body(): whole_tile = lax.all_to_all(chunks, 'ax', 0, 0, tiled=True)  11.5 us
    pallas_call x3, Pallas kernels, run(): call(kernel_of(local_kernel), block, 1, 2, (taller, taller, whole, whole))  6.93 us
    all_to_all x1, starting transfers between devices, body(): whole_tile = lax.all_to_all(chunks, 'ax', 0, 0, tiled=True)  6.11 us
    pallas_call x3, Pallas kernels, substep(): call(kernel_of(join_kernel), (block, *sends), 2, 5)(code_1, left, *terms)  5.5 us
  transfers between devices with their start and end apart: 16, of which 3 were waited for; matrix products, arithmetic and copies ran while one was open for 0% of the time, Pallas kernels for 6%

profile of v4, /device:TPU:16, one launch (start us, length us, event | category | flops | bytes accessed | tf_op | source)
XLA Modules:
  0.0 123.1 jit_solution(15364510351407619310)
XLA Ops:
  0.0 2.2 %shard_map.46 = f32[8,5,32,128]{3,2,1,0:T(8,128)} custom-call(f32[2,32,512]{2,1,0:T(8,128)} %bitcast.13, f32[3,2,32,512]{3,2,1,0:T(8,128)} %bitcast.12, f32[2,32,512]{2,1,0:T(8,128)} %bitcast.14), custom_call_target="tpu_custom_call" | custom-call | flops 8000000 | bytes 3000000 | tf_op jit(solution)/shard_map/pallas_call | solution.py:423
  2.2 6.1 %all-to-all-start = ((f32[8,5,32,128]{3,2,1,0:T(8,128)}), f32[8,5,32,128]{3,2,1,0:T(8,128)S(1)}, u32[]{:S(2)}, u32[]{:S(2)}) async-start(f32[8,5,32,128]{3,2,1,0:T(8,128)} %shard_map.46), calls=%async_computation | async-start | bytes 1310720 | tf_op jit(solution)/shard_map/all_to_all | solution.py:424
  8.3 11.5 %all-to-all-done.in_ref = f32[8,5,32,128]{3,2,1,0:T(8,128)S(1)} async-done(((f32[8,5,32,128]{3,2,1,0:T(8,128)}), f32[8,5,32,128]{3,2,1,0:T(8,128)S(1)}, u32[]{:S(2)}, u32[]{:S(2)}) %all-to-all-start) | async-done | bytes 655392 | tf_op jit(solution)/shard_map/all_to_all | solution.py:424
  19.8 1.9 %collective-permute-start.128 = (f32[20,8,128]{2,1,0:T(8,128)S(1)}, f32[20,8,128]{2,1,0:T(8,128)S(1)}, u32[]{:S(2)}, u32[]{:S(2)}) collective-permute-start(f32[20,8,128]{2,1,0:T(8,128)S(1)} %get-tuple-element.699), channel_id=1, source_target_pairs={{257,0},{0,257},{258,1},{1,258},{259,2},{2,259},{260,3},{3,260},{2... | collective-permute-start | bytes 245768 | tf_op jit(solution)/shard_map/ppermute | solution.py:430
  21.7 0.0 copy-start
  21.7 2.4 %collective-permute-start.130 = (f32[20,8,128]{2,1,0:T(8,128)S(1)}, f32[20,8,128]{2,1,0:T(8,128)S(1)}, u32[]{:S(2)}, u32[]{:S(2)}) collective-permute-start(f32[20,8,128]{2,1,0:T(8,128)S(1)} %get-tuple-element.700), channel_id=1, source_target_pairs={{0,31},{1,0},{2,1},{3,2},{4,3},{5,4},{6,5},{7,6},{8,7},{9,8},{10,9... | collective-permute-start | bytes 245768 | tf_op jit(solution)/shard_map/ppermute | solution.py:431
  24.1 1.5 %collective-permute-done.128 = f32[20,8,128]{2,1,0:T(8,128)S(1)} collective-permute-done((f32[20,8,128]{2,1,0:T(8,128)S(1)}, f32[20,8,128]{2,1,0:T(8,128)S(1)}, u32[]{:S(2)}, u32[]{:S(2)}) %collective-permute-start.128) | collective-permute-done | bytes 81952 | tf_op jit(solution)/shard_map/ppermute | solution.py:430
  25.5 1.9 %collective-permute-start.129 = (f32[20,8,128]{2,1,0:T(8,128)S(1)}, f32[20,8,128]{2,1,0:T(8,128)S(1)}, u32[]{:S(2)}, u32[]{:S(2)}) collective-permute-start(f32[20,8,128]{2,1,0:T(8,128)S(1)} %collective-permute-done.128), channel_id=1, source_target_pairs={{256,0},{0,256},{257,1},{1,257},{258,2},{2,258},{259,3},{3,259},{2... | collective-permute-start | bytes 245768 | tf_op jit(solution)/shard_map/ppermute | solution.py:432
  27.5 0.0 copy-done
  27.5 0.6 fusion
  29.9 0.0 collective-permute-done.130.two_ref
  29.9 0.0 collective-permute-done.129.one_ref
  29.9 0.5 shard_map.48
  30.4 0.1 copy.166
  30.5 75.1 %while.20 = (s32[]{:T(128)}, f32[8,5,40,128]{3,2,1,0:T(8,128)S(1)}, f32[13,8,128]{2,1,0:T(8,128)S(1)}, f32[40,128]{1,0:T(8,128)S(1)}, f32[40,128]{1,0:T(8,128)S(...) while((s32[]{:T(128)}, f32[8,5,40,128]{3,2,1,0:T(8,128)S(1)}, ...), condition=%wide.region_33.0_spmd, body=%wide.region_0.0_spmd.sunk | while | flops 16000019 | bytes 6590408 | solution.py:461
  30.5 27.1 %conditional.2 = (f32[8,5,40,128]{3,2,1,0:T(8,128)S(1)}, f32[13,8,128]{2,1,0:T(8,128)}, f32[13,8,128]{2,1,0:T(8,128)}, f32[40,128]{1,0:T(8,128)}, f32[40,128]{1,0:T(8,128)}) conditional(s32[]{:T(128)} %clamp.6, (s32[1]{0:T(128)}, f32[8,5,40,128]{3,2,1,0:T(8,128)S(1)}, f32[8,5,40,128]{3,2,1,0:T(8,128)S(1)}, ...), branch_computations={%region_1.0_spmd, %region_2.0_spmd, %region_3.0_spmd, %region_4.0_... | conditional | flops 8000000 | bytes 3590024 | solution.py:454
  30.6 13.5 %collective-permute-start.73 = (f32[13,8,128]{2,1,0:T(8,128)S(1)}, f32[13,8,128]{2,1,0:T(8,128)}, u32[]{:S(2)}, u32[]{:S(2)}) collective-permute-start(f32[13,8,128]{2,1,0:T(8,128)S(1)} %get-tuple-element.593), channel_id=1, source_target_pairs={{275,0},{0,275},{276,1},{1,276},{277,2},{2,277},{278,3},{3,278},{2... | collective-permute-start | bytes 159752 | tf_op jit(solution)/shard_map/while/body/eval_jaxpr/cond/branch_18_fun/ppermute | solution.py:441
  44.1 1.9 %collective-permute-start.72 = (f32[13,8,128]{2,1,0:T(8,128)S(1)}, f32[13,8,128]{2,1,0:T(8,128)}, u32[]{:S(2)}, u32[]{:S(2)}) collective-permute-start(f32[13,8,128]{2,1,0:T(8,128)S(1)} %get-tuple-element.593), channel_id=1, source_target_pairs={{274,0},{0,274},{275,1},{1,275},{276,2},{2,276},{277,3},{3,277},{2... | collective-permute-start | bytes 159752 | tf_op jit(solution)/shard_map/while/body/eval_jaxpr/cond/branch_18_fun/ppermute | solution.py:440
  46.0 2.8 %collective-permute-start.74 = (f32[40,128]{1,0:T(8,128)S(1)}, f32[40,128]{1,0:T(8,128)}, u32[]{:S(2)}, u32[]{:S(2)}) collective-permute-start(f32[40,128]{1,0:T(8,128)S(1)} %get-tuple-element.594), channel_id=1, source_target_pairs={{0,32},{1,33},{2,34},{3,35},{4,36},{5,37},{6,38},{7,39},{8,40},{9,... | collective-permute-start | bytes 61448 | tf_op jit(solution)/shard_map/while/body/eval_jaxpr/cond/branch_18_fun/ppermute | solution.py:442
  48.8 1.3 %collective-permute-start.75 = (f32[40,128]{1,0:T(8,128)S(1)}, f32[40,128]{1,0:T(8,128)}, u32[]{:S(2)}, u32[]{:S(2)}) collective-permute-start(f32[40,128]{1,0:T(8,128)S(1)} %get-tuple-element.595), channel_id=1, source_target_pairs={{32,64},{33,65},{34,66},{35,67},{36,68},{37,69},{38,70},{39,71},{4... | collective-permute-start | bytes 61448 | tf_op jit(solution)/shard_map/while/body/eval_jaxpr/cond/branch_18_fun/ppermute | solution.py:443
  50.0 2.3 %branch_18_fun.1 = f32[8,5,40,128]{3,2,1,0:T(8,128)S(1)} custom-call(s32[1]{0:T(128)} %get-tuple-element.590.code_ref, f32[8,5,40,128]{3,2,1,0:T(8,128)S(1)} %get-tuple-element.591.old_ref, f32[8,5,40,128]{3,2,1,0:T(8,128)S(1)} %get-tuple-element.592.now_ref), custom_call_target="tpu_custom_call" | custom-call | flops 8000000 | bytes 3000000 | tf_op jit(solution)/shard_map/while/body/eval_jaxpr/cond/branch_18_fun/pallas_call | solution.py:444
  52.4 0.0 collective-permute-done.74
  52.4 0.0 collective-permute-done.75
  52.4 0.0 collective-permute-done.73
  52.4 5.3 %collective-permute-done.72 = f32[13,8,128]{2,1,0:T(8,128)} collective-permute-done((f32[13,8,128]{2,1,0:T(8,128)S(1)}, f32[13,8,128]{2,1,0:T(8,128)}, u32[]{:S(2)}, u32[]{:S(2)}) %collective-permute-start.72) | collective-permute-done | bytes 53280 | tf_op jit(solution)/shard_map/while/body/eval_jaxpr/cond/branch_18_fun/ppermute | solution.py:440
  57.7 1.8 %eval_jaxpr.3 = (f32[8,5,40,128]{3,2,1,0:T(8,128)S(1)}, f32[13,8,128]{2,1,0:T(8,128)S(1)}, f32[40,128]{1,0:T(8,128)S(1)}, f32[40,128]{1,0:T(8,128)S(1)}) custom-call(s32[1]{0:T(128)} %bitcast.10.code_ref, s32[1]{0:T(128)} %bitcast.11.offsets_ref, f32[8,5,40,128]{3,2,1,0:T(8,128)S(1)} %get-tuple-element.783.base_ref, ...), custom_call_target="tpu_custom_call" | custom-call | flops 8000000 | bytes 3000000 | tf_op jit(solution)/shard_map/while/body/eval_jaxpr/pallas_call | solution.py:457
  59.6 17.6 %conditional.2 = (f32[8,5,40,128]{3,2,1,0:T(8,128)S(1)}, f32[13,8,128]{2,1,0:T(8,128)}, f32[13,8,128]{2,1,0:T(8,128)}, f32[40,128]{1,0:T(8,128)}, f32[40,128]{1,0:T(8,128)}) conditional(s32[]{:T(128)} %clamp.6, (s32[1]{0:T(128)}, f32[8,5,40,128]{3,2,1,0:T(8,128)S(1)}, f32[8,5,40,128]{3,2,1,0:T(8,128)S(1)}, ...), branch_computations={%region_1.0_spmd, %region_2.0_spmd, %region_3.0_spmd, %region_4.0_... | conditional | flops 8000000 | bytes 3590024 | solution.py:454
  59.6 3.7 %collective-permute-start.97 = (f32[13,8,128]{2,1,0:T(8,128)S(1)}, f32[13,8,128]{2,1,0:T(8,128)}, u32[]{:S(2)}, u32[]{:S(2)}) collective-permute-start(f32[13,8,128]{2,1,0:T(8,128)S(1)} %get-tuple-element.629), channel_id=1, source_target_pairs={{281,0},{0,281},{282,1},{1,282},{283,2},{2,283},{284,3},{3,284},{2... | collective-permute-start | bytes 159752 | tf_op jit(solution)/shard_map/while/body/eval_jaxpr/cond/branch_24_fun/ppermute | solution.py:441
  63.3 4.0 %collective-permute-start.96 = (f32[13,8,128]{2,1,0:T(8,128)S(1)}, f32[13,8,128]{2,1,0:T(8,128)}, u32[]{:S(2)}, u32[]{:S(2)}) collective-permute-start(f32[13,8,128]{2,1,0:T(8,128)S(1)} %get-tuple-element.629), channel_id=1, source_target_pairs={{280,0},{0,280},{281,1},{1,281},{282,2},{2,282},{283,3},{3,283},{2... | collective-permute-start | bytes 159752 | tf_op jit(solution)/shard_map/while/body/eval_jaxpr/cond/branch_24_fun/ppermute | solution.py:440
  67.3 6.2 %collective-permute-start.98 = (f32[40,128]{1,0:T(8,128)S(1)}, f32[40,128]{1,0:T(8,128)}, u32[]{:S(2)}, u32[]{:S(2)}) collective-permute-start(f32[40,128]{1,0:T(8,128)S(1)} %get-tuple-element.630), channel_id=1, source_target_pairs={{0,32},{1,33},{2,34},{3,35},{4,36},{5,37},{6,38},{7,39},{8,40},{9,... | collective-permute-start | bytes 61448 | tf_op jit(solution)/shard_map/while/body/eval_jaxpr/cond/branch_24_fun/ppermute | solution.py:442
  73.5 1.3 %collective-permute-start.99 = (f32[40,128]{1,0:T(8,128)S(1)}, f32[40,128]{1,0:T(8,128)}, u32[]{:S(2)}, u32[]{:S(2)}) collective-permute-start(f32[40,128]{1,0:T(8,128)S(1)} %get-tuple-element.631), channel_id=1, source_target_pairs={{32,64},{33,65},{34,66},{35,67},{36,68},{37,69},{38,70},{39,71},{4... | collective-permute-start | bytes 61448 | tf_op jit(solution)/shard_map/while/body/eval_jaxpr/cond/branch_24_fun/ppermute | solution.py:443
  74.8 2.3 %branch_24_fun.1 = f32[8,5,40,128]{3,2,1,0:T(8,128)S(1)} custom-call(s32[1]{0:T(128)} %get-tuple-element.626.code_ref, f32[8,5,40,128]{3,2,1,0:T(8,128)S(1)} %get-tuple-element.627.old_ref, f32[8,5,40,128]{3,2,1,0:T(8,128)S(1)} %get-tuple-element.628.now_ref), custom_call_target="tpu_custom_call" | custom-call | flops 8000000 | bytes 3000000 | tf_op jit(solution)/shard_map/while/body/eval_jaxpr/cond/branch_24_fun/pallas_call | solution.py:444
  77.1 0.0 collective-permute-done.98
  77.1 0.0 collective-permute-done.99
  77.1 0.0 collective-permute-done.97
  77.1 0.0 collective-permute-done.96
  77.1 1.8 %eval_jaxpr.3 = (f32[8,5,40,128]{3,2,1,0:T(8,128)S(1)}, f32[13,8,128]{2,1,0:T(8,128)S(1)}, f32[40,128]{1,0:T(8,128)S(1)}, f32[40,128]{1,0:T(8,128)S(1)}) custom-call(s32[1]{0:T(128)} %bitcast.10.code_ref, s32[1]{0:T(128)} %bitcast.11.offsets_ref, f32[8,5,40,128]{3,2,1,0:T(8,128)S(1)} %get-tuple-element.783.base_ref, ...), custom_call_target="tpu_custom_call" | custom-call | flops 8000000 | bytes 3000000 | tf_op jit(solution)/shard_map/while/body/eval_jaxpr/pallas_call | solution.py:457
  79.0 24.7 %conditional.2 = (f32[8,5,40,128]{3,2,1,0:T(8,128)S(1)}, f32[13,8,128]{2,1,0:T(8,128)}, f32[13,8,128]{2,1,0:T(8,128)}, f32[40,128]{1,0:T(8,128)}, f32[40,128]{1,0:T(8,128)}) conditional(s32[]{:T(128)} %clamp.6, (s32[1]{0:T(128)}, f32[8,5,40,128]{3,2,1,0:T(8,128)S(1)}, f32[8,5,40,128]{3,2,1,0:T(8,128)S(1)}, ...), branch_computations={%region_1.0_spmd, %region_2.0_spmd, %region_3.0_spmd, %region_4.0_... | conditional | flops 8000000 | bytes 3590024 | solution.py:454
  79.1 1.9 %collective-permute-start.81 = (f32[13,8,128]{2,1,0:T(8,128)S(1)}, f32[13,8,128]{2,1,0:T(8,128)}, u32[]{:S(2)}, u32[]{:S(2)}) collective-permute-start(f32[13,8,128]{2,1,0:T(8,128)S(1)} %get-tuple-element.605), channel_id=1, source_target_pairs={{277,0},{0,277},{278,1},{1,278},{279,2},{2,279},{280,3},{3,280},{2... | collective-permute-start | bytes 159752 | tf_op jit(solution)/shard_map/while/body/eval_jaxpr/cond/branch_20_fun/ppermute | solution.py:441
  81.0 14.1 %collective-permute-start.80 = (f32[13,8,128]{2,1,0:T(8,128)S(1)}, f32[13,8,128]{2,1,0:T(8,128)}, u32[]{:S(2)}, u32[]{:S(2)}) collective-permute-start(f32[13,8,128]{2,1,0:T(8,128)S(1)} %get-tuple-element.605), channel_id=1, source_target_pairs={{276,0},{0,276},{277,1},{1,277},{278,2},{2,278},{279,3},{3,279},{2... | collective-permute-start | bytes 159752 | tf_op jit(solution)/shard_map/while/body/eval_jaxpr/cond/branch_20_fun/ppermute | solution.py:440
  95.1 4.9 %collective-permute-start.82 = (f32[40,128]{1,0:T(8,128)S(1)}, f32[40,128]{1,0:T(8,128)}, u32[]{:S(2)}, u32[]{:S(2)}) collective-permute-start(f32[40,128]{1,0:T(8,128)S(1)} %get-tuple-element.606), channel_id=1, source_target_pairs={{0,32},{1,33},{2,34},{3,35},{4,36},{5,37},{6,38},{7,39},{8,40},{9,... | collective-permute-start | bytes 61448 | tf_op jit(solution)/shard_map/while/body/eval_jaxpr/cond/branch_20_fun/ppermute | solution.py:442
  100.1 1.3 %collective-permute-start.83 = (f32[40,128]{1,0:T(8,128)S(1)}, f32[40,128]{1,0:T(8,128)}, u32[]{:S(2)}, u32[]{:S(2)}) collective-permute-start(f32[40,128]{1,0:T(8,128)S(1)} %get-tuple-element.607), channel_id=1, source_target_pairs={{32,64},{33,65},{34,66},{35,67},{36,68},{37,69},{38,70},{39,71},{4... | collective-permute-start | bytes 61448 | tf_op jit(solution)/shard_map/while/body/eval_jaxpr/cond/branch_20_fun/ppermute | solution.py:443
  101.4 2.3 %branch_20_fun.1 = f32[8,5,40,128]{3,2,1,0:T(8,128)S(1)} custom-call(s32[1]{0:T(128)} %get-tuple-element.602.code_ref, f32[8,5,40,128]{3,2,1,0:T(8,128)S(1)} %get-tuple-element.603.old_ref, f32[8,5,40,128]{3,2,1,0:T(8,128)S(1)} %get-tuple-element.604.now_ref), custom_call_target="tpu_custom_call" | custom-call | flops 8000000 | bytes 3000000 | tf_op jit(solution)/shard_map/while/body/eval_jaxpr/cond/branch_20_fun/pallas_call | solution.py:444
  103.7 0.0 collective-permute-done.82
  103.7 0.0 collective-permute-done.83
  103.7 0.0 collective-permute-done.81
  103.7 0.0 collective-permute-done.80
  103.7 1.8 %eval_jaxpr.3 = (f32[8,5,40,128]{3,2,1,0:T(8,128)S(1)}, f32[13,8,128]{2,1,0:T(8,128)S(1)}, f32[40,128]{1,0:T(8,128)S(1)}, f32[40,128]{1,0:T(8,128)S(1)}) custom-call(s32[1]{0:T(128)} %bitcast.10.code_ref, s32[1]{0:T(128)} %bitcast.11.offsets_ref, f32[8,5,40,128]{3,2,1,0:T(8,128)S(1)} %get-tuple-element.783.base_ref, ...), custom_call_target="tpu_custom_call" | custom-call | flops 8000000 | bytes 3000000 | tf_op jit(solution)/shard_map/while/body/eval_jaxpr/pallas_call | solution.py:457
  105.6 0.1 slice.15
  105.7 16.3 %all_to_all.10.in_ref = f32[8,5,32,128]{3,2,1,0:T(8,128)S(1)} all-to-all(f32[8,5,32,128]{3,2,1,0:T(8,128)S(1)} %slice.15), channel_id=1, replica_groups=mesh['row'=2,'ax'=8,'az'=32] {'ax'}, dimensions={0} | all-to-all | bytes 1310720 | tf_op jit(solution)/shard_map/all_to_all | solution.py:462
  122.0 1.1 shard_map.49
  (1 shorter events, 0.0 us)
Async XLA Ops:
  2.2 17.6 %all-to-all-start = ((f32[8,5,32,128]{3,2,1,0:T(8,128)}), f32[8,5,32,128]{3,2,1,0:T(8,128)S(1)}, u32[]{:S(2)}, u32[]{:S(2)}) async-start(f32[8,5,32,128]{3,2,1,0:T(8,128)} %shard_map.46), calls=%async_computation | async-start | bytes 1310720 | tf_op jit(solution)/shard_map/all_to_all | solution.py:424
  19.8 5.8 %collective-permute-start.128 = (f32[20,8,128]{2,1,0:T(8,128)S(1)}, f32[20,8,128]{2,1,0:T(8,128)S(1)}, u32[]{:S(2)}, u32[]{:S(2)}) collective-permute-start(f32[20,8,128]{2,1,0:T(8,128)S(1)} %get-tuple-element.699), channel_id=1, source_target_pairs={{257,0},{0,257},{258,1},{1,258},{259,2},{2,259},{260,3},{3,260},{2... | collective-permute-start | bytes 245768 | tf_op jit(solution)/shard_map/ppermute | solution.py:430
  21.7 5.8 %copy-start = (s32[3]{0:T(128)S(1)}, s32[3]{0:T(128)}, u32[]{:S(2)}) copy-start(s32[3]{0:T(128)} %param.41) | copy-start | bytes 40
  21.7 8.2 %collective-permute-start.130 = (f32[20,8,128]{2,1,0:T(8,128)S(1)}, f32[20,8,128]{2,1,0:T(8,128)S(1)}, u32[]{:S(2)}, u32[]{:S(2)}) collective-permute-start(f32[20,8,128]{2,1,0:T(8,128)S(1)} %get-tuple-element.700), channel_id=1, source_target_pairs={{0,31},{1,0},{2,1},{3,2},{4,3},{5,4},{6,5},{7,6},{8,7},{9,8},{10,9... | collective-permute-start | bytes 245768 | tf_op jit(solution)/shard_map/ppermute | solution.py:431
  25.5 4.3 %collective-permute-start.129 = (f32[20,8,128]{2,1,0:T(8,128)S(1)}, f32[20,8,128]{2,1,0:T(8,128)S(1)}, u32[]{:S(2)}, u32[]{:S(2)}) collective-permute-start(f32[20,8,128]{2,1,0:T(8,128)S(1)} %collective-permute-done.128), channel_id=1, source_target_pairs={{256,0},{0,256},{257,1},{1,257},{258,2},{2,258},{259,3},{3,259},{2... | collective-permute-start | bytes 245768 | tf_op jit(solution)/shard_map/ppermute | solution.py:432
  30.6 21.8 %collective-permute-start.73 = (f32[13,8,128]{2,1,0:T(8,128)S(1)}, f32[13,8,128]{2,1,0:T(8,128)}, u32[]{:S(2)}, u32[]{:S(2)}) collective-permute-start(f32[13,8,128]{2,1,0:T(8,128)S(1)} %get-tuple-element.593), channel_id=1, source_target_pairs={{275,0},{0,275},{276,1},{1,276},{277,2},{2,277},{278,3},{3,278},{2... | collective-permute-start | bytes 159752 | tf_op jit(solution)/shard_map/while/body/eval_jaxpr/cond/branch_18_fun/ppermute | solution.py:441
  44.1 13.6 %collective-permute-start.72 = (f32[13,8,128]{2,1,0:T(8,128)S(1)}, f32[13,8,128]{2,1,0:T(8,128)}, u32[]{:S(2)}, u32[]{:S(2)}) collective-permute-start(f32[13,8,128]{2,1,0:T(8,128)S(1)} %get-tuple-element.593), channel_id=1, source_target_pairs={{274,0},{0,274},{275,1},{1,275},{276,2},{2,276},{277,3},{3,277},{2... | collective-permute-start | bytes 159752 | tf_op jit(solution)/shard_map/while/body/eval_jaxpr/cond/branch_18_fun/ppermute | solution.py:440
  46.0 6.4 %collective-permute-start.74 = (f32[40,128]{1,0:T(8,128)S(1)}, f32[40,128]{1,0:T(8,128)}, u32[]{:S(2)}, u32[]{:S(2)}) collective-permute-start(f32[40,128]{1,0:T(8,128)S(1)} %get-tuple-element.594), channel_id=1, source_target_pairs={{0,32},{1,33},{2,34},{3,35},{4,36},{5,37},{6,38},{7,39},{8,40},{9,... | collective-permute-start | bytes 61448 | tf_op jit(solution)/shard_map/while/body/eval_jaxpr/cond/branch_18_fun/ppermute | solution.py:442
  48.8 3.6 %collective-permute-start.75 = (f32[40,128]{1,0:T(8,128)S(1)}, f32[40,128]{1,0:T(8,128)}, u32[]{:S(2)}, u32[]{:S(2)}) collective-permute-start(f32[40,128]{1,0:T(8,128)S(1)} %get-tuple-element.595), channel_id=1, source_target_pairs={{32,64},{33,65},{34,66},{35,67},{36,68},{37,69},{38,70},{39,71},{4... | collective-permute-start | bytes 61448 | tf_op jit(solution)/shard_map/while/body/eval_jaxpr/cond/branch_18_fun/ppermute | solution.py:443
  59.6 17.5 %collective-permute-start.97 = (f32[13,8,128]{2,1,0:T(8,128)S(1)}, f32[13,8,128]{2,1,0:T(8,128)}, u32[]{:S(2)}, u32[]{:S(2)}) collective-permute-start(f32[13,8,128]{2,1,0:T(8,128)S(1)} %get-tuple-element.629), channel_id=1, source_target_pairs={{281,0},{0,281},{282,1},{1,282},{283,2},{2,283},{284,3},{3,284},{2... | collective-permute-start | bytes 159752 | tf_op jit(solution)/shard_map/while/body/eval_jaxpr/cond/branch_24_fun/ppermute | solution.py:441
  63.3 13.8 %collective-permute-start.96 = (f32[13,8,128]{2,1,0:T(8,128)S(1)}, f32[13,8,128]{2,1,0:T(8,128)}, u32[]{:S(2)}, u32[]{:S(2)}) collective-permute-start(f32[13,8,128]{2,1,0:T(8,128)S(1)} %get-tuple-element.629), channel_id=1, source_target_pairs={{280,0},{0,280},{281,1},{1,281},{282,2},{2,282},{283,3},{3,283},{2... | collective-permute-start | bytes 159752 | tf_op jit(solution)/shard_map/while/body/eval_jaxpr/cond/branch_24_fun/ppermute | solution.py:440
  67.3 9.8 %collective-permute-start.98 = (f32[40,128]{1,0:T(8,128)S(1)}, f32[40,128]{1,0:T(8,128)}, u32[]{:S(2)}, u32[]{:S(2)}) collective-permute-start(f32[40,128]{1,0:T(8,128)S(1)} %get-tuple-element.630), channel_id=1, source_target_pairs={{0,32},{1,33},{2,34},{3,35},{4,36},{5,37},{6,38},{7,39},{8,40},{9,... | collective-permute-start | bytes 61448 | tf_op jit(solution)/shard_map/while/body/eval_jaxpr/cond/branch_24_fun/ppermute | solution.py:442
  73.5 3.6 %collective-permute-start.99 = (f32[40,128]{1,0:T(8,128)S(1)}, f32[40,128]{1,0:T(8,128)}, u32[]{:S(2)}, u32[]{:S(2)}) collective-permute-start(f32[40,128]{1,0:T(8,128)S(1)} %get-tuple-element.631), channel_id=1, source_target_pairs={{32,64},{33,65},{34,66},{35,67},{36,68},{37,69},{38,70},{39,71},{4... | collective-permute-start | bytes 61448 | tf_op jit(solution)/shard_map/while/body/eval_jaxpr/cond/branch_24_fun/ppermute | solution.py:443
  79.1 24.6 %collective-permute-start.81 = (f32[13,8,128]{2,1,0:T(8,128)S(1)}, f32[13,8,128]{2,1,0:T(8,128)}, u32[]{:S(2)}, u32[]{:S(2)}) collective-permute-start(f32[13,8,128]{2,1,0:T(8,128)S(1)} %get-tuple-element.605), channel_id=1, source_target_pairs={{277,0},{0,277},{278,1},{1,278},{279,2},{2,279},{280,3},{3,280},{2... | collective-permute-start | bytes 159752 | tf_op jit(solution)/shard_map/while/body/eval_jaxpr/cond/branch_20_fun/ppermute | solution.py:441
  81.0 22.7 %collective-permute-start.80 = (f32[13,8,128]{2,1,0:T(8,128)S(1)}, f32[13,8,128]{2,1,0:T(8,128)}, u32[]{:S(2)}, u32[]{:S(2)}) collective-permute-start(f32[13,8,128]{2,1,0:T(8,128)S(1)} %get-tuple-element.605), channel_id=1, source_target_pairs={{276,0},{0,276},{277,1},{1,277},{278,2},{2,278},{279,3},{3,279},{2... | collective-permute-start | bytes 159752 | tf_op jit(solution)/shard_map/while/body/eval_jaxpr/cond/branch_20_fun/ppermute | solution.py:440
  95.1 8.5 %collective-permute-start.82 = (f32[40,128]{1,0:T(8,128)S(1)}, f32[40,128]{1,0:T(8,128)}, u32[]{:S(2)}, u32[]{:S(2)}) collective-permute-start(f32[40,128]{1,0:T(8,128)S(1)} %get-tuple-element.606), channel_id=1, source_target_pairs={{0,32},{1,33},{2,34},{3,35},{4,36},{5,37},{6,38},{7,39},{8,40},{9,... | collective-permute-start | bytes 61448 | tf_op jit(solution)/shard_map/while/body/eval_jaxpr/cond/branch_20_fun/ppermute | solution.py:442
  100.1 3.6 %collective-permute-start.83 = (f32[40,128]{1,0:T(8,128)S(1)}, f32[40,128]{1,0:T(8,128)}, u32[]{:S(2)}, u32[]{:S(2)}) collective-permute-start(f32[40,128]{1,0:T(8,128)S(1)} %get-tuple-element.607), channel_id=1, source_target_pairs={{32,64},{33,65},{34,66},{35,67},{36,68},{37,69},{38,70},{39,71},{4... | collective-permute-start | bytes 61448 | tf_op jit(solution)/shard_map/while/body/eval_jaxpr/cond/branch_20_fun/ppermute | solution.py:443

commit v5 on v4

--- a/solution.py
+++ b/solution.py
@@ -363,7 +363,8 @@
         turned = jnp.where(upper_half, mixed, 0.0)
         signed = -rate_w if k == 3 else rate_w
         state_ref[pairs - 1, k] = state_ref[pairs - 1, k] + signed * turned
-    write_sends(state_ref, co, segment, *sends)
+    if sends:
+        write_sends(state_ref, co, segment, *sends)
 
 
 def body(density, velocity, pressure, offsets):
@@ -454,7 +455,15 @@
         terms = lax.switch(
             index, [branch(by) for by in range(n_az)], code_1, *cells_and_edges
         )
-        state = call(kernel_of(join_kernel), (block, *sends), 2, 5)(code_1, left, *terms)
+
+        def usual(*operands):
+            return tuple(call(kernel_of(join_kernel), (block, *sends), 2, 5)(*operands))
+
+        def final(*operands):
+            state, = call(kernel_of(join_kernel), (block,), 2, 5)(*operands)
+            return (state, *cells_and_edges[1:])
+
+        state = lax.cond(lax.rem(code, 4) == 2, final, usual, code_1, left, *terms)
         return (*state, code + 1, lax.div(packed, cycle_cells))
 
     carry = (*carry, code, packed)

time: 125 us -> 124 us (level); the launches traced: 123 us -> 124 us
  Pallas kernels: 16.2 us -> 21.7 us
  waiting for transfers between devices: 18.3 us -> 13 us
  starting transfers between devices: 69.1 us -> 66.8 us
  local copies, waits for them, and re-layouts: 0.75 us -> 2.72 us
  blocking collectives: 16.3 us -> 18 us
    ppermute x3, waiting for transfers between devices: 5.29 us -> 0.01 us  [run(): turn1 = lax.ppermute(up, AXES, turned(by))]
    pallas_call x3, Pallas kernels: 6.93 us -> 10.4 us  [run(): call(kernel_of(local_kernel), block, 1, 2, (taller, taller, whole, whole))]
    ppermute x3, starting transfers between devices: 19.1 us -> 16.2 us  [run(): turn2 = lax.ppermute(up, AXES, turned((by + 1) % n_az))]
    ppermute x3, starting transfers between devices: 20 us -> 22.3 us  [run(): turn1 = lax.ppermute(up, AXES, turned(by))]
    pallas_call x3, Pallas kernels: 5.5 us -> 7.59 us  [the longest x2 5.31 us: usual(): return tuple(call(kernel_of(join_kernel), (block, *sends), 2, 5)(*operands))]
    all_to_all x1, blocking collectives: 16.3 us -> 18 us  [body(): lax.all_to_all(carry[0][:, :, EDGE:EDGE + tile], 'ax', 0, 0, tiled=True)]
    ppermute x3, starting transfers between devices: 13.9 us -> 12.3 us  [run(): one = lax.ppermute(one, AXES, swapped(0))]
  transfers between devices with their start and end apart: 16 -> 16, of which waited for: 3 -> 2; matrix products, arithmetic and copies ran while one was open for 0% -> 0% of each run, Pallas kernels for 6% -> 8%
where the time goes in v5:
time: 124 us
  starting transfers between devices  66.8 us (54%)
  Pallas kernels  21.7 us (18%)
  blocking collectives  18 us (15%)
  waiting for transfers between devices  13 us (10%)
  local copies, waits for them, and re-layouts  2.72 us (2%)
  between operations  1.89 us (2%)
    ppermute x3, starting transfers between devices, run(): turn1 = lax.ppermute(up, AXES, turned(by))  22.3 us
    all_to_all x1, blocking collectives, body(): lax.all_to_all(carry[0][:, :, EDGE:EDGE + tile], 'ax', 0, 0, tiled=True)  18 us
    ppermute x3, starting transfers between devices, run(): turn2 = lax.ppermute(up, AXES, turned((by + 1) % n_az))  16.2 us
    ppermute x3, starting transfers between devices, run(): one = lax.ppermute(one, AXES, swapped(0))  12.3 us
    all_to_all x1, waiting for transfers between devices, body(): whole_tile = lax.all_to_all(chunks, 'ax', 0, 0, tiled=True)  11.5 us
    pallas_call x3, Pallas kernels, run(): call(kernel_of(local_kernel), block, 1, 2, (taller, taller, whole, whole))  10.4 us
    all_to_all x1, starting transfers between devices, body(): whole_tile = lax.all_to_all(chunks, 'ax', 0, 0, tiled=True)  6.11 us
    pallas_call x2, Pallas kernels, usual(): return tuple(call(kernel_of(join_kernel), (block, *sends), 2, 5)(*operands))  5.31 us
  transfers between devices with their start and end apart: 16, of which 2 were waited for; matrix products, arithmetic and copies ran while one was open for 0% of the time, Pallas kernels for 8%

profile of v5, /device:TPU:16, one launch (start us, length us, event | category | flops | bytes accessed | tf_op | source)
XLA Modules:
  0.0 124.4 jit_solution(14089261070505435561)
XLA Ops:
  0.0 2.2 %shard_map.46 = f32[8,5,32,128]{3,2,1,0:T(8,128)} custom-call(f32[2,32,512]{2,1,0:T(8,128)} %bitcast.13, f32[3,2,32,512]{3,2,1,0:T(8,128)} %bitcast.12, f32[2,32,512]{2,1,0:T(8,128)} %bitcast.14), custom_call_target="tpu_custom_call" | custom-call | flops 8000000 | bytes 3000000 | tf_op jit(solution)/shard_map/pallas_call | solution.py:424
  2.2 6.1 %all-to-all-start = ((f32[8,5,32,128]{3,2,1,0:T(8,128)}), f32[8,5,32,128]{3,2,1,0:T(8,128)S(1)}, u32[]{:S(2)}, u32[]{:S(2)}) async-start(f32[8,5,32,128]{3,2,1,0:T(8,128)} %shard_map.46), calls=%async_computation | async-start | bytes 1310720 | tf_op jit(solution)/shard_map/all_to_all | solution.py:425
  8.3 11.5 %all-to-all-done.in_ref = f32[8,5,32,128]{3,2,1,0:T(8,128)S(1)} async-done(((f32[8,5,32,128]{3,2,1,0:T(8,128)}), f32[8,5,32,128]{3,2,1,0:T(8,128)S(1)}, u32[]{:S(2)}, u32[]{:S(2)}) %all-to-all-start) | async-done | bytes 655392 | tf_op jit(solution)/shard_map/all_to_all | solution.py:425
  19.8 1.9 %collective-permute-start.128 = (f32[20,8,128]{2,1,0:T(8,128)S(1)}, f32[20,8,128]{2,1,0:T(8,128)S(1)}, u32[]{:S(2)}, u32[]{:S(2)}) collective-permute-start(f32[20,8,128]{2,1,0:T(8,128)S(1)} %get-tuple-element.750), channel_id=1, source_target_pairs={{257,0},{0,257},{258,1},{1,258},{259,2},{2,259},{260,3},{3,260},{2... | collective-permute-start | bytes 245768 | tf_op jit(solution)/shard_map/ppermute | solution.py:431
  21.7 0.0 copy-start
  21.7 2.4 %collective-permute-start.130 = (f32[20,8,128]{2,1,0:T(8,128)S(1)}, f32[20,8,128]{2,1,0:T(8,128)S(1)}, u32[]{:S(2)}, u32[]{:S(2)}) collective-permute-start(f32[20,8,128]{2,1,0:T(8,128)S(1)} %get-tuple-element.751), channel_id=1, source_target_pairs={{0,31},{1,0},{2,1},{3,2},{4,3},{5,4},{6,5},{7,6},{8,7},{9,8},{10,9... | collective-permute-start | bytes 245768 | tf_op jit(solution)/shard_map/ppermute | solution.py:432
  24.1 1.5 %collective-permute-done.128 = f32[20,8,128]{2,1,0:T(8,128)S(1)} collective-permute-done((f32[20,8,128]{2,1,0:T(8,128)S(1)}, f32[20,8,128]{2,1,0:T(8,128)S(1)}, u32[]{:S(2)}, u32[]{:S(2)}) %collective-permute-start.128) | collective-permute-done | bytes 81952 | tf_op jit(solution)/shard_map/ppermute | solution.py:431
  25.5 1.9 %collective-permute-start.129 = (f32[20,8,128]{2,1,0:T(8,128)S(1)}, f32[20,8,128]{2,1,0:T(8,128)S(1)}, u32[]{:S(2)}, u32[]{:S(2)}) collective-permute-start(f32[20,8,128]{2,1,0:T(8,128)S(1)} %collective-permute-done.128), channel_id=1, source_target_pairs={{256,0},{0,256},{257,1},{1,257},{258,2},{2,258},{259,3},{3,259},{2... | collective-permute-start | bytes 245768 | tf_op jit(solution)/shard_map/ppermute | solution.py:433
  27.5 0.0 copy-done
  27.5 0.6 fusion
  29.9 0.0 collective-permute-done.130.two_ref
  29.9 0.0 collective-permute-done.129.one_ref
  29.9 0.5 shard_map.48
  30.4 0.9 copy.174
  31.3 72.8 %while.20 = (s32[]{:T(128)}, f32[8,5,40,128]{3,2,1,0:T(8,128)}, f32[13,8,128]{2,1,0:T(8,128)S(1)}, f32[40,128]{1,0:T(8,128)S(1)}, f32[40,128]{1,0:T(8,128)S(1)},...) while((s32[]{:T(128)}, f32[8,5,40,128]{3,2,1,0:T(8,128)}, ...), condition=%wide.region_35.0_spmd, body=%wide.region_0.0_spmd.sunk | while | flops 16000027 | bytes 6590677 | solution.py:470
  31.3 16.0 %conditional.4 = (f32[8,5,40,128]{3,2,1,0:T(8,128)S(1)}, f32[13,8,128]{2,1,0:T(8,128)}, f32[13,8,128]{2,1,0:T(8,128)}, f32[40,128]{1,0:T(8,128)}, f32[40,128]{1,0:T(8,128)}) conditional(s32[]{:T(128)} %clamp.6, (s32[1]{0:T(128)}, f32[8,5,40,128]{3,2,1,0:T(8,128)S(1)}, f32[8,5,40,128]{3,2,1,0:T(8,128)}, ...), branch_computations={%region_1.0_spmd, %region_2.0_spmd, %region_3.0_spmd, %region_4.0_... | conditional | flops 8000000 | bytes 3590024 | solution.py:455
  31.3 6.0 %collective-permute-start.13 = (f32[13,8,128]{2,1,0:T(8,128)S(1)}, f32[13,8,128]{2,1,0:T(8,128)}, u32[]{:S(2)}, u32[]{:S(2)}) collective-permute-start(f32[13,8,128]{2,1,0:T(8,128)S(1)} %get-tuple-element.537), channel_id=1, source_target_pairs={{260,0},{0,260},{261,1},{1,261},{262,2},{2,262},{263,3},{3,263},{2... | collective-permute-start | bytes 159752 | tf_op jit(solution)/shard_map/while/body/eval_jaxpr/cond/branch_3_fun/ppermute | solution.py:442
  37.4 2.4 %collective-permute-start.12 = (f32[13,8,128]{2,1,0:T(8,128)S(1)}, f32[13,8,128]{2,1,0:T(8,128)}, u32[]{:S(2)}, u32[]{:S(2)}) collective-permute-start(f32[13,8,128]{2,1,0:T(8,128)S(1)} %get-tuple-element.537), channel_id=1, source_target_pairs={{259,0},{0,259},{260,1},{1,260},{261,2},{2,261},{262,3},{3,262},{2... | collective-permute-start | bytes 159752 | tf_op jit(solution)/shard_map/while/body/eval_jaxpr/cond/branch_3_fun/ppermute | solution.py:441
  39.8 2.8 %collective-permute-start.14 = (f32[40,128]{1,0:T(8,128)S(1)}, f32[40,128]{1,0:T(8,128)}, u32[]{:S(2)}, u32[]{:S(2)}) collective-permute-start(f32[40,128]{1,0:T(8,128)S(1)} %get-tuple-element.538), channel_id=1, source_target_pairs={{0,32},{1,33},{2,34},{3,35},{4,36},{5,37},{6,38},{7,39},{8,40},{9,... | collective-permute-start | bytes 61448 | tf_op jit(solution)/shard_map/while/body/eval_jaxpr/cond/branch_3_fun/ppermute | solution.py:443
  42.6 1.3 %collective-permute-start.15 = (f32[40,128]{1,0:T(8,128)S(1)}, f32[40,128]{1,0:T(8,128)}, u32[]{:S(2)}, u32[]{:S(2)}) collective-permute-start(f32[40,128]{1,0:T(8,128)S(1)} %get-tuple-element.539), channel_id=1, source_target_pairs={{32,64},{33,65},{34,66},{35,67},{36,68},{37,69},{38,70},{39,71},{4... | collective-permute-start | bytes 61448 | tf_op jit(solution)/shard_map/while/body/eval_jaxpr/cond/branch_3_fun/ppermute | solution.py:444
  43.8 3.5 %branch_3_fun.1 = f32[8,5,40,128]{3,2,1,0:T(8,128)S(1)} custom-call(s32[1]{0:T(128)} %get-tuple-element.534.code_ref, f32[8,5,40,128]{3,2,1,0:T(8,128)S(1)} %get-tuple-element.535.old_ref, f32[8,5,40,128]{3,2,1,0:T(8,128)} %get-tuple-element.536.now_ref), custom_call_target="tpu_custom_call" | custom-call | flops 8000000 | bytes 3000000 | tf_op jit(solution)/shard_map/while/body/eval_jaxpr/cond/branch_3_fun/pallas_call | solution.py:445
  47.3 0.0 collective-permute-done.14
  47.3 0.0 collective-permute-done.15
  47.3 0.0 collective-permute-done.13
  47.3 0.0 collective-permute-done.12
  47.4 2.7 %conditional.5 = ((f32[8,5,40,128]{3,2,1,0:T(8,128)}, f32[13,8,128]{2,1,0:T(8,128)S(1)}, f32[40,128]{1,0:T(8,128)S(1)}, f32[40,128]{1,0:T(8,128)S(1)})) conditional(s32[]{:T(128)} %convert_element_type.6, (s32[1]{0:T(128)}, s32[1]{0:T(128)}, f32[8,5,40,128]{3,2,1,0:T(8,128)S(1)}, f32[13,8,128]{2,1,0:T(8,128)}, f32[13,8,128]{2,1,0:T(8,128)}, ...), branch_computations={%region_33.0_spmd, %region_34.0_spmd} | conditional | flops 8000000 | bytes 3000040 | solution.py:466
  47.4 2.7 %branch_0_fun.3 = (f32[8,5,40,128]{3,2,1,0:T(8,128)}, f32[13,8,128]{2,1,0:T(8,128)S(1)}, f32[40,128]{1,0:T(8,128)S(1)}, f32[40,128]{1,0:T(8,128)S(1)}) custom-call(s32[1]{0:T(128)} %get-tuple-element.708.code_ref, s32[1]{0:T(128)} %get-tuple-element.709.offsets_ref, f32[8,5,40,128]{3,2,1,0:T(8,128)S(1)} %get-tuple-element.710.base_ref, ...), custom_call_target="tpu_custom_call" | custom-call | flops 8000000 | bytes 3000000 | tf_op jit(solution)/shard_map/while/body/eval_jaxpr/cond/branch_0_fun/pallas_call | solution.py:460
  50.0 28.1 %conditional.4 = (f32[8,5,40,128]{3,2,1,0:T(8,128)S(1)}, f32[13,8,128]{2,1,0:T(8,128)}, f32[13,8,128]{2,1,0:T(8,128)}, f32[40,128]{1,0:T(8,128)}, f32[40,128]{1,0:T(8,128)}) conditional(s32[]{:T(128)} %clamp.6, (s32[1]{0:T(128)}, f32[8,5,40,128]{3,2,1,0:T(8,128)S(1)}, f32[8,5,40,128]{3,2,1,0:T(8,128)}, ...), branch_computations={%region_1.0_spmd, %region_2.0_spmd, %region_3.0_spmd, %region_4.0_... | conditional | flops 8000000 | bytes 3590024 | solution.py:455
  50.0 8.2 %collective-permute-start.17 = (f32[13,8,128]{2,1,0:T(8,128)S(1)}, f32[13,8,128]{2,1,0:T(8,128)}, u32[]{:S(2)}, u32[]{:S(2)}) collective-permute-start(f32[13,8,128]{2,1,0:T(8,128)S(1)} %get-tuple-element.543), channel_id=1, source_target_pairs={{261,0},{0,261},{262,1},{1,262},{263,2},{2,263},{264,3},{3,264},{2... | collective-permute-start | bytes 159752 | tf_op jit(solution)/shard_map/while/body/eval_jaxpr/cond/branch_4_fun/ppermute | solution.py:442
  58.3 9.8 %collective-permute-start.16 = (f32[13,8,128]{2,1,0:T(8,128)S(1)}, f32[13,8,128]{2,1,0:T(8,128)}, u32[]{:S(2)}, u32[]{:S(2)}) collective-permute-start(f32[13,8,128]{2,1,0:T(8,128)S(1)} %get-tuple-element.543), channel_id=1, source_target_pairs={{260,0},{0,260},{261,1},{1,261},{262,2},{2,262},{263,3},{3,263},{2... | collective-permute-start | bytes 159752 | tf_op jit(solution)/shard_map/while/body/eval_jaxpr/cond/branch_4_fun/ppermute | solution.py:441
  68.1 5.2 %collective-permute-start.18 = (f32[40,128]{1,0:T(8,128)S(1)}, f32[40,128]{1,0:T(8,128)}, u32[]{:S(2)}, u32[]{:S(2)}) collective-permute-start(f32[40,128]{1,0:T(8,128)S(1)} %get-tuple-element.544), channel_id=1, source_target_pairs={{0,32},{1,33},{2,34},{3,35},{4,36},{5,37},{6,38},{7,39},{8,40},{9,... | collective-permute-start | bytes 61448 | tf_op jit(solution)/shard_map/while/body/eval_jaxpr/cond/branch_4_fun/ppermute | solution.py:443
  73.3 1.3 %collective-permute-start.19 = (f32[40,128]{1,0:T(8,128)S(1)}, f32[40,128]{1,0:T(8,128)}, u32[]{:S(2)}, u32[]{:S(2)}) collective-permute-start(f32[40,128]{1,0:T(8,128)S(1)} %get-tuple-element.545), channel_id=1, source_target_pairs={{32,64},{33,65},{34,66},{35,67},{36,68},{37,69},{38,70},{39,71},{4... | collective-permute-start | bytes 61448 | tf_op jit(solution)/shard_map/while/body/eval_jaxpr/cond/branch_4_fun/ppermute | solution.py:444
  74.6 3.5 %branch_4_fun.1 = f32[8,5,40,128]{3,2,1,0:T(8,128)S(1)} custom-call(s32[1]{0:T(128)} %get-tuple-element.540.code_ref, f32[8,5,40,128]{3,2,1,0:T(8,128)S(1)} %get-tuple-element.541.old_ref, f32[8,5,40,128]{3,2,1,0:T(8,128)} %get-tuple-element.542.now_ref), custom_call_target="tpu_custom_call" | custom-call | flops 8000000 | bytes 3000000 | tf_op jit(solution)/shard_map/while/body/eval_jaxpr/cond/branch_4_fun/pallas_call | solution.py:445
  78.1 0.0 collective-permute-done.18
  78.1 0.0 collective-permute-done.19
  78.1 0.0 collective-permute-done.17
  78.1 0.0 collective-permute-done.16
  78.1 2.7 %conditional.5 = ((f32[8,5,40,128]{3,2,1,0:T(8,128)}, f32[13,8,128]{2,1,0:T(8,128)S(1)}, f32[40,128]{1,0:T(8,128)S(1)}, f32[40,128]{1,0:T(8,128)S(1)})) conditional(s32[]{:T(128)} %convert_element_type.6, (s32[1]{0:T(128)}, s32[1]{0:T(128)}, f32[8,5,40,128]{3,2,1,0:T(8,128)S(1)}, f32[13,8,128]{2,1,0:T(8,128)}, f32[13,8,128]{2,1,0:T(8,128)}, ...), branch_computations={%region_33.0_spmd, %region_34.0_spmd} | conditional | flops 8000000 | bytes 3000040 | solution.py:466
  78.2 2.7 %branch_0_fun.3 = (f32[8,5,40,128]{3,2,1,0:T(8,128)}, f32[13,8,128]{2,1,0:T(8,128)S(1)}, f32[40,128]{1,0:T(8,128)S(1)}, f32[40,128]{1,0:T(8,128)S(1)}) custom-call(s32[1]{0:T(128)} %get-tuple-element.708.code_ref, s32[1]{0:T(128)} %get-tuple-element.709.offsets_ref, f32[8,5,40,128]{3,2,1,0:T(8,128)S(1)} %get-tuple-element.710.base_ref, ...), custom_call_target="tpu_custom_call" | custom-call | flops 8000000 | bytes 3000000 | tf_op jit(solution)/shard_map/while/body/eval_jaxpr/cond/branch_0_fun/pallas_call | solution.py:460
  80.8 21.0 %conditional.4 = (f32[8,5,40,128]{3,2,1,0:T(8,128)S(1)}, f32[13,8,128]{2,1,0:T(8,128)}, f32[13,8,128]{2,1,0:T(8,128)}, f32[40,128]{1,0:T(8,128)}, f32[40,128]{1,0:T(8,128)}) conditional(s32[]{:T(128)} %clamp.6, (s32[1]{0:T(128)}, f32[8,5,40,128]{3,2,1,0:T(8,128)S(1)}, f32[8,5,40,128]{3,2,1,0:T(8,128)}, ...), branch_computations={%region_1.0_spmd, %region_2.0_spmd, %region_3.0_spmd, %region_4.0_... | conditional | flops 8000000 | bytes 3590024 | solution.py:455
  80.8 1.9 %collective-permute-start.21 = (f32[13,8,128]{2,1,0:T(8,128)S(1)}, f32[13,8,128]{2,1,0:T(8,128)}, u32[]{:S(2)}, u32[]{:S(2)}) collective-permute-start(f32[13,8,128]{2,1,0:T(8,128)S(1)} %get-tuple-element.549), channel_id=1, source_target_pairs={{262,0},{0,262},{263,1},{1,263},{264,2},{2,264},{265,3},{3,265},{2... | collective-permute-start | bytes 159752 | tf_op jit(solution)/shard_map/while/body/eval_jaxpr/cond/branch_5_fun/ppermute | solution.py:442
  82.7 10.0 %collective-permute-start.20 = (f32[13,8,128]{2,1,0:T(8,128)S(1)}, f32[13,8,128]{2,1,0:T(8,128)}, u32[]{:S(2)}, u32[]{:S(2)}) collective-permute-start(f32[13,8,128]{2,1,0:T(8,128)S(1)} %get-tuple-element.549), channel_id=1, source_target_pairs={{261,0},{0,261},{262,1},{1,262},{263,2},{2,263},{264,3},{3,264},{2... | collective-permute-start | bytes 159752 | tf_op jit(solution)/shard_map/while/body/eval_jaxpr/cond/branch_5_fun/ppermute | solution.py:441
  92.8 4.3 %collective-permute-start.22 = (f32[40,128]{1,0:T(8,128)S(1)}, f32[40,128]{1,0:T(8,128)}, u32[]{:S(2)}, u32[]{:S(2)}) collective-permute-start(f32[40,128]{1,0:T(8,128)S(1)} %get-tuple-element.550), channel_id=1, source_target_pairs={{0,32},{1,33},{2,34},{3,35},{4,36},{5,37},{6,38},{7,39},{8,40},{9,... | collective-permute-start | bytes 61448 | tf_op jit(solution)/shard_map/while/body/eval_jaxpr/cond/branch_5_fun/ppermute | solution.py:443
  97.0 1.3 %collective-permute-start.23 = (f32[40,128]{1,0:T(8,128)S(1)}, f32[40,128]{1,0:T(8,128)}, u32[]{:S(2)}, u32[]{:S(2)}) collective-permute-start(f32[40,128]{1,0:T(8,128)S(1)} %get-tuple-element.551), channel_id=1, source_target_pairs={{32,64},{33,65},{34,66},{35,67},{36,68},{37,69},{38,70},{39,71},{4... | collective-permute-start | bytes 61448 | tf_op jit(solution)/shard_map/while/body/eval_jaxpr/cond/branch_5_fun/ppermute | solution.py:444
  98.3 3.5 %branch_5_fun.1 = f32[8,5,40,128]{3,2,1,0:T(8,128)S(1)} custom-call(s32[1]{0:T(128)} %get-tuple-element.546.code_ref, f32[8,5,40,128]{3,2,1,0:T(8,128)S(1)} %get-tuple-element.547.old_ref, f32[8,5,40,128]{3,2,1,0:T(8,128)} %get-tuple-element.548.now_ref), custom_call_target="tpu_custom_call" | custom-call | flops 8000000 | bytes 3000000 | tf_op jit(solution)/shard_map/while/body/eval_jaxpr/cond/branch_5_fun/pallas_call | solution.py:445
  101.8 0.0 collective-permute-done.22
  101.8 0.0 collective-permute-done.23
  101.8 0.0 collective-permute-done.21
  101.8 0.0 collective-permute-done.20
  101.8 2.3 %conditional.5 = ((f32[8,5,40,128]{3,2,1,0:T(8,128)}, f32[13,8,128]{2,1,0:T(8,128)S(1)}, f32[40,128]{1,0:T(8,128)S(1)}, f32[40,128]{1,0:T(8,128)S(1)})) conditional(s32[]{:T(128)} %convert_element_type.6, (s32[1]{0:T(128)}, s32[1]{0:T(128)}, f32[8,5,40,128]{3,2,1,0:T(8,128)S(1)}, f32[13,8,128]{2,1,0:T(8,128)}, f32[13,8,128]{2,1,0:T(8,128)}, ...), branch_computations={%region_33.0_spmd, %region_34.0_spmd} | conditional | flops 8000000 | bytes 3000040 | solution.py:466
  101.8 2.3 %branch_1_fun.3 = f32[8,5,40,128]{3,2,1,0:T(8,128)} custom-call(s32[1]{0:T(128)} %get-tuple-element.715.code_ref, s32[1]{0:T(128)} %get-tuple-element.716.offsets_ref, f32[8,5,40,128]{3,2,1,0:T(8,128)S(1)} %get-tuple-element.717.base_ref, f32[13,8,128]{2,1,0:T(8,128)} %get-tuple-element.718.turn_ref, f32[13,8,128]{2,1,0:T(8,128)} %get-tuple-element.719.turn2_ref, ...), custom_call_target="tpu_custom_call" | custom-call | flops 8000000 | bytes 3000000 | tf_op jit(solution)/shard_map/while/body/eval_jaxpr/cond/branch_1_fun/pallas_call | solution.py:463
  104.1 1.2 slice.15
  105.4 18.0 %all_to_all.10.in_ref = f32[8,5,32,128]{3,2,1,0:T(8,128)S(1)} all-to-all(f32[8,5,32,128]{3,2,1,0:T(8,128)S(1)} %slice.15), channel_id=1, replica_groups=mesh['row'=2,'ax'=8,'az'=32] {'ax'}, dimensions={0} | all-to-all | bytes 1310720 | tf_op jit(solution)/shard_map/all_to_all | solution.py:471
  123.4 1.1 shard_map.49
  (1 shorter events, 0.0 us)
Async XLA Ops:
  2.2 17.6 %all-to-all-start = ((f32[8,5,32,128]{3,2,1,0:T(8,128)}), f32[8,5,32,128]{3,2,1,0:T(8,128)S(1)}, u32[]{:S(2)}, u32[]{:S(2)}) async-start(f32[8,5,32,128]{3,2,1,0:T(8,128)} %shard_map.46), calls=%async_computation | async-start | bytes 1310720 | tf_op jit(solution)/shard_map/all_to_all | solution.py:425
  19.8 5.8 %collective-permute-start.128 = (f32[20,8,128]{2,1,0:T(8,128)S(1)}, f32[20,8,128]{2,1,0:T(8,128)S(1)}, u32[]{:S(2)}, u32[]{:S(2)}) collective-permute-start(f32[20,8,128]{2,1,0:T(8,128)S(1)} %get-tuple-element.750), channel_id=1, source_target_pairs={{257,0},{0,257},{258,1},{1,258},{259,2},{2,259},{260,3},{3,260},{2... | collective-permute-start | bytes 245768 | tf_op jit(solution)/shard_map/ppermute | solution.py:431
  21.7 5.8 %copy-start = (s32[3]{0:T(128)S(1)}, s32[3]{0:T(128)}, u32[]{:S(2)}) copy-start(s32[3]{0:T(128)} %param.43) | copy-start | bytes 40
  21.7 8.2 %collective-permute-start.130 = (f32[20,8,128]{2,1,0:T(8,128)S(1)}, f32[20,8,128]{2,1,0:T(8,128)S(1)}, u32[]{:S(2)}, u32[]{:S(2)}) collective-permute-start(f32[20,8,128]{2,1,0:T(8,128)S(1)} %get-tuple-element.751), channel_id=1, source_target_pairs={{0,31},{1,0},{2,1},{3,2},{4,3},{5,4},{6,5},{7,6},{8,7},{9,8},{10,9... | collective-permute-start | bytes 245768 | tf_op jit(solution)/shard_map/ppermute | solution.py:432
  25.5 4.3 %collective-permute-start.129 = (f32[20,8,128]{2,1,0:T(8,128)S(1)}, f32[20,8,128]{2,1,0:T(8,128)S(1)}, u32[]{:S(2)}, u32[]{:S(2)}) collective-permute-start(f32[20,8,128]{2,1,0:T(8,128)S(1)} %collective-permute-done.128), channel_id=1, source_target_pairs={{256,0},{0,256},{257,1},{1,257},{258,2},{2,258},{259,3},{3,259},{2... | collective-permute-start | bytes 245768 | tf_op jit(solution)/shard_map/ppermute | solution.py:433
  31.3 16.0 %collective-permute-start.13 = (f32[13,8,128]{2,1,0:T(8,128)S(1)}, f32[13,8,128]{2,1,0:T(8,128)}, u32[]{:S(2)}, u32[]{:S(2)}) collective-permute-start(f32[13,8,128]{2,1,0:T(8,128)S(1)} %get-tuple-element.537), channel_id=1, source_target_pairs={{260,0},{0,260},{261,1},{1,261},{262,2},{2,262},{263,3},{3,263},{2... | collective-permute-start | bytes 159752 | tf_op jit(solution)/shard_map/while/body/eval_jaxpr/cond/branch_3_fun/ppermute | solution.py:442
  37.4 10.0 %collective-permute-start.12 = (f32[13,8,128]{2,1,0:T(8,128)S(1)}, f32[13,8,128]{2,1,0:T(8,128)}, u32[]{:S(2)}, u32[]{:S(2)}) collective-permute-start(f32[13,8,128]{2,1,0:T(8,128)S(1)} %get-tuple-element.537), channel_id=1, source_target_pairs={{259,0},{0,259},{260,1},{1,260},{261,2},{2,261},{262,3},{3,262},{2... | collective-permute-start | bytes 159752 | tf_op jit(solution)/shard_map/while/body/eval_jaxpr/cond/branch_3_fun/ppermute | solution.py:441
  39.8 7.5 %collective-permute-start.14 = (f32[40,128]{1,0:T(8,128)S(1)}, f32[40,128]{1,0:T(8,128)}, u32[]{:S(2)}, u32[]{:S(2)}) collective-permute-start(f32[40,128]{1,0:T(8,128)S(1)} %get-tuple-element.538), channel_id=1, source_target_pairs={{0,32},{1,33},{2,34},{3,35},{4,36},{5,37},{6,38},{7,39},{8,40},{9,... | collective-permute-start | bytes 61448 | tf_op jit(solution)/shard_map/while/body/eval_jaxpr/cond/branch_3_fun/ppermute | solution.py:443
  42.6 4.7 %collective-permute-start.15 = (f32[40,128]{1,0:T(8,128)S(1)}, f32[40,128]{1,0:T(8,128)}, u32[]{:S(2)}, u32[]{:S(2)}) collective-permute-start(f32[40,128]{1,0:T(8,128)S(1)} %get-tuple-element.539), channel_id=1, source_target_pairs={{32,64},{33,65},{34,66},{35,67},{36,68},{37,69},{38,70},{39,71},{4... | collective-permute-start | bytes 61448 | tf_op jit(solution)/shard_map/while/body/eval_jaxpr/cond/branch_3_fun/ppermute | solution.py:444
  50.0 28.1 %collective-permute-start.17 = (f32[13,8,128]{2,1,0:T(8,128)S(1)}, f32[13,8,128]{2,1,0:T(8,128)}, u32[]{:S(2)}, u32[]{:S(2)}) collective-permute-start(f32[13,8,128]{2,1,0:T(8,128)S(1)} %get-tuple-element.543), channel_id=1, source_target_pairs={{261,0},{0,261},{262,1},{1,262},{263,2},{2,263},{264,3},{3,264},{2... | collective-permute-start | bytes 159752 | tf_op jit(solution)/shard_map/while/body/eval_jaxpr/cond/branch_4_fun/ppermute | solution.py:442
  58.3 19.8 %collective-permute-start.16 = (f32[13,8,128]{2,1,0:T(8,128)S(1)}, f32[13,8,128]{2,1,0:T(8,128)}, u32[]{:S(2)}, u32[]{:S(2)}) collective-permute-start(f32[13,8,128]{2,1,0:T(8,128)S(1)} %get-tuple-element.543), channel_id=1, source_target_pairs={{260,0},{0,260},{261,1},{1,261},{262,2},{2,262},{263,3},{3,263},{2... | collective-permute-start | bytes 159752 | tf_op jit(solution)/shard_map/while/body/eval_jaxpr/cond/branch_4_fun/ppermute | solution.py:441
  68.1 10.0 %collective-permute-start.18 = (f32[40,128]{1,0:T(8,128)S(1)}, f32[40,128]{1,0:T(8,128)}, u32[]{:S(2)}, u32[]{:S(2)}) collective-permute-start(f32[40,128]{1,0:T(8,128)S(1)} %get-tuple-element.544), channel_id=1, source_target_pairs={{0,32},{1,33},{2,34},{3,35},{4,36},{5,37},{6,38},{7,39},{8,40},{9,... | collective-permute-start | bytes 61448 | tf_op jit(solution)/shard_map/while/body/eval_jaxpr/cond/branch_4_fun/ppermute | solution.py:443
  73.3 4.7 %collective-permute-start.19 = (f32[40,128]{1,0:T(8,128)S(1)}, f32[40,128]{1,0:T(8,128)}, u32[]{:S(2)}, u32[]{:S(2)}) collective-permute-start(f32[40,128]{1,0:T(8,128)S(1)} %get-tuple-element.545), channel_id=1, source_target_pairs={{32,64},{33,65},{34,66},{35,67},{36,68},{37,69},{38,70},{39,71},{4... | collective-permute-start | bytes 61448 | tf_op jit(solution)/shard_map/while/body/eval_jaxpr/cond/branch_4_fun/ppermute | solution.py:444
  80.8 21.0 %collective-permute-start.21 = (f32[13,8,128]{2,1,0:T(8,128)S(1)}, f32[13,8,128]{2,1,0:T(8,128)}, u32[]{:S(2)}, u32[]{:S(2)}) collective-permute-start(f32[13,8,128]{2,1,0:T(8,128)S(1)} %get-tuple-element.549), channel_id=1, source_target_pairs={{262,0},{0,262},{263,1},{1,263},{264,2},{2,264},{265,3},{3,265},{2... | collective-permute-start | bytes 159752 | tf_op jit(solution)/shard_map/while/body/eval_jaxpr/cond/branch_5_fun/ppermute | solution.py:442
  82.7 19.1 %collective-permute-start.20 = (f32[13,8,128]{2,1,0:T(8,128)S(1)}, f32[13,8,128]{2,1,0:T(8,128)}, u32[]{:S(2)}, u32[]{:S(2)}) collective-permute-start(f32[13,8,128]{2,1,0:T(8,128)S(1)} %get-tuple-element.549), channel_id=1, source_target_pairs={{261,0},{0,261},{262,1},{1,262},{263,2},{2,263},{264,3},{3,264},{2... | collective-permute-start | bytes 159752 | tf_op jit(solution)/shard_map/while/body/eval_jaxpr/cond/branch_5_fun/ppermute | solution.py:441
  92.8 9.0 %collective-permute-start.22 = (f32[40,128]{1,0:T(8,128)S(1)}, f32[40,128]{1,0:T(8,128)}, u32[]{:S(2)}, u32[]{:S(2)}) collective-permute-start(f32[40,128]{1,0:T(8,128)S(1)} %get-tuple-element.550), channel_id=1, source_target_pairs={{0,32},{1,33},{2,34},{3,35},{4,36},{5,37},{6,38},{7,39},{8,40},{9,... | collective-permute-start | bytes 61448 | tf_op jit(solution)/shard_map/while/body/eval_jaxpr/cond/branch_5_fun/ppermute | solution.py:443
  97.0 4.7 %collective-permute-start.23 = (f32[40,128]{1,0:T(8,128)S(1)}, f32[40,128]{1,0:T(8,128)}, u32[]{:S(2)}, u32[]{:S(2)}) collective-permute-start(f32[40,128]{1,0:T(8,128)S(1)} %get-tuple-element.551), channel_id=1, source_target_pairs={{32,64},{33,65},{34,66},{35,67},{36,68},{37,69},{38,70},{39,71},{4... | collective-permute-start | bytes 61448 | tf_op jit(solution)/shard_map/while/body/eval_jaxpr/cond/branch_5_fun/ppermute | solution.py:444
